TPU v7x, 32 devices: a whole 2x2x4 slice. The times are simulated.
32 devices in a mesh: ping: 4 (over z), band: 8 (over y, x, core).
Axes of the slice: x: 2, y: 2, z: 4, core: 2. Of those that a mesh axis runs over, the one named last changes fastest.
Arguments:
- staves: bfloat16 [2, 64, 256, 8, 512], P(None, 'ping', 'band'), may hold values from -6 to 6
- weights: bfloat16 [2, 256, 512, 512], P(None, 'band'), may hold values from -0.25 to 0.25
- replica: float32 [2, 2048], replicated, may hold values from -5 to 5
- start: int32 [64, 512], P('ping', 'band'), may hold values from 0 to 1535
- length: int32 [64, 512], P('ping', 'band'), may hold values from 64 to 512
Outputs:
- centroid: float32 [64, 512], P('ping', 'band')
- energy: float32 [64, 512], P('ping', 'band')
Inputs may be any that keep to these rules, and one draw needn't show every extreme that they name: Every window lies inside the beam's samples: start + length <= 2048.
All inputs are finite; a program needn't handle non-finite values.
Results may differ from a plain program's by a relative error of at most 0.0004.
Values may be sent and summed in bfloat16 or wider, within the bound.
No kernel may reach another device: no remote copies, remote signals or barrier semaphores. Data moves between devices by JAX's collectives and lax.ppermute only.
A program may use at most 192 MiB of HBM per device.

v0:
```python
import math

import jax
import jax.numpy as jnp
from jax import lax
from jax.sharding import PartitionSpec as P

TAPS = (1.0, 2.0, 3.0, 4.0, 5.0, 4.0, 3.0, 2.0, 1.0)


def extended(array, sides, width):
    for axis, dim in sides:
        count, length = (lax.axis_size(axis), array.shape[dim])
        up = [(i, (i + 1) % count) for i in range(count - 1)]
        down = [(j, i) for i, j in up]
        last = lax.slice_in_dim(array, length - width, length, axis=dim)
        initial = lax.slice_in_dim(array, 0, width, axis=dim)
        before = lax.ppermute(last, axis, up)
        after = lax.ppermute(initial, axis, down)
        array = jnp.concatenate([before, array, after], axis=dim)
    return array


def dft_tables(length_total):
    freqs = jnp.arange(length_total, dtype=jnp.int32)
    phases = freqs[:, None] * freqs[None, :] % length_total
    angles = phases.astype(jnp.float32) * (2.0 * math.pi / length_total)
    return (jnp.cos(angles).astype(jnp.bfloat16), jnp.sin(angles).astype(jnp.bfloat16))


def envelope_rows(spec_re, spec_im, replica, cos_table, sin_table):
    comp_re = (spec_re * replica[0] + spec_im * replica[1]).astype(jnp.bfloat16)
    comp_im = (spec_im * replica[0] - spec_re * replica[1]).astype(jnp.bfloat16)
    wave_re = jnp.dot(comp_re, cos_table, preferred_element_type=jnp.float32) - jnp.dot(
        comp_im, sin_table, preferred_element_type=jnp.float32
    )
    wave_im = jnp.dot(comp_re, sin_table, preferred_element_type=jnp.float32) + jnp.dot(
        comp_im, cos_table, preferred_element_type=jnp.float32
    )
    return (wave_re * wave_re + wave_im * wave_im) * (1.0 / (16.0 * cos_table.shape[0]))


def smooth_pings(padded, first_ping, total_pings, ping_count):
    positions = first_ping + jnp.arange(ping_count + 8, dtype=jnp.int32) - 4
    inside = ((positions >= 0) & (positions < total_pings)).astype(jnp.float32)
    summed = jnp.zeros((ping_count,) + padded.shape[1:], jnp.float32)
    weight_sum = jnp.zeros((ping_count,), jnp.float32)
    for offset in range(9):
        summed = summed + TAPS[offset] * padded[offset : offset + ping_count]
        weight_sum = weight_sum + TAPS[offset] * inside[offset : offset + ping_count]
    return summed / weight_sum[:, None, None]


def window_stats(smoothed, start, length):
    samples = jnp.arange(smoothed.shape[-1], dtype=jnp.int32)
    window_start = start[..., None]
    finish = (start + length)[..., None]
    inside = (samples >= window_start) & (samples < finish)
    offsets = samples.astype(jnp.float32) - start.astype(jnp.float32)[..., None] + 0.5
    energy_total = jnp.sum(jnp.where(inside, smoothed, 0.0), axis=-1)
    moment = jnp.sum(jnp.where(inside, smoothed * offsets, 0.0), axis=-1)
    widths = length.astype(jnp.float32)
    return (moment / (widths * (energy_total + 1e-06)), energy_total / widths)


def local(staves, weights, replica, start, length):
    ping_index = lax.axis_index("ping")
    ping_total = lax.axis_size("ping")
    beam_re = jnp.einsum(
        "pkfs,ksb->kpfb", staves[0], weights[0], preferred_element_type=jnp.float32
    ) - jnp.einsum("pkfs,ksb->kpfb", staves[1], weights[1], preferred_element_type=jnp.float32)
    beam_im = jnp.einsum(
        "pkfs,ksb->kpfb", staves[0], weights[1], preferred_element_type=jnp.float32
    ) + jnp.einsum("pkfs,ksb->kpfb", staves[1], weights[0], preferred_element_type=jnp.float32)
    beams = jnp.stack([beam_re, beam_im]).astype(jnp.bfloat16)
    cos_table, sin_table = dft_tables(replica.shape[1])
    turned = lax.all_to_all(beams, "band", split_axis=4, concat_axis=1, tiled=True)
    pings_here = turned.shape[2]
    beams_here = turned.shape[4]
    flat_rows = jnp.transpose(turned, (0, 2, 4, 1, 3)).reshape(2, pings_here * beams_here, -1)
    energy_rows = envelope_rows(
        flat_rows[0].astype(jnp.float32),
        flat_rows[1].astype(jnp.float32),
        replica,
        cos_table,
        sin_table,
    )
    envelope = energy_rows.reshape(pings_here, beams_here, -1)
    ping_count = envelope.shape[0]
    padded = extended(envelope.astype(jnp.bfloat16), (("ping", 0),), 4).astype(envelope.dtype)
    smoothed = smooth_pings(padded, ping_index * ping_count, ping_total * ping_count, ping_count)
    centroid, energy = window_stats(smoothed, start, length)
    return (centroid, energy)


def solution(mesh):
    in_specs = (
        P(None, "ping", "band", None, None),
        P(None, "band", None, None),
        P(),
        P("ping", "band"),
        P("ping", "band"),
    )
    out_specs = (P("ping", "band"), P("ping", "band"))
    return jax.shard_map(local, mesh=mesh, in_specs=in_specs, out_specs=out_specs, check_vma=False)
```

profile of v0, /device:TPU:0, one launch (start us, length us, event | category | flops | bytes accessed | tf_op | source)
XLA Modules:
  0.0 726.0 jit_solution(8714346446857145853)
XLA Ops:
  0.6 5.9 fusion.53
  6.5 12.7 %fusion.5 = f32[32,16,8,512]{3,2,1,0:T(8,128)} fusion(bf16[2,32,512,512]{3,2,1,0:T(8,128)(2,1)} %param.6, bf16[1,16,32,8,512]{4,3,2,1,0:T(8,128)(2,1)} %get-tuple-element.8), kind=kOutput, calls=%fused_computation.8 | convolution fusion | flops 2147483648 | bytes 29360128 | tf_op jit(solution)/shard_map/pkfs,ksb->kpfb/dot_general | solution.py:69
  19.2 12.7 %fusion.3 = f32[32,16,8,512]{3,2,1,0:T(8,128)} fusion(bf16[2,32,512,512]{3,2,1,0:T(8,128)(2,1)} %param.6, bf16[1,16,32,8,512]{4,3,2,1,0:T(8,128)(2,1)} %get-tuple-element.9), kind=kOutput, calls=%fused_computation.6 | convolution fusion | flops 2147483648 | bytes 29360128 | tf_op jit(solution)/shard_map/pkfs,ksb->kpfb/dot_general | solution.py:74
  31.8 12.8 %fusion.31 = bf16[1,32,16,8,512]{4,3,2,1,0:T(8,128)(2,1)} fusion(f32[32,16,8,512]{3,2,1,0:T(8,128)} %fusion.5, bf16[2,32,512,512]{3,2,1,0:T(8,128)(2,1)} %param.6, bf16[1,16,32,8,512]{4,3,2,1,0:T(8,128)(2,1)} %get-tuple-element.9), kind=kOutput, calls=%fused_computation.55 | convolution fusion | flops 2151677952 | bytes 33554432 | tf_op jit(solution)/shard_map/pkfs,ksb->kpfb/dot_general | solution.py:71
  44.6 12.7 %fusion.32 = bf16[1,32,16,8,512]{4,3,2,1,0:T(8,128)(2,1)} fusion(f32[32,16,8,512]{3,2,1,0:T(8,128)} %fusion.3, bf16[2,32,512,512]{3,2,1,0:T(8,128)(2,1)} %param.6, bf16[1,16,32,8,512]{4,3,2,1,0:T(8,128)(2,1)} %get-tuple-element.8), kind=kOutput, calls=%fused_computation.56 | convolution fusion | flops 2151677952 | bytes 33554432 | tf_op jit(solution)/shard_map/pkfs,ksb->kpfb/dot_general | solution.py:72
  57.4 7.5 %pad_maximum_fusion = bf16[2,32,16,8,512]{4,3,2,1,0:T(8,128)(2,1)} fusion(bf16[1,32,16,8,512]{4,3,2,1,0:T(8,128)(2,1)} %fusion.32, bf16[1,32,16,8,512]{4,3,2,1,0:T(8,128)(2,1)} %fusion.31), kind=kLoop, calls=%fused_computation.39 | loop fusion | flops 4194304 | bytes 16777216 | tf_op jit(solution)/shard_map/stack | solution.py:75
  64.8 55.3 %copy.28 = bf16[2,32,16,8,512]{1,3,2,0,4:T(8,128)(2,1)} copy(bf16[2,32,16,8,512]{4,3,2,1,0:T(8,128)(2,1)} %pad_maximum_fusion) | data formatting | bytes 16777216 | tf_op jit(solution)/shard_map/stack | solution.py:75
  120.1 35.5 %reshape.29 = bf16[8,2,262144]{2,1,0:T(2,128)(2,1)} reshape(bf16[512,2,16,8,32]{4,3,2,1,0:T(8,128)(2,1)} %bitcast.67) | data formatting | bytes 16777216
  155.6 5.3 all-to-all-start
  160.9 62.2 %cosine_convert_fusion.5 = bf16[2048,2048]{1,0:T(8,128)(2,1)} fusion(), kind=kLoop, calls=%fused_computation.15.clone.clone.1 | loop fusion | flops 62914560 | bytes 8388608 | tf_op jit(solution)/shard_map/dot_general | solution.py:37
  223.1 62.1 %cosine_convert_fusion.6 = bf16[2048,2048]{1,0:T(8,128)(2,1)} fusion(), kind=kLoop, calls=%fused_computation.15.clone.1.clone | loop fusion | flops 62914560 | bytes 8388608 | tf_op jit(solution)/shard_map/dot_general | solution.py:34
  285.2 62.7 %sine_convert_fusion.10 = bf16[2048,2048]{1,0:T(8,128)(2,1)} fusion(), kind=kLoop, calls=%fused_computation.14.clone.clone.1 | loop fusion | flops 62914560 | bytes 8388608 | tf_op jit(solution)/shard_map/dot_general | solution.py:37
  347.9 62.7 %sine_convert_fusion.9 = bf16[2048,2048]{1,0:T(8,128)(2,1)} fusion(), kind=kLoop, calls=%fused_computation.14.clone.1.clone.clone.clone.1 | loop fusion | flops 62914560 | bytes 8388608 | tf_op jit(solution)/shard_map/dot_general | solution.py:34
  410.6 20.9 %reshape.30 = bf16[512,2,16,8,32]{4,3,2,1,0:T(8,128)(2,1)} reshape(bf16[8,2,262144]{2,1,0:T(2,128)(2,1)} %all-to-all-done) | data formatting | bytes 16777216
  431.4 52.5 %copy.29 = bf16[2,32,16,8,8,64]{5,3,2,1,4,0:T(8,128)(2,1)} copy(bf16[2,32,16,8,8,64]{1,3,2,0,5,4:T(8,128)(2,1)} %bitcast.68) | data formatting | bytes 16777216 | tf_op jit(solution)/shard_map/all_to_all | solution.py:77
  483.9 30.8 %copy.30 = bf16[2,256,16,8,64]{1,3,4,2,0:T(8,128)(2,1)} copy(bf16[2,256,16,8,64]{4,3,2,1,0:T(8,128)(2,1)} %bitcast.69) | data formatting | bytes 16777216 | tf_op jit(solution)/shard_map/all_to_all | solution.py:77
  514.7 11.3 %slice_convert_fusion.1 = (f32[1,16,64,256,8]{3,4,2,1,0:T(8,128)}, f32[1,16,64,256,8]{3,4,2,1,0:T(8,128)}) fusion(bf16[2,16,64,256,8]{3,4,2,1,0:T(8,128)(2,1)} %bitcast.70), kind=kLoop, calls=%fused_computation.58 | loop fusion | flops 4194304 | bytes 25165824 | tf_op jit(solution)/shard_map/convert_element_type | solution.py:82
  526.0 16.1 %copy.31 = f32[1,16,64,256,8]{2,1,4,3,0:T(8,128)} copy(f32[1,16,64,256,8]{3,4,2,1,0:T(8,128)} %get-tuple-element.6) | data formatting | bytes 16777216 | tf_op jit(solution)/shard_map/convert_element_type | solution.py:82
  542.1 14.5 %reshape.25 = f32[1024,2048]{0,1:T(8,128)} reshape(f32[1,16,64,256,8]{2,1,4,3,0:T(8,128)} %copy.31) | data formatting | bytes 16777216 | tf_op jit(solution)/shard_map/convert_element_type | solution.py:82
  556.6 16.1 %copy.32 = f32[1,16,64,256,8]{2,1,4,3,0:T(8,128)} copy(f32[1,16,64,256,8]{3,4,2,1,0:T(8,128)} %get-tuple-element.7) | data formatting | bytes 16777216 | tf_op jit(solution)/shard_map/convert_element_type | solution.py:83
  572.7 14.5 %reshape.26 = f32[1024,2048]{0,1:T(8,128)} reshape(f32[1,16,64,256,8]{2,1,4,3,0:T(8,128)} %copy.32) | data formatting | bytes 16777216 | tf_op jit(solution)/shard_map/convert_element_type | solution.py:83
  587.2 7.1 subtract_convert_fusion
  594.3 15.4 %fusion.27 = f32[1024,2048]{1,0:T(8,128)} fusion(bf16[1024,2048]{0,1:T(8,128)(2,1)S(1)} %get-tuple-element.5, bf16[2048,2048]{1,0:T(8,128)(2,1)} %cosine_convert_fusion.6), kind=kOutput, calls=%fused_computation.45 | convolution fusion | flops 8589934592 | bytes 20971520 | tf_op jit(solution)/shard_map/dot_general | solution.py:34
  609.7 11.5 %fusion.28 = f32[1024,2048]{1,0:T(8,128)} fusion(bf16[1024,2048]{0,1:T(8,128)(2,1)S(1)} %get-tuple-element.5, bf16[2048,2048]{1,0:T(8,128)(2,1)S(1)} %bitcast.75), kind=kOutput, calls=%fused_computation.46 | convolution fusion | flops 8589934592 | bytes 20971520 | tf_op jit(solution)/shard_map/dot_general | solution.py:37
  621.2 11.7 %fusion.26 = f32[1024,2048]{1,0:T(8,128)} fusion(bf16[1024,2048]{0,1:T(8,128)(2,1)S(1)} %get-tuple-element.4, bf16[2048,2048]{1,0:T(8,128)(2,1)S(1)} %bitcast.73), kind=kOutput, calls=%fused_computation.44 | convolution fusion | flops 8589934592 | bytes 20971520 | tf_op jit(solution)/shard_map/dot_general | solution.py:37
  633.0 18.7 %multiply_convert_fusion = bf16[1024,2048]{1,0:T(8,128)(2,1)S(1)} fusion(f32[1024,2048]{1,0:T(8,128)} %fusion.28, f32[1024,2048]{1,0:T(8,128)} %fusion.26, f32[1024,2048]{1,0:T(8,128)} %fusion.27, bf16[1024,2048]{0,1:T(8,128)(2,1)} %copy-done.1, bf16[2048,2048]{1,0:T(8,128)(2,1)} %sine_convert_fusion.9), kind=kOutput, calls=%fused_computation.42 | convolution fusion | flops 8604614656 | bytes 41943040 | tf_op jit(solution)/shard_map/dot_general | solution.py:34
  651.7 1.9 copy-done
  654.8 4.8 collective-permute-start
  661.0 21.7 %collective-permute-done = bf16[4,64,2048]{2,1,0:T(8,128)(2,1)S(1)} collective-permute-done((bf16[4,64,2048]{2,1,0:T(8,128)(2,1)}, bf16[4,64,2048]{2,1,0:T(8,128)(2,1)S(1)}, u32[]{:S(2)}, u32[]{:S(2)}) %collective-permute-start) | collective-permute-done | bytes 1048608 | tf_op jit(solution)/shard_map/ppermute | solution.py:18
  682.7 3.9 collective-permute-done.1
  686.6 7.7 %maximum_convert_fusion = f32[24,64,2048]{2,1,0:T(8,128)} fusion(bf16[4,64,2048]{2,1,0:T(8,128)(2,1)S(1)} %collective-permute-done.1, bf16[16,64,2048]{2,1,0:T(8,128)(2,1)} %bitcast.71, bf16[4,64,2048]{2,1,0:T(8,128)(2,1)S(1)} %collective-permute-done), kind=kLoop, calls=%fused_computation.54 | loop fusion | flops 9437184 | bytes 18874368 | tf_op jit(solution)/shard_map/convert_element_type | solution.py:90
  694.3 30.6 %select_reduce_fusion = (f32[16,64]{1,0:T(8,128)S(1)}, f32[16,64]{1,0:T(8,128)S(1)}) fusion(s32[16,64]{1,0:T(8,128)S(1)} %get-tuple-element.17, s32[16,64]{1,0:T(8,128)S(1)} %copy-done.2, f32[16,64]{1,0:T(8,128)S(1)} %get-tuple-element.16, f32[2048]{0:T(1024)S(1)} %iota_convert_fusion, f32[16]{0:T(128)S(1)} %slice_add_fusion.1, ...), kind=kLoop, calls=%fused_computation.40 | loop fusion | flops 54523904 | bytes 75526208 | tf_op jit(solution)/shard_map/reduce_sum | solution.py:60
  (28 shorter events, 3.2 us)
Async XLA Ops:
  155.6 5.3 copy-start.4
  155.6 255.0 %all-to-all-start = ((bf16[8,2,262144]{2,1,0:T(2,128)(2,1)}), bf16[8,2,262144]{2,1,0:T(2,128)(2,1)}, u32[]{:S(2)}, u32[]{:S(2)}) async-start(bf16[8,2,262144]{2,1,0:T(2,128)(2,1)} %reshape.29), calls=%async_computation | async-start | bytes 16777216 | tf_op jit(solution)/shard_map/all_to_all | solution.py:77
  587.2 22.5 %slice-start.2 = ((s8[8388608]{0:T(1024)(128)(4,1)}), s8[4194304]{0:T(1024)(128)(4,1)S(1)}, s32[]{:S(2)}) async-start(s8[8388608]{0:T(1024)(128)(4,1)} %bitcast.74), calls=%async_computation.3 | async-start | bytes 8388608
  594.3 26.9 %copy-start.1 = (bf16[1024,2048]{0,1:T(8,128)(2,1)}, bf16[1024,2048]{0,1:T(8,128)(2,1)S(1)}, u32[]{:S(2)}) copy-start(bf16[1024,2048]{0,1:T(8,128)(2,1)S(1)} %get-tuple-element.4) | copy-start | bytes 12582916
  594.3 15.4 %slice-start.3 = ((s8[8388608]{0:T(1024)(128)(4,1)}), s8[4194304]{0:T(1024)(128)(4,1)S(1)}, s32[]{:S(2)}) async-start(s8[8388608]{0:T(1024)(128)(4,1)} %bitcast.74), calls=%async_computation.4 | async-start | bytes 8388608
  594.3 26.9 %slice-start = ((s8[8388608]{0:T(1024)(128)(4,1)}), s8[4194304]{0:T(1024)(128)(4,1)S(1)}, s32[]{:S(2)}) async-start(s8[8388608]{0:T(1024)(128)(4,1)} %bitcast.72), calls=%async_computation.1 | async-start | bytes 8388608
  609.7 11.5 %slice-start.1 = ((s8[8388608]{0:T(1024)(128)(4,1)}), s8[4194304]{0:T(1024)(128)(4,1)S(1)}, s32[]{:S(2)}) async-start(s8[8388608]{0:T(1024)(128)(4,1)} %bitcast.72), calls=%async_computation.2 | async-start | bytes 8388608
  633.0 28.0 %copy-start.2 = (s32[16,64]{1,0:T(8,128)S(1)}, s32[16,64]{1,0:T(8,128)}, u32[]{:S(2)}) copy-start(s32[16,64]{1,0:T(8,128)} %param.8) | copy-start | bytes 12292
  633.0 28.0 %copy-start.3 = (s32[16,64]{1,0:T(8,128)S(1)}, s32[16,64]{1,0:T(8,128)}, u32[]{:S(2)}) copy-start(s32[16,64]{1,0:T(8,128)} %param.9) | copy-start | bytes 12292
  651.7 1.9 copy-start
  654.8 28.0 %collective-permute-start = (bf16[4,64,2048]{2,1,0:T(8,128)(2,1)}, bf16[4,64,2048]{2,1,0:T(8,128)(2,1)S(1)}, u32[]{:S(2)}, u32[]{:S(2)}) collective-permute-start(bf16[4,64,2048]{2,1,0:T(8,128)(2,1)} %bitcast.18), channel_id=1, source_target_pairs={{0,8},{8,16},{16,24},{1,9},{9,17},{17,25},{2,10},{10,18},{18,26},{... | collective-permute-start | bytes 3145736 | tf_op jit(solution)/shard_map/ppermute | solution.py:18
  659.5 27.0 %collective-permute-start.1 = (bf16[4,64,2048]{2,1,0:T(8,128)(2,1)S(1)}, bf16[4,64,2048]{2,1,0:T(8,128)(2,1)S(1)}, u32[]{:S(2)}, u32[]{:S(2)}) collective-permute-start(bf16[4,64,2048]{2,1,0:T(8,128)(2,1)S(1)} %bitcast.76), channel_id=1, source_target_pairs={{8,0},{16,8},{24,16},{9,1},{17,9},{25,17},{10,2},{18,10},{26,18},{... | collective-permute-start | bytes 3145736 | tf_op jit(solution)/shard_map/ppermute | solution.py:19
where the time goes:
time: 735 us; the launch traced here: 726 us
  other arithmetic  315 us (43%)
  local copies, waits for them, and re-layouts  265 us (36%)
  matrix products  108 us (15%)
  waiting for transfers between devices  25.6 us (3%)
  starting transfers between devices  11.4 us (2%)
    all_to_all x2, local copies, waits for them, and re-layouts, local(): lax.all_to_all(beams, 'band', split_axis=4, concat_axis=1, tiled=True)  83.3 us
    dot_general x1, other arithmetic, envelope_rows(): jnp.dot(comp_re, sin_table, preferred_element_type=jnp.float32)  62.7 us
    dot_general x1, other arithmetic, envelope_rows(): jnp.dot(comp_im, sin_table, preferred_element_type=jnp.float32)  62.7 us
    dot_general x1, other arithmetic, envelope_rows(): jnp.dot(comp_im, cos_table, preferred_element_type=jnp.float32)  62.2 us
    dot_general x1, other arithmetic, envelope_rows(): jnp.dot(comp_re, cos_table, preferred_element_type=jnp.float32)  62.1 us
    unnamed x20, local copies, waits for them, and re-layouts  58.3 us
    another operation x1, local copies, waits for them, and re-layouts, local(): beams = jnp.stack([beam_re, beam_im]).astype(jnp.bfloat16)  55.3 us
    reduce_sum x1, other arithmetic, window_stats(): energy_total = jnp.sum(jnp.where(inside, smoothed, 0.0), axis=-1)  30.6 us
  transfers between devices with their start and end apart: 3, of which 2 were waited for; matrix products, arithmetic and copies ran while one was open for 34% of the time, Pallas kernels for 0%

commit v1 on v0

--- a/solution.py
+++ b/solution.py
@@ -1,11 +1,21 @@
+import functools
 import math
 
 import jax
 import jax.numpy as jnp
 from jax import lax
+from jax.experimental import pallas as pl
+from jax.experimental.pallas import tpu as pltpu
 from jax.sharding import PartitionSpec as P
 
+
 TAPS = (1.0, 2.0, 3.0, 4.0, 5.0, 4.0, 3.0, 2.0, 1.0)
+REACH = len(TAPS) // 2
+LANES = 128
+PAIR = 2
+BLOCK = 16
+HEAD_STEPS = 4
+STEP_BANDS = 2
 
 
 def extended(array, sides, width):
@@ -40,15 +50,20 @@
     return (wave_re * wave_re + wave_im * wave_im) * (1.0 / (16.0 * cos_table.shape[0]))
 
 
+def tap_weights(first_ping, total_pings, ping_count):
+    positions = first_ping + jnp.arange(ping_count + 2 * REACH, dtype=jnp.int32) - REACH
+    inside = ((positions >= 0) & (positions < total_pings)).astype(jnp.float32)
+    weight_sum = jnp.zeros((ping_count,), jnp.float32)
+    for offset, tap in enumerate(TAPS):
+        weight_sum = weight_sum + tap * inside[offset : offset + ping_count]
+    return weight_sum
+
+
 def smooth_pings(padded, first_ping, total_pings, ping_count):
-    positions = first_ping + jnp.arange(ping_count + 8, dtype=jnp.int32) - 4
-    inside = ((positions >= 0) & (positions < total_pings)).astype(jnp.float32)
     summed = jnp.zeros((ping_count,) + padded.shape[1:], jnp.float32)
-    weight_sum = jnp.zeros((ping_count,), jnp.float32)
-    for offset in range(9):
-        summed = summed + TAPS[offset] * padded[offset : offset + ping_count]
-        weight_sum = weight_sum + TAPS[offset] * inside[offset : offset + ping_count]
-    return summed / weight_sum[:, None, None]
+    for offset, tap in enumerate(TAPS):
+        summed = summed + tap * padded[offset : offset + ping_count]
+    return summed / tap_weights(first_ping, total_pings, ping_count)[:, None, None]
 
 
 def window_stats(smoothed, start, length):
@@ -63,7 +78,7 @@
     return (moment / (widths * (energy_total + 1e-06)), energy_total / widths)
 
 
-def local(staves, weights, replica, start, length):
+def local_plain(staves, weights, replica, start, length):
     ping_index = lax.axis_index("ping")
     ping_total = lax.axis_size("ping")
     beam_re = jnp.einsum(
@@ -87,10 +102,405 @@
     )
     envelope = energy_rows.reshape(pings_here, beams_here, -1)
     ping_count = envelope.shape[0]
-    padded = extended(envelope.astype(jnp.bfloat16), (("ping", 0),), 4).astype(envelope.dtype)
+    padded = extended(envelope.astype(jnp.bfloat16), (("ping", 0),), REACH).astype(envelope.dtype)
     smoothed = smooth_pings(padded, ping_index * ping_count, ping_total * ping_count, ping_count)
     centroid, energy = window_stats(smoothed, start, length)
     return (centroid, energy)
+
+
+def beam_kernel(me_ref, x_ref, w_ref, rep_ref, *outs, count, first_band, splits):
+    bands = x_ref.shape[2]
+    pings, bins, staves = x_ref.shape[1], x_ref.shape[3], x_ref.shape[4]
+    rows = pings * bins
+    step = pl.program_id(0)
+    base = (first_band + step * bands) * bins
+    q_rows = lax.broadcasted_iota(jnp.int32, (bins, rep_ref.shape[1]), 0)
+    q_cols = lax.broadcasted_iota(jnp.int32, (bins, rep_ref.shape[1]), 1)
+    lower = lax.broadcasted_iota(jnp.int32, (2 * bins, LANES), 1) < LANES // PAIR
+    swap = jnp.broadcast_to(lax.bitwise_and(me_ref[0], PAIR - 1) == 1, (2 * bins, LANES))
+    places = [(i, at) for i, size in enumerate(splits) for at in range(size)]
+
+    def spectra(k):
+        def part(which):
+            flat = x_ref[which, :, k].astype(jnp.float32).reshape(rows, staves)
+            return flat.astype(jnp.bfloat16)
+
+        re, im = part(0), part(1)
+        both = jnp.concatenate(
+            [jnp.concatenate([re, -im], axis=1), jnp.concatenate([im, re], axis=1)], axis=0
+        )
+        mine = q_cols == q_rows + (base + k * bins)
+        rep = [
+            jnp.sum(jnp.where(mine, rep_ref[i : i + 1, :], 0.0), axis=1, keepdims=True)
+            for i in range(2)
+        ]
+        return both, rep
+
+    def compressed(k, both, rep, groups):
+        weights = jnp.concatenate(
+            [
+                jnp.concatenate([w_ref[which, k, :, lanes] for lanes in groups], axis=1)
+                for which in range(2)
+            ],
+            axis=0,
+        )
+        beam = jnp.dot(both, weights, preferred_element_type=jnp.float32)
+        beam = beam.astype(jnp.bfloat16).astype(jnp.float32)
+        beam_re = beam[:rows].reshape(pings, bins, beam.shape[1])
+        beam_im = beam[rows:].reshape(pings, bins, beam.shape[1])
+        return (beam_re * rep[0] + beam_im * rep[1], beam_im * rep[0] - beam_re * rep[1])
+
+    for k in range(0, bands, 2):
+        pair = [spectra(k), spectra(k + 1)]
+        here = slice(k * bins, (k + 2) * bins)
+        there = pl.ds(pl.multiple_of((step * bands + k) * bins, 2 * bins), 2 * bins)
+        for near in range(0, count, 2 * PAIR):
+            groups = []
+            for r in (near, near + PAIR):
+                group = lax.shift_right_logical(lax.bitwise_xor(me_ref[0], r), 1)
+                groups.append(pl.ds(pl.multiple_of(group * LANES, LANES), LANES))
+            done = [compressed(k + i, *pair[i], groups) for i in range(2)]
+            for which in range(2):
+                joined = jnp.concatenate([done[0][which], done[1][which]], axis=1)
+                for part in range(len(groups)):
+                    lane = slice(part * LANES, (part + 1) * LANES)
+                    r = near + PAIR * part
+                    for slot, (i, at) in enumerate(places):
+                        one, two = joined[slot, :, lane], joined[pings - 1 - slot, :, lane]
+                        first = jnp.where(lower, one, pltpu.roll(two, LANES // PAIR, 1))
+                        second = jnp.where(lower, pltpu.roll(one, LANES // PAIR, 1), two)
+                        first, second = first.astype(jnp.bfloat16), second.astype(jnp.bfloat16)
+                        to = here if r == 0 else there
+                        outs[i * count + r][which, at, to, :] = jnp.where(swap, second, first)
+                        outs[i * count + r + 1][which, at, there, :] = jnp.where(swap, first, second)
+
+
+def beamform(me, staves, weights, replica, count, first_band, steps, bands, splits):
+    pings, bins = staves.shape[1], staves.shape[3]
+    depth, beams = weights.shape[2], weights.shape[3]
+    local_q = weights.shape[1] * bins
+    skip = first_band // bands
+    rows = bands * bins
+    shapes = [
+        jax.ShapeDtypeStruct((2, size, steps * rows, LANES), jnp.bfloat16)
+        for size in splits
+        for _ in range(count)
+    ]
+    flops = 8 * steps * bands * pings * bins * depth * beams
+    moved = 4 * steps * bands * depth * beams + 8 * steps * bands * pings * bins * depth
+    return pl.pallas_call(
+        functools.partial(beam_kernel, count=count, first_band=first_band, splits=splits),
+        grid_spec=pltpu.PrefetchScalarGridSpec(
+            num_scalar_prefetch=1,
+            grid=(steps,),
+            in_specs=[
+                pl.BlockSpec((2, pings, bands, bins, depth), lambda s, me: (0, 0, skip + s, 0, 0)),
+                pl.BlockSpec((2, bands, depth, beams), lambda s, me: (0, skip + s, 0, 0)),
+                pl.BlockSpec((2, local_q), lambda s, me: (0, me[0])),
+            ],
+            out_specs=[
+                pl.BlockSpec((2, size, rows, LANES), lambda s, me: (0, 0, s, 0))
+                if r == 0
+                else pl.BlockSpec(memory_space=pltpu.VMEM)
+                for size in splits
+                for r in range(count)
+            ],
+        ),
+        out_shape=shapes,
+        compiler_params=pltpu.CompilerParams(vmem_limit_bytes=24 << 20),
+        cost_estimate=pl.CostEstimate(flops=flops, bytes_accessed=moved, transcendentals=0),
+        name="beamform",
+    )(me, *(pltpu.with_memory_space_constraint(a, pltpu.HBM) for a in (staves, weights, replica)))
+
+
+def add(a, b):
+    return (a[0] + b[0], a[1] + b[1])
+
+
+def sub(a, b):
+    return (a[0] - b[0], a[1] - b[1])
+
+
+def turned(z, steps, signs, count):
+    cos, sin = 1.0, 0.0
+    for bit in range(steps.bit_length()):
+        if steps >> bit & 1:
+            angle = 2.0 * math.pi * (1 << bit) / count
+            quarter = 4 << bit == count
+            c, s = 0.0 if quarter else math.cos(angle), signs[bit] * math.sin(angle)
+            if quarter:
+                cos, sin = (-1.0 * sin * s if not isinstance(sin, float) else 0.0), cos * s
+            else:
+                cos, sin = c, s
+    if isinstance(cos, float) and cos == 0.0:
+        return (z[1] * -sin, z[0] * sin)
+    return (z[0] * cos - z[1] * sin, z[1] * cos + z[0] * sin)
+
+
+def small_dft(values, signs):
+    count = len(values)
+    if count == 1:
+        return values
+    middle = count // 2
+    even = small_dft([add(values[i], values[i + middle]) for i in range(middle)], signs)
+    apart = [sub(values[i], values[i + middle]) for i in range(middle)]
+    odd = small_dft(
+        [apart[0]] + [turned(apart[i], i, signs, count) for i in range(1, middle)], signs
+    )
+    return [even[i // 2] if i % 2 == 0 else odd[i // 2] for i in range(count)]
+
+
+def turned_kernel(me_ref, *refs, count, width, together):
+    heads, tails = refs[:count], refs[count : 2 * count]
+    cos_ref, sin_ref, window_ref, out_ref, spec, power, kept, acc = refs[2 * count :]
+    step = pl.program_id(0)
+    slots = 2
+    head_rows, tail_rows = heads[0].shape[2], tails[0].shape[2]
+    depth = head_rows + tail_rows
+    signs = [
+        (1 - 2 * lax.bitwise_and(lax.shift_right_logical(me_ref[0], b), 1)).astype(jnp.float32)
+        for b in range(count.bit_length() - 2)
+    ]
+
+    def transform(sources, slot, row, to):
+        values = [
+            tuple(ref[i, slot, pl.ds(row, BLOCK), :].astype(jnp.float32) for i in range(2))
+            for ref in sources
+        ]
+        for m, z in enumerate(small_dft(values, signs)):
+            spec[m, slot, pl.ds(to, BLOCK), :] = z[0].astype(jnp.bfloat16)
+            spec[m, slot, pl.ds(depth + to, BLOCK), :] = z[1].astype(jnp.bfloat16)
+
+    @pl.when(step == 0)
+    def _():
+        acc[...] = jnp.zeros_like(acc)
+        for slot in range(slots):
+
+            @pl.loop(0, head_rows // BLOCK)
+            def _(i):
+                row = pl.multiple_of(i * BLOCK, BLOCK)
+                transform(heads, slot, row, row)
+
+            @pl.loop(0, tail_rows // BLOCK)
+            def _(i):
+                row = pl.multiple_of(i * BLOCK, BLOCK)
+                transform(tails, slot, row, pl.multiple_of(head_rows + row, BLOCK))
+
+    for j in range(together):
+        m = step * together + j
+        cos, sin = cos_ref[j], sin_ref[j]
+        table = jnp.concatenate(
+            [jnp.concatenate([cos, -sin], axis=1), jnp.concatenate([sin, cos], axis=1)], axis=0
+        )
+        spectra = jnp.concatenate([spec[m, 0], spec[m, 1]], axis=1)
+        wave = jnp.dot(table, spectra, preferred_element_type=jnp.float32)
+        power[j] = wave[:depth] * wave[:depth] + wave[depth:] * wave[depth:]
+
+    shift = count.bit_length() - 1
+    first_row = lax.broadcasted_iota(jnp.int32, (BLOCK, LANES), 0)
+    for j in range(together):
+        m = step * together + j
+        edges = [
+            [
+                jnp.broadcast_to(
+                    lax.shift_right_arithmetic(window_ref[i, o : o + 1, :] + (count - 1 - m), shift)
+                    .astype(jnp.float32)
+                    .astype(jnp.bfloat16),
+                    (BLOCK, LANES),
+                )
+                for o in range(width)
+            ]
+            for i in range(2)
+        ]
+
+        def windowed(i, carry):
+            row = pl.multiple_of(i * BLOCK, BLOCK)
+            one = power[j, pl.ds(row, BLOCK), :LANES]
+            two = power[j, pl.ds(row, BLOCK), LANES:]
+            both = one + two
+            rows = (first_row + row).astype(jnp.float32).astype(jnp.bfloat16)
+
+            def keep(o, value):
+                inside = (rows >= edges[0][o]) & (rows < edges[1][o])
+                value = jnp.where(inside, value.astype(jnp.bfloat16), jnp.bfloat16(0))
+                kept[j, o, pl.ds(row, BLOCK), :] = value
+
+            for o in range(REACH + 1):
+                keep(o, one)
+                keep(width - 1 - o, two)
+                if o < REACH:
+                    one, two = one + both, two + both
+            return carry
+
+        lax.fori_loop(0, depth // BLOCK, windowed, 0, unroll=2)
+
+    sum_row = lax.broadcasted_iota(jnp.int32, (BLOCK, depth), 0)
+    sum_col = lax.broadcasted_iota(jnp.int32, (BLOCK, depth), 1)
+    for j in range(together):
+        m = step * together + j
+        sums = jnp.where(sum_row == 0, 1, jnp.where(sum_row == 1, count * sum_col, 0))
+        sums = jnp.where(sum_row == 2, m, sums).astype(jnp.float32).astype(jnp.bfloat16)
+        for o in range(0, width, 2):
+            pair = jnp.concatenate([kept[j, o], kept[j, o + 1]], axis=1)
+            lanes = slice(o * LANES, (o + 2) * LANES)
+            acc[:, lanes] += jnp.dot(sums, pair, preferred_element_type=jnp.float32)[:8]
+
+    @pl.when(step == count // together - 1)
+    def _():
+        out_ref[...] = acc[...]
+
+
+def window_sums(me, heads, tails, tables, windows, chunk):
+    count = len(heads)
+    width = 2 * REACH + 2
+    together = 2
+    head_rows, tail_rows = heads[0].shape[2], tails[0].shape[2]
+    depth = head_rows + tail_rows
+    flops = 2 * count * (2 * depth) * (2 * depth) * (2 * LANES)
+    moved = 4 * tables[0].size + 16 * count * depth * LANES
+    sums = pl.pallas_call(
+        functools.partial(turned_kernel, count=count, width=width, together=together),
+        grid_spec=pltpu.PrefetchScalarGridSpec(
+            num_scalar_prefetch=1,
+            grid=(count // together,),
+            in_specs=[
+                pl.BlockSpec((2, 2, head_rows, LANES), lambda s, me: (0, chunk, 0, 0))
+                for _ in range(count)
+            ]
+            + [
+                pl.BlockSpec((2, 2, tail_rows, LANES), lambda s, me: (0, 0, 0, 0))
+                for _ in range(count)
+            ]
+            + [pl.BlockSpec((together, depth, depth), lambda s, me: (s, 0, 0)) for _ in range(2)]
+            + [pl.BlockSpec((2, width, LANES), lambda s, me: (0, 0, 0))],
+            out_specs=pl.BlockSpec((8, width * LANES), lambda s, me: (0, 0)),
+            scratch_shapes=[
+                pltpu.VMEM((count, 2, 2 * depth, LANES), jnp.bfloat16),
+                pltpu.VMEM((together, depth, 2 * LANES), jnp.float32),
+                pltpu.VMEM((together, width, depth, LANES), jnp.bfloat16),
+                pltpu.VMEM((8, width * LANES), jnp.float32),
+            ],
+        ),
+        out_shape=jax.ShapeDtypeStruct((8, width * LANES), jnp.float32),
+        compiler_params=pltpu.CompilerParams(vmem_limit_bytes=14 << 20),
+        cost_estimate=pl.CostEstimate(flops=flops, bytes_accessed=moved, transcendentals=0),
+        name="window_sums",
+    )(me, *heads, *tails, *tables, windows)
+    return jnp.stack([sums[0], sums[1] + sums[2]]).reshape(2, width, LANES)
+
+
+def wave_tables(count, depth, after):
+    total = count * depth
+    index = jnp.arange(depth, dtype=jnp.int32)
+    index, _ = lax.optimization_barrier((index, after))
+    angle = ((index[:, None] * index[None, :]) % depth).astype(jnp.float32) * (2.0 * math.pi / depth)
+    turn = (jnp.arange(count, dtype=jnp.int32)[:, None] * index[None, :]).astype(jnp.float32)
+    turn = turn * (2.0 * math.pi / total)
+    small = (jnp.cos(angle), jnp.sin(angle), jnp.cos(turn), jnp.sin(turn))
+    cos_a, sin_a, cos_b, sin_b = lax.optimization_barrier(small)
+    cos_b, sin_b = cos_b[:, None, :], sin_b[:, None, :]
+    cos = (cos_a * cos_b - sin_a * sin_b).astype(jnp.bfloat16)
+    sin = (sin_a * cos_b + cos_a * sin_b).astype(jnp.bfloat16)
+    return lax.optimization_barrier((cos, sin))
+
+
+def local_fast(staves, weights, replica, start, length):
+    count = lax.axis_size("band")
+    blocks = lax.axis_size("ping")
+    me = jnp.reshape(lax.axis_index("band"), (1,)).astype(jnp.int32)
+    block = lax.axis_index("ping")
+    pings, bands, bins = staves.shape[1:4]
+    half = pings // PAIR
+    chunks = half // 2
+    depth = bands * bins
+    mine = start.shape[1]
+
+    def send(array, r):
+        return lax.ppermute(array, "band", [(i, i ^ r) for i in range(count)])
+
+    def up(array):
+        return lax.ppermute(array, "ping", [(i, i + 1) for i in range(blocks - 1)])
+
+    def down(array):
+        return lax.ppermute(array, "ping", [(i + 1, i) for i in range(blocks - 1)])
+
+    head_bands = HEAD_STEPS * STEP_BANDS
+    heads = beamform(me, staves, weights, replica, count, 0, HEAD_STEPS, STEP_BANDS, (half,))
+    got_heads = [heads[0]] + [send(heads[r], r) for r in range(1, count)]
+
+    rest = (bands - head_bands) // (2 * STEP_BANDS)
+    me_next, _ = lax.optimization_barrier((me, heads[0]))
+    tails = beamform(
+        me_next, staves, weights, replica, count, head_bands, rest, 2 * STEP_BANDS, (2,) * chunks
+    )
+    got_tails = []
+    for i in range(chunks):
+        own = tails[i * count : (i + 1) * count]
+        got_tails.append([own[0]] + [send(own[r], r) for r in range(1, count)])
+
+    own_start, own_length, _ = lax.optimization_barrier((start, length, tails[0]))
+    spans = jnp.stack([own_start, own_start + own_length])
+    reach = half + REACH
+    before = up(spans[:, pings - REACH :])
+    after = down(spans[:, :REACH])
+    left = jnp.concatenate([before, spans[:, :reach]], axis=1)
+    right = jnp.concatenate([spans[:, pings - reach :], after], axis=1)
+    windows = jnp.concatenate([left, jnp.flip(right, 1)], axis=2)
+
+    tables = wave_tables(count, depth, tails[0])
+
+    width = 2 * REACH + 2
+    reached = half + 2 * REACH
+    sums = jnp.zeros((2, reached, LANES), jnp.float32)
+    for i in range(chunks):
+        reached_windows = windows[:, 2 * i : 2 * i + width]
+        if i == chunks - 1:
+            reached_windows, edge_left, edge_right = lax.optimization_barrier(
+                (reached_windows, edge_left, edge_right)
+            )
+        part = window_sums(me, got_heads, got_tails[i], tables, reached_windows, i)
+        sums = sums + jnp.pad(part, ((0, 0), (2 * i, reached - width - 2 * i), (0, 0)))
+        if 2 * (i + 1) == REACH:
+            edge_left = down(sums[:, :REACH, :mine])
+            edge_right = up(jnp.flip(sums[:, :REACH, mine:], 1))
+
+    def placed(array, before):
+        after = pings - before - array.shape[1]
+        return jnp.pad(array, ((0, 0), (before, after), (0, 0)))
+
+    whole = placed(sums[:, REACH:, :mine], 0)
+    whole = whole + placed(jnp.flip(sums[:, REACH:, mine:], 1), pings - reach)
+    whole = whole + placed(edge_left, pings - REACH) + placed(edge_right, 0)
+
+    weight_sum = tap_weights(block * pings, blocks * pings, pings)
+    scale = (1.0 / (16.0 * count * depth)) / weight_sum[:, None]
+    widths = length.astype(jnp.float32)
+    energy_total = whole[0] * scale
+    moment = (whole[1] - whole[0] * (start.astype(jnp.float32) - 0.5)) * scale
+    return (moment / (widths * (energy_total + 1e-06)), energy_total / widths)
+
+
+def fits(mesh, staves, weights):
+    count, blocks = mesh.shape["band"], mesh.shape["ping"]
+    pings, bands = staves.shape[1] // blocks, staves.shape[2] // count
+    bins, depth = staves.shape[3:]
+    beams = weights.shape[3]
+    half = pings // PAIR
+    head_bands = HEAD_STEPS * STEP_BANDS
+    return (
+        count == 8
+        and beams * PAIR == LANES * count
+        and beams % (2 * LANES) == 0
+        and pings % (2 * PAIR) == 0
+        and half > REACH
+        and bins == 8
+        and depth % LANES == 0
+        and bands * bins % LANES == 0
+        and bands * bins <= 2 * LANES
+        and bands > head_bands
+        and (bands - head_bands) % (2 * STEP_BANDS) == 0
+        and head_bands % (2 * STEP_BANDS) == 0
+    )
 
 
 def solution(mesh):
@@ -102,4 +512,16 @@
         P("ping", "band"),
     )
     out_specs = (P("ping", "band"), P("ping", "band"))
-    return jax.shard_map(local, mesh=mesh, in_specs=in_specs, out_specs=out_specs, check_vma=False)
+
+    def run(staves, weights, replica, start, length):
+        quick = fits(mesh, staves, weights)
+
+        def local(*arrays):
+            return (local_fast if quick else local_plain)(*arrays)
+
+        body = jax.shard_map(
+            local, mesh=mesh, in_specs=in_specs, out_specs=out_specs, check_vma=False
+        )
+        return body(staves, weights, replica, start, length)
+
+    return run

time: 735 us -> 171 us (0.23); the launches traced: 726 us -> 170 us
  other arithmetic: 315 us -> 2.83 us
  local copies, waits for them, and re-layouts: 265 us -> 24.8 us
  matrix products: 108 us -> 0 us
  Pallas kernels: 0 us -> 51.5 us
  starting transfers between devices: 11.4 us -> 52.7 us
  waiting for transfers between devices: 25.6 us -> 37.4 us
    dot_general x4 -> x0, other arithmetic: 250 us -> none  [the longest x1 62.7 us: envelope_rows(): jnp.dot(comp_re, sin_table, preferred_element_type=jnp.float32)]
    dot_general x8 -> x0, matrix products: 108 us -> none  [the longest x1 18.7 us: envelope_rows(): jnp.dot(comp_im, sin_table, preferred_element_type=jnp.float32)]
    all_to_all x2 -> x0, local copies, waits for them, and re-layouts: 83.3 us -> none  [local(): lax.all_to_all(beams, 'band', split_axis=4, concat_axis=1, tiled=True)]
    convert_element_type x4 -> x0, local copies, waits for them, and re-layouts: 61.2 us -> none  [the longest x2 30.6 us: local(): flat_rows[1].astype(jnp.float32)]
    another operation x1 -> x0, local copies, waits for them, and re-layouts: 55.3 us -> none  [local(): beams = jnp.stack([beam_re, beam_im]).astype(jnp.bfloat16)]
    pallas_call x0 -> x6, Pallas kernels: none -> 51.5 us  [the longest x4 28.6 us: window_sums(): pl.pallas_call(functools.partial(turned_kernel, count=count, width=width,...]
    ppermute x2 -> x39, starting transfers between devices: 6.07 us -> 52.7 us  [the longest x35 41 us: send(): return lax.ppermute(array, 'band', [(i, i ^ r) for i in range(count)])]
    unnamed x20 -> x110, local copies, waits for them, and re-layouts: 58.3 us -> 24.5 us
  transfers between devices with their start and end apart: 3 -> 39, of which waited for: 2 -> 9; matrix products, arithmetic and copies ran while one was open for 34% -> 1% of each run, Pallas kernels for 0% -> 13%
where the time goes in v1:
time: 171 us; the launch traced here: 170 us
  starting transfers between devices  52.7 us (31%)
  Pallas kernels  51.5 us (30%)
  waiting for transfers between devices  37.4 us (22%)
  local copies, waits for them, and re-layouts  24.8 us (15%)
  other arithmetic  2.83 us (2%)
    ppermute x35, starting transfers between devices, send(): return lax.ppermute(array, 'band', [(i, i ^ r) for i in range(count)])  41 us
    ppermute x35, waiting for transfers between devices, send(): return lax.ppermute(array, 'band', [(i, i ^ r) for i in range(count)])  37.4 us
    pallas_call x4, Pallas kernels, window_sums(): pl.pallas_call(functools.partial(turned_kernel, count=count, width=width,...  28.6 us
    unnamed x110, local copies, waits for them, and re-layouts  24.5 us
    pallas_call x2, Pallas kernels, beamform(): pl.pallas_call(functools.partial(beam_kernel, count=count, first_band=fir...  22.9 us
    ppermute x2, starting transfers between devices, up(): return lax.ppermute(array, 'ping', [(i, i + 1) for i in range(blocks - 1)])  9.06 us
  transfers between devices with their start and end apart: 39, of which 9 were waited for; matrix products, arithmetic and copies ran while one was open for 1% of the time, Pallas kernels for 13%

profile of v1, /device:TPU:0, one launch (start us, length us, event | category | flops | bytes accessed | tf_op | source)
XLA Modules:
  0.0 170.3 jit_solution(7796765828547398469)
XLA Ops:
  0.6 7.4 %beamform.2 = (bf16[2,8,64,128]{3,2,1,0:T(8,128)(2,1)S(1)}, bf16[2,8,64,128]{3,2,1,0:T(8,128)(2,1)}, bf16[2,8,64,128]{3,2,1,0:T(8,128)(2,1)}, bf16[2,8,64,128]{3...) custom-call(s32[1]{0:T(128)} %bitcast.me_ref, ...), custom_call_target="tpu_custom_call" | custom-call | flops 2147483648 | bytes 12582912 | tf_op jit(solution)/shard_map/beamform/pallas_call | solution.py:191
  11.5 15.6 %beamform.3 = (bf16[2,2,192,128]{3,2,1,0:T(8,128)(2,1)S(1)}, bf16[2,2,192,128]{3,2,1,0:T(8,128)(2,1)}, bf16[2,2,192,128]{3,2,1,0:T(8,128)(2,1)}, bf16[2,2,192,12...) custom-call(s32[1]{0:T(128)} %bitcast.me_ref, ...), custom_call_target="tpu_custom_call" | custom-call | flops 6442450944 | bytes 37748736 | tf_op jit(solution)/shard_map/beamform/pallas_call | solution.py:191
  31.4 1.3 collective-permute-start.15
  32.7 5.6 %collective-permute-start.14 = (s32[2,4,64]{2,1,0:T(4,128)S(1)}, s32[2,4,64]{2,1,0:T(4,128)S(1)}, u32[]{:S(2)}, u32[]{:S(2)}) collective-permute-start(s32[2,4,64]{2,1,0:T(4,128)S(1)} %get-tuple-element.128), channel_id=1, source_target_pairs={{0,8},{8,16},{16,24},{1,9},{9,17},{17,25},{2,10},{10,18},{18,26},{... | collective-permute-start | bytes 6152 | tf_op jit(solution)/shard_map/ppermute | solution.py:422
  38.2 2.2 %collective-permute-start.10 = (bf16[2,2,192,128]{3,2,1,0:T(8,128)(2,1)S(1)}, bf16[2,2,192,128]{3,2,1,0:T(8,128)(2,1)S(1)}, u32[]{:S(2)}, u32[]{:S(2)}) collective-permute-start(bf16[2,2,192,128]{3,2,1,0:T(8,128)(2,1)S(1)} %get-tuple-element.68), channel_id=1, source_target_pairs={{0,4},{1,5},{2,6},{3,7},{4,0},{5,1},{6,2},{7,3},{8,12},{9,13},{10,... | collective-permute-start | bytes 589832 | tf_op jit(solution)/shard_map/ppermute | solution.py:419
  40.4 1.5 collective-permute-start.12
  44.7 9.8 %collective-permute-done.10.refs_12_ = bf16[2,2,192,128]{3,2,1,0:T(8,128)(2,1)S(1)} collective-permute-done((bf16[2,2,192,128]{3,2,1,0:T(8,128)(2,1)S(1)}, bf16[2,2,192,128]{3,2,1,0:T(8,128)(2,1)S(1)}, u32[]{:S(2)}, u32[]{:S(2)}) %collective-permute-start.10) | collective-permute-done | bytes 196640 | tf_op jit(solution)/shard_map/ppermute | solution.py:419
  54.5 1.7 collective-permute-start.8
  58.6 1.6 collective-permute-start.1
  63.0 1.6 collective-permute-start.17
  64.6 6.8 %collective-permute-done.9.refs_11_ = bf16[2,2,192,128]{3,2,1,0:T(8,128)(2,1)S(1)} collective-permute-done((bf16[2,2,192,128]{3,2,1,0:T(8,128)(2,1)}, bf16[2,2,192,128]{3,2,1,0:T(8,128)(2,1)S(1)}, u32[]{:S(2)}, u32[]{:S(2)}) %collective-permute-start.9) | collective-permute-done | bytes 196640 | tf_op jit(solution)/shard_map/ppermute | solution.py:419
  72.1 1.8 %collective-permute-start.2 = (bf16[2,8,64,128]{3,2,1,0:T(8,128)(2,1)}, bf16[2,8,64,128]{3,2,1,0:T(8,128)(2,1)S(1)}, u32[]{:S(2)}, u32[]{:S(2)}) collective-permute-start(bf16[2,8,64,128]{3,2,1,0:T(8,128)(2,1)} %copy-done.34), channel_id=1, source_target_pairs={{0,3},{1,2},{2,1},{3,0},{4,7},{5,6},{6,5},{7,4},{8,11},{9,10},{10,... | collective-permute-start | bytes 786440 | tf_op jit(solution)/shard_map/ppermute | solution.py:419
  73.9 1.6 collective-permute-start.3
  76.5 2.7 %collective-permute-start.5 = (bf16[2,8,64,128]{3,2,1,0:T(8,128)(2,1)}, bf16[2,8,64,128]{3,2,1,0:T(8,128)(2,1)S(1)}, u32[]{:S(2)}, u32[]{:S(2)}) collective-permute-start(bf16[2,8,64,128]{3,2,1,0:T(8,128)(2,1)} %copy-done.31), channel_id=1, source_target_pairs={{0,6},{1,7},{2,4},{3,5},{4,2},{5,3},{6,0},{7,1},{8,14},{9,15},{10,... | collective-permute-start | bytes 786440 | tf_op jit(solution)/shard_map/ppermute | solution.py:419
  80.6 1.9 %collective-permute-start.18 = (bf16[2,2,192,128]{3,2,1,0:T(8,128)(2,1)}, bf16[2,2,192,128]{3,2,1,0:T(8,128)(2,1)S(1)}, u32[]{:S(2)}, u32[]{:S(2)}) collective-permute-start(bf16[2,2,192,128]{3,2,1,0:T(8,128)(2,1)} %copy-done.49), channel_id=1, source_target_pairs={{0,3},{1,2},{2,1},{3,0},{4,7},{5,6},{6,5},{7,4},{8,11},{9,10},{10,... | collective-permute-start | bytes 589832 | tf_op jit(solution)/shard_map/ppermute | solution.py:419
  82.5 11.9 %collective-permute-done.3.refs_4_ = bf16[2,8,64,128]{3,2,1,0:T(8,128)(2,1)S(1)} collective-permute-done((bf16[2,8,64,128]{3,2,1,0:T(8,128)(2,1)}, bf16[2,8,64,128]{3,2,1,0:T(8,128)(2,1)S(1)}, u32[]{:S(2)}, u32[]{:S(2)}) %collective-permute-start.3) | collective-permute-done | bytes 262176 | tf_op jit(solution)/shard_map/ppermute | solution.py:419
  94.4 1.4 collective-permute-start.19
  95.8 3.2 %collective-permute-done.4.refs_5_ = bf16[2,8,64,128]{3,2,1,0:T(8,128)(2,1)S(1)} collective-permute-done((bf16[2,8,64,128]{3,2,1,0:T(8,128)(2,1)}, bf16[2,8,64,128]{3,2,1,0:T(8,128)(2,1)S(1)}, u32[]{:S(2)}, u32[]{:S(2)}) %collective-permute-start.4) | collective-permute-done | bytes 262176 | tf_op jit(solution)/shard_map/ppermute | solution.py:419
  99.0 1.8 %collective-permute-start.20 = (bf16[2,2,192,128]{3,2,1,0:T(8,128)(2,1)}, bf16[2,2,192,128]{3,2,1,0:T(8,128)(2,1)S(1)}, u32[]{:S(2)}, u32[]{:S(2)}) collective-permute-start(bf16[2,2,192,128]{3,2,1,0:T(8,128)(2,1)} %copy-done.47), channel_id=1, source_target_pairs={{0,5},{1,4},{2,7},{3,6},{4,1},{5,0},{6,3},{7,2},{8,13},{9,12},{10,... | collective-permute-start | bytes 589832 | tf_op jit(solution)/shard_map/ppermute | solution.py:419
  109.6 6.6 %window_sums.4 = f32[8,1280]{1,0:T(8,128)S(1)} custom-call(s32[1]{0:T(128)} %bitcast.me_ref, bf16[2,8,64,128]{3,2,1,0:T(8,128)(2,1)S(1)} %get-tuple-element.55.refs_0_, bf16[2,8,64,128]{3,2,1,0:T(8,128)(2,1)S(1)} %collective-permute-done.refs_1_, bf16[2,8,64,128]{3,2,1,0:T(8,128)(2,1)S(1)} %collective-permute-done.1.refs_2_, ...), custom_call_target="tpu_custom_call" | custom-call | flops 1073741824 | bytes 6291456 | tf_op jit(solution)/shard_map/window_sums/pallas_call | solution.py:361
  116.2 1.8 %collective-permute-start.23 = (bf16[2,2,192,128]{3,2,1,0:T(8,128)(2,1)S(1)}, bf16[2,2,192,128]{3,2,1,0:T(8,128)(2,1)S(1)}, u32[]{:S(2)}, u32[]{:S(2)}) collective-permute-start(bf16[2,2,192,128]{3,2,1,0:T(8,128)(2,1)S(1)} %copy-done.44), channel_id=1, source_target_pairs={{0,1},{1,0},{2,3},{3,2},{4,5},{5,4},{6,7},{7,6},{8,9},{9,8},{10,11... | collective-permute-start | bytes 589832 | tf_op jit(solution)/shard_map/ppermute | solution.py:419
  120.1 1.4 collective-permute-start.27
  121.5 7.6 %window_sums.5 = f32[8,1280]{1,0:T(8,128)S(1)} custom-call(s32[1]{0:T(128)} %bitcast.me_ref, bf16[2,8,64,128]{3,2,1,0:T(8,128)(2,1)S(1)} %get-tuple-element.55.refs_0_, bf16[2,8,64,128]{3,2,1,0:T(8,128)(2,1)S(1)} %collective-permute-done.refs_1_, bf16[2,8,64,128]{3,2,1,0:T(8,128)(2,1)S(1)} %collective-permute-done.1.refs_2_, ...), custom_call_target="tpu_custom_call" | custom-call | flops 1073741824 | bytes 6291456 | tf_op jit(solution)/shard_map/window_sums/pallas_call | solution.py:361
  130.7 1.7 %collective-permute-start.29 = (bf16[2,2,192,128]{3,2,1,0:T(8,128)(2,1)}, bf16[2,2,192,128]{3,2,1,0:T(8,128)(2,1)S(1)}, u32[]{:S(2)}, u32[]{:S(2)}) collective-permute-start(bf16[2,2,192,128]{3,2,1,0:T(8,128)(2,1)} %copy-done.42), channel_id=1, source_target_pairs={{0,7},{1,6},{2,5},{3,4},{4,3},{5,2},{6,1},{7,0},{8,15},{9,14},{10,... | collective-permute-start | bytes 589832 | tf_op jit(solution)/shard_map/ppermute | solution.py:419
  134.0 3.5 %collective-permute-start.38 = (f32[2,4,64]{2,1,0:T(4,128)S(1)}, f32[2,4,64]{2,1,0:T(4,128)S(1)}, u32[]{:S(2)}, u32[]{:S(2)}) collective-permute-start(f32[2,4,64]{2,1,0:T(4,128)S(1)} %rev.13), channel_id=1, source_target_pairs={{0,8},{8,16},{16,24},{1,9},{9,17},{17,25},{2,10},{10,18},{18,26},{... | collective-permute-start | bytes 6152 | tf_op jit(solution)/shard_map/ppermute | solution.py:422
  137.5 1.4 collective-permute-done.28.refs_14_
  141.2 2.1 %collective-permute-start.32 = (bf16[2,2,192,128]{3,2,1,0:T(8,128)(2,1)}, bf16[2,2,192,128]{3,2,1,0:T(8,128)(2,1)S(1)}, u32[]{:S(2)}, u32[]{:S(2)}) collective-permute-start(bf16[2,2,192,128]{3,2,1,0:T(8,128)(2,1)} %copy-done.39), channel_id=1, source_target_pairs={{0,3},{1,2},{2,1},{3,0},{4,7},{5,6},{6,5},{7,4},{8,11},{9,10},{10,... | collective-permute-start | bytes 589832 | tf_op jit(solution)/shard_map/ppermute | solution.py:419
  143.7 2.5 %collective-permute-done.31.refs_10_ = bf16[2,2,192,128]{3,2,1,0:T(8,128)(2,1)S(1)} collective-permute-done((bf16[2,2,192,128]{3,2,1,0:T(8,128)(2,1)}, bf16[2,2,192,128]{3,2,1,0:T(8,128)(2,1)S(1)}, u32[]{:S(2)}, u32[]{:S(2)}) %collective-permute-start.31) | collective-permute-done | bytes 196640 | tf_op jit(solution)/shard_map/ppermute | solution.py:419
  146.2 1.9 %collective-permute-start.35 = (bf16[2,2,192,128]{3,2,1,0:T(8,128)(2,1)}, bf16[2,2,192,128]{3,2,1,0:T(8,128)(2,1)S(1)}, u32[]{:S(2)}, u32[]{:S(2)}) collective-permute-start(bf16[2,2,192,128]{3,2,1,0:T(8,128)(2,1)} %copy-done.36), channel_id=1, source_target_pairs={{0,6},{1,7},{2,4},{3,5},{4,2},{5,3},{6,0},{7,1},{8,14},{9,15},{10,... | collective-permute-start | bytes 589832 | tf_op jit(solution)/shard_map/ppermute | solution.py:419
  148.1 2.0 %collective-permute-start.36 = (bf16[2,2,192,128]{3,2,1,0:T(8,128)(2,1)}, bf16[2,2,192,128]{3,2,1,0:T(8,128)(2,1)S(1)}, u32[]{:S(2)}, u32[]{:S(2)}) collective-permute-start(bf16[2,2,192,128]{3,2,1,0:T(8,128)(2,1)} %copy-done.35), channel_id=1, source_target_pairs={{0,7},{1,6},{2,5},{3,4},{4,3},{5,2},{6,1},{7,0},{8,15},{9,14},{10,... | collective-permute-start | bytes 589832 | tf_op jit(solution)/shard_map/ppermute | solution.py:419
  154.9 7.9 %window_sums.6 = f32[8,1280]{1,0:T(8,128)S(1)} custom-call(s32[1]{0:T(128)} %bitcast.me_ref, bf16[2,8,64,128]{3,2,1,0:T(8,128)(2,1)S(1)} %get-tuple-element.55.refs_0_, bf16[2,8,64,128]{3,2,1,0:T(8,128)(2,1)S(1)} %collective-permute-done.refs_1_, bf16[2,8,64,128]{3,2,1,0:T(8,128)(2,1)S(1)} %collective-permute-done.1.refs_2_, ...), custom_call_target="tpu_custom_call" | custom-call | flops 1073741824 | bytes 6291456 | tf_op jit(solution)/shard_map/window_sums/pallas_call | solution.py:361
  162.8 6.6 %window_sums.7 = f32[8,1280]{1,0:T(8,128)S(1)} custom-call(s32[1]{0:T(128)} %bitcast.me_ref, bf16[2,8,64,128]{3,2,1,0:T(8,128)(2,1)S(1)} %get-tuple-element.55.refs_0_, bf16[2,8,64,128]{3,2,1,0:T(8,128)(2,1)S(1)} %collective-permute-done.refs_1_, bf16[2,8,64,128]{3,2,1,0:T(8,128)(2,1)S(1)} %collective-permute-done.1.refs_2_, ...), custom_call_target="tpu_custom_call" | custom-call | flops 1073741824 | bytes 6291456 | tf_op jit(solution)/shard_map/window_sums/pallas_call | solution.py:361
  (187 shorter events, 40.9 us)
Async XLA Ops:
  31.4 11.8 %collective-permute-start.15 = (s32[2,4,64]{2,1,0:T(4,128)S(1)}, s32[2,4,64]{2,1,0:T(4,128)S(1)}, u32[]{:S(2)}, u32[]{:S(2)}) collective-permute-start(s32[2,4,64]{2,1,0:T(4,128)S(1)} %get-tuple-element.129), channel_id=1, source_target_pairs={{8,0},{16,8},{24,16},{9,1},{17,9},{25,17},{10,2},{18,10},{26,18},{... | collective-permute-start | bytes 6152 | tf_op jit(solution)/shard_map/ppermute | solution.py:425
  32.7 11.7 %collective-permute-start.14 = (s32[2,4,64]{2,1,0:T(4,128)S(1)}, s32[2,4,64]{2,1,0:T(4,128)S(1)}, u32[]{:S(2)}, u32[]{:S(2)}) collective-permute-start(s32[2,4,64]{2,1,0:T(4,128)S(1)} %get-tuple-element.128), channel_id=1, source_target_pairs={{0,8},{8,16},{16,24},{1,9},{9,17},{17,25},{2,10},{10,18},{18,26},{... | collective-permute-start | bytes 6152 | tf_op jit(solution)/shard_map/ppermute | solution.py:422
  38.2 16.3 %collective-permute-start.10 = (bf16[2,2,192,128]{3,2,1,0:T(8,128)(2,1)S(1)}, bf16[2,2,192,128]{3,2,1,0:T(8,128)(2,1)S(1)}, u32[]{:S(2)}, u32[]{:S(2)}) collective-permute-start(bf16[2,2,192,128]{3,2,1,0:T(8,128)(2,1)S(1)} %get-tuple-element.68), channel_id=1, source_target_pairs={{0,4},{1,5},{2,6},{3,7},{4,0},{5,1},{6,2},{7,3},{8,12},{9,13},{10,... | collective-permute-start | bytes 589832 | tf_op jit(solution)/shard_map/ppermute | solution.py:419
  40.4 16.4 %collective-permute-start.11 = (bf16[2,2,192,128]{3,2,1,0:T(8,128)(2,1)S(1)}, bf16[2,2,192,128]{3,2,1,0:T(8,128)(2,1)S(1)}, u32[]{:S(2)}, u32[]{:S(2)}) collective-permute-start(bf16[2,2,192,128]{3,2,1,0:T(8,128)(2,1)S(1)} %get-tuple-element.69), channel_id=1, source_target_pairs={{0,5},{1,4},{2,7},{3,6},{4,1},{5,0},{6,3},{7,2},{8,13},{9,12},{10,... | collective-permute-start | bytes 589832 | tf_op jit(solution)/shard_map/ppermute | solution.py:419
  40.4 17.5 %collective-permute-start.12 = (bf16[2,2,192,128]{3,2,1,0:T(8,128)(2,1)S(1)}, bf16[2,2,192,128]{3,2,1,0:T(8,128)(2,1)S(1)}, u32[]{:S(2)}, u32[]{:S(2)}) collective-permute-start(bf16[2,2,192,128]{3,2,1,0:T(8,128)(2,1)S(1)} %get-tuple-element.70), channel_id=1, source_target_pairs={{0,6},{1,7},{2,4},{3,5},{4,2},{5,3},{6,0},{7,1},{8,14},{9,15},{10,... | collective-permute-start | bytes 589832 | tf_op jit(solution)/shard_map/ppermute | solution.py:419
  43.1 17.2 %collective-permute-start.13 = (bf16[2,2,192,128]{3,2,1,0:T(8,128)(2,1)}, bf16[2,2,192,128]{3,2,1,0:T(8,128)(2,1)S(1)}, u32[]{:S(2)}, u32[]{:S(2)}) collective-permute-start(bf16[2,2,192,128]{3,2,1,0:T(8,128)(2,1)} %get-tuple-element.71), channel_id=1, source_target_pairs={{0,7},{1,6},{2,5},{3,4},{4,3},{5,2},{6,1},{7,0},{8,15},{9,14},{10,... | collective-permute-start | bytes 589832 | tf_op jit(solution)/shard_map/ppermute | solution.py:419
  44.3 16.7 %collective-permute-start.7 = (bf16[2,2,192,128]{3,2,1,0:T(8,128)(2,1)}, bf16[2,2,192,128]{3,2,1,0:T(8,128)(2,1)S(1)}, u32[]{:S(2)}, u32[]{:S(2)}) collective-permute-start(bf16[2,2,192,128]{3,2,1,0:T(8,128)(2,1)} %get-tuple-element.65), channel_id=1, source_target_pairs={{0,1},{1,0},{2,3},{3,2},{4,5},{5,4},{6,7},{7,6},{8,9},{9,8},{10,11... | collective-permute-start | bytes 589832 | tf_op jit(solution)/shard_map/ppermute | solution.py:419
  57.5 19.0 %collective-permute-start = (bf16[2,8,64,128]{3,2,1,0:T(8,128)(2,1)}, bf16[2,8,64,128]{3,2,1,0:T(8,128)(2,1)S(1)}, u32[]{:S(2)}, u32[]{:S(2)}) collective-permute-start(bf16[2,8,64,128]{3,2,1,0:T(8,128)(2,1)} %get-tuple-element.56), channel_id=1, source_target_pairs={{0,1},{1,0},{2,3},{3,2},{4,5},{5,4},{6,7},{7,6},{8,9},{9,8},{10,11... | collective-permute-start | bytes 786440 | tf_op jit(solution)/shard_map/ppermute | solution.py:419
  58.6 20.6 %collective-permute-start.1 = (bf16[2,8,64,128]{3,2,1,0:T(8,128)(2,1)}, bf16[2,8,64,128]{3,2,1,0:T(8,128)(2,1)S(1)}, u32[]{:S(2)}, u32[]{:S(2)}) collective-permute-start(bf16[2,8,64,128]{3,2,1,0:T(8,128)(2,1)} %get-tuple-element.57), channel_id=1, source_target_pairs={{0,2},{1,3},{2,0},{3,1},{4,6},{5,7},{6,4},{7,5},{8,10},{9,11},{10,... | collective-permute-start | bytes 786440 | tf_op jit(solution)/shard_map/ppermute | solution.py:419
  61.7 12.2 %collective-permute-start.16 = (bf16[2,2,192,128]{3,2,1,0:T(8,128)(2,1)}, bf16[2,2,192,128]{3,2,1,0:T(8,128)(2,1)}, u32[]{:S(2)}, u32[]{:S(2)}) collective-permute-start(bf16[2,2,192,128]{3,2,1,0:T(8,128)(2,1)} %copy-done.51), channel_id=1, source_target_pairs={{0,1},{1,0},{2,3},{3,2},{4,5},{5,4},{6,7},{7,6},{8,9},{9,8},{10,11... | collective-permute-start | bytes 589832 | tf_op jit(solution)/shard_map/ppermute | solution.py:419
  63.0 12.9 %collective-permute-start.17 = (bf16[2,2,192,128]{3,2,1,0:T(8,128)(2,1)}, bf16[2,2,192,128]{3,2,1,0:T(8,128)(2,1)}, u32[]{:S(2)}, u32[]{:S(2)}) collective-permute-start(bf16[2,2,192,128]{3,2,1,0:T(8,128)(2,1)} %copy-done.50), channel_id=1, source_target_pairs={{0,2},{1,3},{2,0},{3,1},{4,6},{5,7},{6,4},{7,5},{8,10},{9,11},{10,... | collective-permute-start | bytes 589832 | tf_op jit(solution)/shard_map/ppermute | solution.py:419
  73.9 20.5 %collective-permute-start.3 = (bf16[2,8,64,128]{3,2,1,0:T(8,128)(2,1)}, bf16[2,8,64,128]{3,2,1,0:T(8,128)(2,1)S(1)}, u32[]{:S(2)}, u32[]{:S(2)}) collective-permute-start(bf16[2,8,64,128]{3,2,1,0:T(8,128)(2,1)} %copy-done.33), channel_id=1, source_target_pairs={{0,4},{1,5},{2,6},{3,7},{4,0},{5,1},{6,2},{7,3},{8,12},{9,13},{10,... | collective-permute-start | bytes 786440 | tf_op jit(solution)/shard_map/ppermute | solution.py:419
  75.9 23.2 %collective-permute-start.4 = (bf16[2,8,64,128]{3,2,1,0:T(8,128)(2,1)}, bf16[2,8,64,128]{3,2,1,0:T(8,128)(2,1)S(1)}, u32[]{:S(2)}, u32[]{:S(2)}) collective-permute-start(bf16[2,8,64,128]{3,2,1,0:T(8,128)(2,1)} %copy-done.32), channel_id=1, source_target_pairs={{0,5},{1,4},{2,7},{3,6},{4,1},{5,0},{6,3},{7,2},{8,13},{9,12},{10,... | collective-permute-start | bytes 786440 | tf_op jit(solution)/shard_map/ppermute | solution.py:419
  76.5 24.4 %collective-permute-start.5 = (bf16[2,8,64,128]{3,2,1,0:T(8,128)(2,1)}, bf16[2,8,64,128]{3,2,1,0:T(8,128)(2,1)S(1)}, u32[]{:S(2)}, u32[]{:S(2)}) collective-permute-start(bf16[2,8,64,128]{3,2,1,0:T(8,128)(2,1)} %copy-done.31), channel_id=1, source_target_pairs={{0,6},{1,7},{2,4},{3,5},{4,2},{5,3},{6,0},{7,1},{8,14},{9,15},{10,... | collective-permute-start | bytes 786440 | tf_op jit(solution)/shard_map/ppermute | solution.py:419
  79.2 22.3 %collective-permute-start.6 = (bf16[2,8,64,128]{3,2,1,0:T(8,128)(2,1)}, bf16[2,8,64,128]{3,2,1,0:T(8,128)(2,1)S(1)}, u32[]{:S(2)}, u32[]{:S(2)}) collective-permute-start(bf16[2,8,64,128]{3,2,1,0:T(8,128)(2,1)} %copy-done.30), channel_id=1, source_target_pairs={{0,7},{1,6},{2,5},{3,4},{4,3},{5,2},{6,1},{7,0},{8,15},{9,14},{10,... | collective-permute-start | bytes 786440 | tf_op jit(solution)/shard_map/ppermute | solution.py:419
  80.6 35.6 %collective-permute-start.18 = (bf16[2,2,192,128]{3,2,1,0:T(8,128)(2,1)}, bf16[2,2,192,128]{3,2,1,0:T(8,128)(2,1)S(1)}, u32[]{:S(2)}, u32[]{:S(2)}) collective-permute-start(bf16[2,2,192,128]{3,2,1,0:T(8,128)(2,1)} %copy-done.49), channel_id=1, source_target_pairs={{0,3},{1,2},{2,1},{3,0},{4,7},{5,6},{6,5},{7,4},{8,11},{9,10},{10,... | collective-permute-start | bytes 589832 | tf_op jit(solution)/shard_map/ppermute | solution.py:419
  94.4 23.6 %collective-permute-start.19 = (bf16[2,2,192,128]{3,2,1,0:T(8,128)(2,1)}, bf16[2,2,192,128]{3,2,1,0:T(8,128)(2,1)S(1)}, u32[]{:S(2)}, u32[]{:S(2)}) collective-permute-start(bf16[2,2,192,128]{3,2,1,0:T(8,128)(2,1)} %copy-done.48), channel_id=1, source_target_pairs={{0,4},{1,5},{2,6},{3,7},{4,0},{5,1},{6,2},{7,3},{8,12},{9,13},{10,... | collective-permute-start | bytes 589832 | tf_op jit(solution)/shard_map/ppermute | solution.py:419
  99.0 19.9 %collective-permute-start.20 = (bf16[2,2,192,128]{3,2,1,0:T(8,128)(2,1)}, bf16[2,2,192,128]{3,2,1,0:T(8,128)(2,1)S(1)}, u32[]{:S(2)}, u32[]{:S(2)}) collective-permute-start(bf16[2,2,192,128]{3,2,1,0:T(8,128)(2,1)} %copy-done.47), channel_id=1, source_target_pairs={{0,5},{1,4},{2,7},{3,6},{4,1},{5,0},{6,3},{7,2},{8,13},{9,12},{10,... | collective-permute-start | bytes 589832 | tf_op jit(solution)/shard_map/ppermute | solution.py:419
  100.8 18.6 %collective-permute-start.21 = (bf16[2,2,192,128]{3,2,1,0:T(8,128)(2,1)}, bf16[2,2,192,128]{3,2,1,0:T(8,128)(2,1)S(1)}, u32[]{:S(2)}, u32[]{:S(2)}) collective-permute-start(bf16[2,2,192,128]{3,2,1,0:T(8,128)(2,1)} %copy-done.46), channel_id=1, source_target_pairs={{0,6},{1,7},{2,4},{3,5},{4,2},{5,3},{6,0},{7,1},{8,14},{9,15},{10,... | collective-permute-start | bytes 589832 | tf_op jit(solution)/shard_map/ppermute | solution.py:419
  101.5 18.6 %collective-permute-start.22 = (bf16[2,2,192,128]{3,2,1,0:T(8,128)(2,1)}, bf16[2,2,192,128]{3,2,1,0:T(8,128)(2,1)S(1)}, u32[]{:S(2)}, u32[]{:S(2)}) collective-permute-start(bf16[2,2,192,128]{3,2,1,0:T(8,128)(2,1)} %copy-done.45), channel_id=1, source_target_pairs={{0,7},{1,6},{2,5},{3,4},{4,3},{5,2},{6,1},{7,0},{8,15},{9,14},{10,... | collective-permute-start | bytes 589832 | tf_op jit(solution)/shard_map/ppermute | solution.py:419
  116.2 13.0 %collective-permute-start.23 = (bf16[2,2,192,128]{3,2,1,0:T(8,128)(2,1)S(1)}, bf16[2,2,192,128]{3,2,1,0:T(8,128)(2,1)S(1)}, u32[]{:S(2)}, u32[]{:S(2)}) collective-permute-start(bf16[2,2,192,128]{3,2,1,0:T(8,128)(2,1)S(1)} %copy-done.44), channel_id=1, source_target_pairs={{0,1},{1,0},{2,3},{3,2},{4,5},{5,4},{6,7},{7,6},{8,9},{9,8},{10,11... | collective-permute-start | bytes 589832 | tf_op jit(solution)/shard_map/ppermute | solution.py:419
  118.0 12.7 %collective-permute-start.24 = (bf16[2,2,192,128]{3,2,1,0:T(8,128)(2,1)}, bf16[2,2,192,128]{3,2,1,0:T(8,128)(2,1)}, u32[]{:S(2)}, u32[]{:S(2)}) collective-permute-start(bf16[2,2,192,128]{3,2,1,0:T(8,128)(2,1)} %get-tuple-element.91), channel_id=1, source_target_pairs={{0,2},{1,3},{2,0},{3,1},{4,6},{5,7},{6,4},{7,5},{8,10},{9,11},{10,... | collective-permute-start | bytes 589832 | tf_op jit(solution)/shard_map/ppermute | solution.py:419
  118.9 13.5 %collective-permute-start.25 = (bf16[2,2,192,128]{3,2,1,0:T(8,128)(2,1)}, bf16[2,2,192,128]{3,2,1,0:T(8,128)(2,1)}, u32[]{:S(2)}, u32[]{:S(2)}) collective-permute-start(bf16[2,2,192,128]{3,2,1,0:T(8,128)(2,1)} %get-tuple-element.92), channel_id=1, source_target_pairs={{0,3},{1,2},{2,1},{3,0},{4,7},{5,6},{6,5},{7,4},{8,11},{9,10},{10,... | collective-permute-start | bytes 589832 | tf_op jit(solution)/shard_map/ppermute | solution.py:419
  119.5 13.7 %collective-permute-start.26 = (bf16[2,2,192,128]{3,2,1,0:T(8,128)(2,1)}, bf16[2,2,192,128]{3,2,1,0:T(8,128)(2,1)}, u32[]{:S(2)}, u32[]{:S(2)}) collective-permute-start(bf16[2,2,192,128]{3,2,1,0:T(8,128)(2,1)} %get-tuple-element.93), channel_id=1, source_target_pairs={{0,4},{1,5},{2,6},{3,7},{4,0},{5,1},{6,2},{7,3},{8,12},{9,13},{10,... | collective-permute-start | bytes 589832 | tf_op jit(solution)/shard_map/ppermute | solution.py:419
  120.1 13.9 %collective-permute-start.27 = (bf16[2,2,192,128]{3,2,1,0:T(8,128)(2,1)}, bf16[2,2,192,128]{3,2,1,0:T(8,128)(2,1)}, u32[]{:S(2)}, u32[]{:S(2)}) collective-permute-start(bf16[2,2,192,128]{3,2,1,0:T(8,128)(2,1)} %get-tuple-element.94), channel_id=1, source_target_pairs={{0,5},{1,4},{2,7},{3,6},{4,1},{5,0},{6,3},{7,2},{8,13},{9,12},{10,... | collective-permute-start | bytes 589832 | tf_op jit(solution)/shard_map/ppermute | solution.py:419
  133.1 13.1 %collective-permute-start.31 = (bf16[2,2,192,128]{3,2,1,0:T(8,128)(2,1)}, bf16[2,2,192,128]{3,2,1,0:T(8,128)(2,1)S(1)}, u32[]{:S(2)}, u32[]{:S(2)}) collective-permute-start(bf16[2,2,192,128]{3,2,1,0:T(8,128)(2,1)} %copy-done.40), channel_id=1, source_target_pairs={{0,2},{1,3},{2,0},{3,1},{4,6},{5,7},{6,4},{7,5},{8,10},{9,11},{10,... | collective-permute-start | bytes 589832 | tf_op jit(solution)/shard_map/ppermute | solution.py:419
  134.0 12.2 %collective-permute-start.38 = (f32[2,4,64]{2,1,0:T(4,128)S(1)}, f32[2,4,64]{2,1,0:T(4,128)S(1)}, u32[]{:S(2)}, u32[]{:S(2)}) collective-permute-start(f32[2,4,64]{2,1,0:T(4,128)S(1)} %rev.13), channel_id=1, source_target_pairs={{0,8},{8,16},{16,24},{1,9},{9,17},{17,25},{2,10},{10,18},{18,26},{... | collective-permute-start | bytes 6152 | tf_op jit(solution)/shard_map/ppermute | solution.py:422
  141.2 21.5 %collective-permute-start.32 = (bf16[2,2,192,128]{3,2,1,0:T(8,128)(2,1)}, bf16[2,2,192,128]{3,2,1,0:T(8,128)(2,1)S(1)}, u32[]{:S(2)}, u32[]{:S(2)}) collective-permute-start(bf16[2,2,192,128]{3,2,1,0:T(8,128)(2,1)} %copy-done.39), channel_id=1, source_target_pairs={{0,3},{1,2},{2,1},{3,0},{4,7},{5,6},{6,5},{7,4},{8,11},{9,10},{10,... | collective-permute-start | bytes 589832 | tf_op jit(solution)/shard_map/ppermute | solution.py:419
  143.3 19.4 %collective-permute-start.33 = (bf16[2,2,192,128]{3,2,1,0:T(8,128)(2,1)}, bf16[2,2,192,128]{3,2,1,0:T(8,128)(2,1)S(1)}, u32[]{:S(2)}, u32[]{:S(2)}) collective-permute-start(bf16[2,2,192,128]{3,2,1,0:T(8,128)(2,1)} %copy-done.38), channel_id=1, source_target_pairs={{0,4},{1,5},{2,6},{3,7},{4,0},{5,1},{6,2},{7,3},{8,12},{9,13},{10,... | collective-permute-start | bytes 589832 | tf_op jit(solution)/shard_map/ppermute | solution.py:419
  146.2 16.6 %collective-permute-start.34 = (bf16[2,2,192,128]{3,2,1,0:T(8,128)(2,1)}, bf16[2,2,192,128]{3,2,1,0:T(8,128)(2,1)S(1)}, u32[]{:S(2)}, u32[]{:S(2)}) collective-permute-start(bf16[2,2,192,128]{3,2,1,0:T(8,128)(2,1)} %copy-done.37), channel_id=1, source_target_pairs={{0,5},{1,4},{2,7},{3,6},{4,1},{5,0},{6,3},{7,2},{8,13},{9,12},{10,... | collective-permute-start | bytes 589832 | tf_op jit(solution)/shard_map/ppermute | solution.py:419
  146.2 16.6 %collective-permute-start.35 = (bf16[2,2,192,128]{3,2,1,0:T(8,128)(2,1)}, bf16[2,2,192,128]{3,2,1,0:T(8,128)(2,1)S(1)}, u32[]{:S(2)}, u32[]{:S(2)}) collective-permute-start(bf16[2,2,192,128]{3,2,1,0:T(8,128)(2,1)} %copy-done.36), channel_id=1, source_target_pairs={{0,6},{1,7},{2,4},{3,5},{4,2},{5,3},{6,0},{7,1},{8,14},{9,15},{10,... | collective-permute-start | bytes 589832 | tf_op jit(solution)/shard_map/ppermute | solution.py:419
  148.1 14.7 %collective-permute-start.36 = (bf16[2,2,192,128]{3,2,1,0:T(8,128)(2,1)}, bf16[2,2,192,128]{3,2,1,0:T(8,128)(2,1)S(1)}, u32[]{:S(2)}, u32[]{:S(2)}) collective-permute-start(bf16[2,2,192,128]{3,2,1,0:T(8,128)(2,1)} %copy-done.35), channel_id=1, source_target_pairs={{0,7},{1,6},{2,5},{3,4},{4,3},{5,2},{6,1},{7,0},{8,15},{9,14},{10,... | collective-permute-start | bytes 589832 | tf_op jit(solution)/shard_map/ppermute | solution.py:419
  (62 other events, 657.1 us)

commit v2 on v1

--- a/solution.py
+++ b/solution.py
@@ -16,6 +16,7 @@
 BLOCK = 16
 HEAD_STEPS = 4
 STEP_BANDS = 2
+SPLITS = (4, 2, 2)
 
 
 def extended(array, sides, width):
@@ -153,7 +154,6 @@
     for k in range(0, bands, 2):
         pair = [spectra(k), spectra(k + 1)]
         here = slice(k * bins, (k + 2) * bins)
-        there = pl.ds(pl.multiple_of((step * bands + k) * bins, 2 * bins), 2 * bins)
         for near in range(0, count, 2 * PAIR):
             groups = []
             for r in (near, near + PAIR):
@@ -170,9 +170,12 @@
                         first = jnp.where(lower, one, pltpu.roll(two, LANES // PAIR, 1))
                         second = jnp.where(lower, pltpu.roll(one, LANES // PAIR, 1), two)
                         first, second = first.astype(jnp.bfloat16), second.astype(jnp.bfloat16)
-                        to = here if r == 0 else there
-                        outs[i * count + r][which, at, to, :] = jnp.where(swap, second, first)
-                        outs[i * count + r + 1][which, at, there, :] = jnp.where(swap, first, second)
+                        outs[i * count + r][which, at, here] = jnp.where(swap, second, first)
+                        outs[i * count + r + 1][which, at, here] = jnp.where(swap, first, second)
+
+
+def in_place(array):
+    return pltpu.with_memory_space_constraint(array, pltpu.HBM)
 
 
 def beamform(me, staves, weights, replica, count, first_band, steps, bands, splits):
@@ -182,7 +185,7 @@
     skip = first_band // bands
     rows = bands * bins
     shapes = [
-        jax.ShapeDtypeStruct((2, size, steps * rows, LANES), jnp.bfloat16)
+        pltpu.HBM((2, size, steps * rows, LANES), jnp.bfloat16)
         for size in splits
         for _ in range(count)
     ]
@@ -200,17 +203,15 @@
             ],
             out_specs=[
                 pl.BlockSpec((2, size, rows, LANES), lambda s, me: (0, 0, s, 0))
-                if r == 0
-                else pl.BlockSpec(memory_space=pltpu.VMEM)
                 for size in splits
-                for r in range(count)
+                for _ in range(count)
             ],
         ),
         out_shape=shapes,
         compiler_params=pltpu.CompilerParams(vmem_limit_bytes=24 << 20),
         cost_estimate=pl.CostEstimate(flops=flops, bytes_accessed=moved, transcendentals=0),
         name="beamform",
-    )(me, *(pltpu.with_memory_space_constraint(a, pltpu.HBM) for a in (staves, weights, replica)))
+    )(me, in_place(staves), in_place(weights), in_place(replica))
 
 
 def add(a, b):
@@ -250,11 +251,27 @@
     return [even[i // 2] if i % 2 == 0 else odd[i // 2] for i in range(count)]
 
 
-def turned_kernel(me_ref, *refs, count, width, together):
+def five_wide(values):
+    known = {}
+
+    def run(first, size):
+        if size == 1:
+            return values[first]
+        if (first, size) not in known:
+            part = 1 << (size - 1).bit_length() - 1
+            known[first, size] = run(first, part) + run(first + part, size - part)
+        return known[first, size]
+
+    count = len(values)
+    ends = [(max(0, i - REACH), min(count, i + 1)) for i in range(count + REACH)]
+    return [run(first, last - first) for first, last in ends]
+
+
+def turned_kernel(me_ref, *refs, count, slots, together):
     heads, tails = refs[:count], refs[count : 2 * count]
     cos_ref, sin_ref, window_ref, out_ref, spec, power, kept, acc = refs[2 * count :]
     step = pl.program_id(0)
-    slots = 2
+    width = 2 * REACH + slots
     head_rows, tail_rows = heads[0].shape[2], tails[0].shape[2]
     depth = head_rows + tail_rows
     signs = [
@@ -292,44 +309,26 @@
         table = jnp.concatenate(
             [jnp.concatenate([cos, -sin], axis=1), jnp.concatenate([sin, cos], axis=1)], axis=0
         )
-        spectra = jnp.concatenate([spec[m, 0], spec[m, 1]], axis=1)
-        wave = jnp.dot(table, spectra, preferred_element_type=jnp.float32)
-        power[j] = wave[:depth] * wave[:depth] + wave[depth:] * wave[depth:]
-
-    shift = count.bit_length() - 1
+        for slot in range(0, slots, 2):
+            spectra = jnp.concatenate([spec[m, slot], spec[m, slot + 1]], axis=1)
+            wave = jnp.dot(table, spectra, preferred_element_type=jnp.float32)
+            lanes = slice(slot * LANES, (slot + 2) * LANES)
+            power[j, :, lanes] = wave[:depth] * wave[:depth] + wave[depth:] * wave[depth:]
+
     first_row = lax.broadcasted_iota(jnp.int32, (BLOCK, LANES), 0)
     for j in range(together):
-        m = step * together + j
-        edges = [
-            [
-                jnp.broadcast_to(
-                    lax.shift_right_arithmetic(window_ref[i, o : o + 1, :] + (count - 1 - m), shift)
-                    .astype(jnp.float32)
-                    .astype(jnp.bfloat16),
-                    (BLOCK, LANES),
-                )
-                for o in range(width)
-            ]
-            for i in range(2)
-        ]
 
         def windowed(i, carry):
             row = pl.multiple_of(i * BLOCK, BLOCK)
-            one = power[j, pl.ds(row, BLOCK), :LANES]
-            two = power[j, pl.ds(row, BLOCK), LANES:]
-            both = one + two
             rows = (first_row + row).astype(jnp.float32).astype(jnp.bfloat16)
-
-            def keep(o, value):
-                inside = (rows >= edges[0][o]) & (rows < edges[1][o])
+            values = [
+                power[j, pl.ds(row, BLOCK), slot * LANES : (slot + 1) * LANES]
+                for slot in range(slots)
+            ]
+            for o, value in enumerate(five_wide(five_wide(values))):
+                inside = (rows >= window_ref[j, 0, o]) & (rows < window_ref[j, 1, o])
                 value = jnp.where(inside, value.astype(jnp.bfloat16), jnp.bfloat16(0))
                 kept[j, o, pl.ds(row, BLOCK), :] = value
-
-            for o in range(REACH + 1):
-                keep(o, one)
-                keep(width - 1 - o, two)
-                if o < REACH:
-                    one, two = one + both, two + both
             return carry
 
         lax.fori_loop(0, depth // BLOCK, windowed, 0, unroll=2)
@@ -350,42 +349,44 @@
         out_ref[...] = acc[...]
 
 
-def window_sums(me, heads, tails, tables, windows, chunk):
+def window_sums(me, heads, tails, tables, windows, first_slot):
     count = len(heads)
-    width = 2 * REACH + 2
+    slots = tails[0].shape[1]
+    chunk = first_slot // slots
+    width = 2 * REACH + slots
     together = 2
     head_rows, tail_rows = heads[0].shape[2], tails[0].shape[2]
     depth = head_rows + tail_rows
-    flops = 2 * count * (2 * depth) * (2 * depth) * (2 * LANES)
+    flops = 2 * count * (2 * depth) * (2 * depth) * (slots * LANES)
     moved = 4 * tables[0].size + 16 * count * depth * LANES
     sums = pl.pallas_call(
-        functools.partial(turned_kernel, count=count, width=width, together=together),
+        functools.partial(turned_kernel, count=count, slots=slots, together=together),
         grid_spec=pltpu.PrefetchScalarGridSpec(
             num_scalar_prefetch=1,
             grid=(count // together,),
             in_specs=[
-                pl.BlockSpec((2, 2, head_rows, LANES), lambda s, me: (0, chunk, 0, 0))
+                pl.BlockSpec((2, slots, head_rows, LANES), lambda s, me: (0, chunk, 0, 0))
                 for _ in range(count)
             ]
             + [
-                pl.BlockSpec((2, 2, tail_rows, LANES), lambda s, me: (0, 0, 0, 0))
+                pl.BlockSpec((2, slots, tail_rows, LANES), lambda s, me: (0, 0, 0, 0))
                 for _ in range(count)
             ]
             + [pl.BlockSpec((together, depth, depth), lambda s, me: (s, 0, 0)) for _ in range(2)]
-            + [pl.BlockSpec((2, width, LANES), lambda s, me: (0, 0, 0))],
+            + [pl.BlockSpec((together, 2, width, BLOCK, LANES), lambda s, me: (s, 0, 0, 0, 0))],
             out_specs=pl.BlockSpec((8, width * LANES), lambda s, me: (0, 0)),
             scratch_shapes=[
-                pltpu.VMEM((count, 2, 2 * depth, LANES), jnp.bfloat16),
-                pltpu.VMEM((together, depth, 2 * LANES), jnp.float32),
+                pltpu.VMEM((count, slots, 2 * depth, LANES), jnp.bfloat16),
+                pltpu.VMEM((together, depth, slots * LANES), jnp.float32),
                 pltpu.VMEM((together, width, depth, LANES), jnp.bfloat16),
                 pltpu.VMEM((8, width * LANES), jnp.float32),
             ],
         ),
         out_shape=jax.ShapeDtypeStruct((8, width * LANES), jnp.float32),
-        compiler_params=pltpu.CompilerParams(vmem_limit_bytes=14 << 20),
+        compiler_params=pltpu.CompilerParams(vmem_limit_bytes=(6 + 4 * slots) << 20),
         cost_estimate=pl.CostEstimate(flops=flops, bytes_accessed=moved, transcendentals=0),
         name="window_sums",
-    )(me, *heads, *tails, *tables, windows)
+    )(me, in_place(heads[0]), *heads[1:], in_place(tails[0]), *tails[1:], *tables, windows)
     return jnp.stack([sums[0], sums[1] + sums[2]]).reshape(2, width, LANES)
 
 
@@ -411,7 +412,7 @@
     block = lax.axis_index("ping")
     pings, bands, bins = staves.shape[1:4]
     half = pings // PAIR
-    chunks = half // 2
+    sizes = SPLITS
     depth = bands * bins
     mine = start.shape[1]
 
@@ -431,10 +432,10 @@
     rest = (bands - head_bands) // (2 * STEP_BANDS)
     me_next, _ = lax.optimization_barrier((me, heads[0]))
     tails = beamform(
-        me_next, staves, weights, replica, count, head_bands, rest, 2 * STEP_BANDS, (2,) * chunks
+        me_next, staves, weights, replica, count, head_bands, rest, 2 * STEP_BANDS, sizes
     )
     got_tails = []
-    for i in range(chunks):
+    for i in range(len(sizes)):
         own = tails[i * count : (i + 1) * count]
         got_tails.append([own[0]] + [send(own[r], r) for r in range(1, count)])
 
@@ -446,23 +447,26 @@
     left = jnp.concatenate([before, spans[:, :reach]], axis=1)
     right = jnp.concatenate([spans[:, pings - reach :], after], axis=1)
     windows = jnp.concatenate([left, jnp.flip(right, 1)], axis=2)
+    phase = jnp.arange(count, dtype=jnp.int32)[:, None, None, None]
+    windows = lax.div(windows[None] + (count - 1 - phase), count).astype(jnp.bfloat16)
+    windows = jnp.broadcast_to(
+        windows[:, :, :, None, :], windows.shape[:3] + (BLOCK, windows.shape[3])
+    )
 
     tables = wave_tables(count, depth, tails[0])
 
-    width = 2 * REACH + 2
     reached = half + 2 * REACH
     sums = jnp.zeros((2, reached, LANES), jnp.float32)
-    for i in range(chunks):
-        reached_windows = windows[:, 2 * i : 2 * i + width]
-        if i == chunks - 1:
-            reached_windows, edge_left, edge_right = lax.optimization_barrier(
-                (reached_windows, edge_left, edge_right)
-            )
-        part = window_sums(me, got_heads, got_tails[i], tables, reached_windows, i)
-        sums = sums + jnp.pad(part, ((0, 0), (2 * i, reached - width - 2 * i), (0, 0)))
-        if 2 * (i + 1) == REACH:
+    slot = 0
+    for i, size in enumerate(sizes):
+        width = 2 * REACH + size
+        near = windows[:, :, slot : slot + width]
+        part = window_sums(me, got_heads, got_tails[i], tables, near, slot)
+        sums = sums + jnp.pad(part, ((0, 0), (slot, reached - width - slot), (0, 0)))
+        if slot < REACH <= slot + size:
             edge_left = down(sums[:, :REACH, :mine])
             edge_right = up(jnp.flip(sums[:, :REACH, mine:], 1))
+        slot += size
 
     def placed(array, before):
         after = pings - before - array.shape[1]
@@ -492,7 +496,7 @@
         and beams * PAIR == LANES * count
         and beams % (2 * LANES) == 0
         and pings % (2 * PAIR) == 0
-        and half > REACH
+        and half == sum(SPLITS)
         and bins == 8
         and depth % LANES == 0
         and bands * bins % LANES == 0

time: 171 us -> 163 us (0.953)
  waiting for transfers between devices: 37.4 us -> 48.3 us
  starting transfers between devices: 52.7 us -> 41.9 us
  local copies, waits for them, and re-layouts: 24.8 us -> 14 us
  other arithmetic: 2.83 us -> 7.2 us
    unnamed x110 -> x54, local copies, waits for them, and re-layouts: 24.5 us -> 12.2 us
    ppermute x35 -> x28, starting transfers between devices: 41 us -> 30.3 us  [send(): return lax.ppermute(array, 'band', [(i, i ^ r) for i in range(count)])]
    ppermute x35 -> x28, waiting for transfers between devices: 37.4 us -> 44.2 us  [send(): return lax.ppermute(array, 'band', [(i, i ^ r) for i in range(count)])]
    ppermute x2, waiting for transfers between devices: 0.01 us -> 4.08 us  [down(): return lax.ppermute(array, 'ping', [(i + 1, i) for i in range(blocks - 1)])]
    pallas_call x4 -> x3, Pallas kernels: 28.6 us -> 25.6 us  [window_sums(): pl.pallas_call(functools.partial(turned_kernel, count=count, slots=slots,...]
  transfers between devices with their start and end apart: 39 -> 32, of which waited for: 9 -> 10; matrix products, arithmetic and copies ran while one was open for 1% -> 5% of each run, Pallas kernels for 13% -> 9%
where the time goes in v2:
time: 163 us; the launch traced here: 162 us
  Pallas kernels  49.8 us (31%)
  waiting for transfers between devices  48.3 us (30%)
  starting transfers between devices  41.9 us (26%)
  local copies, waits for them, and re-layouts  14 us (9%)
  other arithmetic  7.2 us (4%)
    ppermute x28, waiting for transfers between devices, send(): return lax.ppermute(array, 'band', [(i, i ^ r) for i in range(count)])  44.2 us
    ppermute x28, starting transfers between devices, send(): return lax.ppermute(array, 'band', [(i, i ^ r) for i in range(count)])  30.3 us
    pallas_call x3, Pallas kernels, window_sums(): pl.pallas_call(functools.partial(turned_kernel, count=count, slots=slots,...  25.6 us
    pallas_call x2, Pallas kernels, beamform(): pl.pallas_call(functools.partial(beam_kernel, count=count, first_band=fir...  24.2 us
    unnamed x54, local copies, waits for them, and re-layouts  12.2 us
    ppermute x2, starting transfers between devices, up(): return lax.ppermute(array, 'ping', [(i, i + 1) for i in range(blocks - 1)])  8.95 us
    ppermute x2, waiting for transfers between devices, down(): return lax.ppermute(array, 'ping', [(i + 1, i) for i in range(blocks - 1)])  4.08 us
  transfers between devices with their start and end apart: 32, of which 10 were waited for; matrix products, arithmetic and copies ran while one was open for 5% of the time, Pallas kernels for 9%

profile of v2, /device:TPU:0, one launch (start us, length us, event | category | flops | bytes accessed | tf_op | source)
XLA Modules:
  0.0 162.1 jit_solution(17363691224987107376)
XLA Ops:
  0.6 7.6 %beamform.2 = (bf16[2,8,64,128]{3,2,1,0:T(8,128)(2,1)}, bf16[2,8,64,128]{3,2,1,0:T(8,128)(2,1)}, bf16[2,8,64,128]{3,2,1,0:T(8,128)(2,1)}, bf16[2,8,64,128]{3,2,1...) custom-call(s32[1]{0:T(128)} %bitcast.me_ref, ...), custom_call_target="tpu_custom_call" | custom-call | flops 2147483648 | bytes 12582912 | tf_op jit(solution)/shard_map/beamform/pallas_call | solution.py:194
  8.3 16.6 %beamform.3 = (bf16[2,4,192,128]{3,2,1,0:T(8,128)(2,1)}, bf16[2,4,192,128]{3,2,1,0:T(8,128)(2,1)}, bf16[2,4,192,128]{3,2,1,0:T(8,128)(2,1)}, bf16[2,4,192,128]{3...) custom-call(s32[1]{0:T(128)} %bitcast.me_ref, ...), custom_call_target="tpu_custom_call" | custom-call | flops 6442450944 | bytes 37748736 | tf_op jit(solution)/shard_map/beamform/pallas_call | solution.py:194
  24.9 1.3 collective-permute-start.15
  26.2 5.6 %collective-permute-start.14 = (s32[2,4,64]{2,1,0:T(4,128)S(1)}, s32[2,4,64]{2,1,0:T(4,128)S(1)}, u32[]{:S(2)}, u32[]{:S(2)}) collective-permute-start(s32[2,4,64]{2,1,0:T(4,128)S(1)} %get-tuple-element.102), channel_id=1, source_target_pairs={{0,8},{8,16},{16,24},{1,9},{9,17},{17,25},{2,10},{10,18},{18,26},{... | collective-permute-start | bytes 6152 | tf_op jit(solution)/shard_map/ppermute | solution.py:423
  31.9 2.0 %collective-permute-start.24 = (bf16[2,2,192,128]{3,2,1,0:T(8,128)(2,1)}, bf16[2,2,192,128]{3,2,1,0:T(8,128)(2,1)S(1)}, u32[]{:S(2)}, u32[]{:S(2)}) collective-permute-start(bf16[2,2,192,128]{3,2,1,0:T(8,128)(2,1)} %get-tuple-element.80), channel_id=1, source_target_pairs={{0,2},{1,3},{2,0},{3,1},{4,6},{5,7},{6,4},{7,5},{8,10},{9,11},{10,... | collective-permute-start | bytes 589832 | tf_op jit(solution)/shard_map/ppermute | solution.py:420
  35.1 1.9 %collective-permute-start.26 = (bf16[2,2,192,128]{3,2,1,0:T(8,128)(2,1)}, bf16[2,2,192,128]{3,2,1,0:T(8,128)(2,1)S(1)}, u32[]{:S(2)}, u32[]{:S(2)}) collective-permute-start(bf16[2,2,192,128]{3,2,1,0:T(8,128)(2,1)} %get-tuple-element.82), channel_id=1, source_target_pairs={{0,4},{1,5},{2,6},{3,7},{4,0},{5,1},{6,2},{7,3},{8,12},{9,13},{10,... | collective-permute-start | bytes 589832 | tf_op jit(solution)/shard_map/ppermute | solution.py:420
  37.0 2.6 %collective-permute-start.28 = (bf16[2,2,192,128]{3,2,1,0:T(8,128)(2,1)}, bf16[2,2,192,128]{3,2,1,0:T(8,128)(2,1)S(1)}, u32[]{:S(2)}, u32[]{:S(2)}) collective-permute-start(bf16[2,2,192,128]{3,2,1,0:T(8,128)(2,1)} %get-tuple-element.84), channel_id=1, source_target_pairs={{0,6},{1,7},{2,4},{3,5},{4,2},{5,3},{6,0},{7,1},{8,14},{9,15},{10,... | collective-permute-start | bytes 589832 | tf_op jit(solution)/shard_map/ppermute | solution.py:420
  39.9 1.6 collective-permute-start.29
  42.1 1.6 collective-permute-done.25.refs_11_
  45.6 2.0 %collective-permute-start.17 = (bf16[2,2,192,128]{3,2,1,0:T(8,128)(2,1)}, bf16[2,2,192,128]{3,2,1,0:T(8,128)(2,1)S(1)}, u32[]{:S(2)}, u32[]{:S(2)}) collective-permute-start(bf16[2,2,192,128]{3,2,1,0:T(8,128)(2,1)} %get-tuple-element.72), channel_id=1, source_target_pairs={{0,2},{1,3},{2,0},{3,1},{4,6},{5,7},{6,4},{7,5},{8,10},{9,11},{10,... | collective-permute-start | bytes 589832 | tf_op jit(solution)/shard_map/ppermute | solution.py:420
  47.6 7.1 %collective-permute-done.27.refs_13_ = bf16[2,2,192,128]{3,2,1,0:T(8,128)(2,1)S(1)} collective-permute-done((bf16[2,2,192,128]{3,2,1,0:T(8,128)(2,1)}, bf16[2,2,192,128]{3,2,1,0:T(8,128)(2,1)S(1)}, u32[]{:S(2)}, u32[]{:S(2)}) %collective-permute-start.27) | collective-permute-done | bytes 196640 | tf_op jit(solution)/shard_map/ppermute | solution.py:420
  55.4 2.0 %collective-permute-start.18 = (bf16[2,2,192,128]{3,2,1,0:T(8,128)(2,1)}, bf16[2,2,192,128]{3,2,1,0:T(8,128)(2,1)S(1)}, u32[]{:S(2)}, u32[]{:S(2)}) collective-permute-start(bf16[2,2,192,128]{3,2,1,0:T(8,128)(2,1)} %get-tuple-element.73), channel_id=1, source_target_pairs={{0,3},{1,2},{2,1},{3,0},{4,7},{5,6},{6,5},{7,4},{8,11},{9,10},{10,... | collective-permute-start | bytes 589832 | tf_op jit(solution)/shard_map/ppermute | solution.py:420
  58.0 1.5 collective-permute-start.19
  65.4 1.5 collective-permute-start.1
  66.8 3.2 %collective-permute-done.19.refs_12_ = bf16[2,2,192,128]{3,2,1,0:T(8,128)(2,1)S(1)} collective-permute-done((bf16[2,2,192,128]{3,2,1,0:T(8,128)(2,1)}, bf16[2,2,192,128]{3,2,1,0:T(8,128)(2,1)S(1)}, u32[]{:S(2)}, u32[]{:S(2)}) %collective-permute-start.19) | collective-permute-done | bytes 196640 | tf_op jit(solution)/shard_map/ppermute | solution.py:420
  70.7 1.7 %collective-permute-done.20.refs_13_ = bf16[2,2,192,128]{3,2,1,0:T(8,128)(2,1)S(1)} collective-permute-done((bf16[2,2,192,128]{3,2,1,0:T(8,128)(2,1)}, bf16[2,2,192,128]{3,2,1,0:T(8,128)(2,1)S(1)}, u32[]{:S(2)}, u32[]{:S(2)}) %collective-permute-start.20) | collective-permute-done | bytes 196640 | tf_op jit(solution)/shard_map/ppermute | solution.py:420
  73.1 1.2 collective-permute-start.3
  76.7 1.3 pad_add_fusion
  78.0 1.3 rev.12
  80.1 5.3 %collective-permute-done.22.refs_15_ = bf16[2,2,192,128]{3,2,1,0:T(8,128)(2,1)} collective-permute-done((bf16[2,2,192,128]{3,2,1,0:T(8,128)(2,1)}, bf16[2,2,192,128]{3,2,1,0:T(8,128)(2,1)}, u32[]{:S(2)}, u32[]{:S(2)}) %collective-permute-start.22) | collective-permute-done | bytes 196640 | tf_op jit(solution)/shard_map/ppermute | solution.py:420
  85.4 1.5 collective-permute-start.4
  87.2 2.4 %collective-permute-start.6 = (bf16[2,8,64,128]{3,2,1,0:T(8,128)(2,1)}, bf16[2,8,64,128]{3,2,1,0:T(8,128)(2,1)S(1)}, u32[]{:S(2)}, u32[]{:S(2)}) collective-permute-start(bf16[2,8,64,128]{3,2,1,0:T(8,128)(2,1)} %get-tuple-element.51), channel_id=1, source_target_pairs={{0,7},{1,6},{2,5},{3,4},{4,3},{5,2},{6,1},{7,0},{8,15},{9,14},{10,... | collective-permute-start | bytes 786440 | tf_op jit(solution)/shard_map/ppermute | solution.py:420
  91.3 13.8 %collective-permute-done.4.refs_5_ = bf16[2,8,64,128]{3,2,1,0:T(8,128)(2,1)S(1)} collective-permute-done((bf16[2,8,64,128]{3,2,1,0:T(8,128)(2,1)}, bf16[2,8,64,128]{3,2,1,0:T(8,128)(2,1)S(1)}, u32[]{:S(2)}, u32[]{:S(2)}) %collective-permute-start.4) | collective-permute-done | bytes 262176 | tf_op jit(solution)/shard_map/ppermute | solution.py:420
  105.5 2.1 %collective-permute-start.10 = (bf16[2,4,192,128]{3,2,1,0:T(8,128)(2,1)}, bf16[2,4,192,128]{3,2,1,0:T(8,128)(2,1)S(1)}, u32[]{:S(2)}, u32[]{:S(2)}) collective-permute-start(bf16[2,4,192,128]{3,2,1,0:T(8,128)(2,1)} %get-tuple-element.57), channel_id=1, source_target_pairs={{0,4},{1,5},{2,6},{3,7},{4,0},{5,1},{6,2},{7,3},{8,12},{9,13},{10,... | collective-permute-start | bytes 1179656 | tf_op jit(solution)/shard_map/ppermute | solution.py:420
  107.6 2.5 %collective-permute-start.12 = (bf16[2,4,192,128]{3,2,1,0:T(8,128)(2,1)}, bf16[2,4,192,128]{3,2,1,0:T(8,128)(2,1)S(1)}, u32[]{:S(2)}, u32[]{:S(2)}) collective-permute-start(bf16[2,4,192,128]{3,2,1,0:T(8,128)(2,1)} %get-tuple-element.59), channel_id=1, source_target_pairs={{0,6},{1,7},{2,4},{3,5},{4,2},{5,3},{6,0},{7,1},{8,14},{9,15},{10,... | collective-permute-start | bytes 1179656 | tf_op jit(solution)/shard_map/ppermute | solution.py:420
  115.3 7.7 %window_sums.5 = f32[8,1280]{1,0:T(8,128)S(1)} custom-call(s32[1]{0:T(128)} %bitcast.me_ref, bf16[2,8,64,128]{3,2,1,0:T(8,128)(2,1)} %get-tuple-element.44.refs_0_, bf16[2,8,64,128]{3,2,1,0:T(8,128)(2,1)S(1)} %collective-permute-done.refs_1_, bf16[2,8,64,128]{3,2,1,0:T(8,128)(2,1)S(1)} %collective-permute-done.1.refs_2_, ...), custom_call_target="tpu_custom_call" | custom-call | flops 1073741824 | bytes 6291456 | tf_op jit(solution)/shard_map/window_sums/pallas_call | solution.py:362
  123.2 7.6 %window_sums.4 = f32[8,1280]{1,0:T(8,128)S(1)} custom-call(s32[1]{0:T(128)} %bitcast.me_ref, bf16[2,8,64,128]{3,2,1,0:T(8,128)(2,1)} %get-tuple-element.44.refs_0_, bf16[2,8,64,128]{3,2,1,0:T(8,128)(2,1)S(1)} %collective-permute-done.refs_1_, bf16[2,8,64,128]{3,2,1,0:T(8,128)(2,1)S(1)} %collective-permute-done.1.refs_2_, ...), custom_call_target="tpu_custom_call" | custom-call | flops 1073741824 | bytes 6291456 | tf_op jit(solution)/shard_map/window_sums/pallas_call | solution.py:362
  130.9 11.0 %collective-permute-done.11.refs_13_ = bf16[2,4,192,128]{3,2,1,0:T(8,128)(2,1)S(1)} collective-permute-done((bf16[2,4,192,128]{3,2,1,0:T(8,128)(2,1)}, bf16[2,4,192,128]{3,2,1,0:T(8,128)(2,1)S(1)}, u32[]{:S(2)}, u32[]{:S(2)}) %collective-permute-start.11) | collective-permute-done | bytes 393248 | tf_op jit(solution)/shard_map/ppermute | solution.py:420
  142.1 10.3 %window_sums.3 = f32[8,1536]{1,0:T(8,128)S(1)} custom-call(s32[1]{0:T(128)} %bitcast.me_ref, bf16[2,8,64,128]{3,2,1,0:T(8,128)(2,1)} %get-tuple-element.44.refs_0_, bf16[2,8,64,128]{3,2,1,0:T(8,128)(2,1)S(1)} %collective-permute-done.refs_1_, bf16[2,8,64,128]{3,2,1,0:T(8,128)(2,1)S(1)} %collective-permute-done.1.refs_2_, ...), custom_call_target="tpu_custom_call" | custom-call | flops 2147483648 | bytes 6291456 | tf_op jit(solution)/shard_map/window_sums/pallas_call | solution.py:362
  152.5 3.4 %collective-permute-start.31 = (f32[2,4,64]{2,1,0:T(4,128)S(1)}, f32[2,4,64]{2,1,0:T(4,128)S(1)}, u32[]{:S(2)}, u32[]{:S(2)}) collective-permute-start(f32[2,4,64]{2,1,0:T(4,128)S(1)} %rev.14), channel_id=1, source_target_pairs={{0,8},{8,16},{16,24},{1,9},{9,17},{17,25},{2,10},{10,18},{18,26},{... | collective-permute-start | bytes 6152 | tf_op jit(solution)/shard_map/ppermute | solution.py:423
  155.9 1.3 collective-permute-start.30
  157.3 4.1 %collective-permute-done.30 = f32[2,4,64]{2,1,0:T(4,128)S(1)} collective-permute-done((f32[2,4,64]{2,1,0:T(4,128)S(1)}, f32[2,4,64]{2,1,0:T(4,128)S(1)}, u32[]{:S(2)}, u32[]{:S(2)}) %collective-permute-start.30) | collective-permute-done | bytes 2080 | tf_op jit(solution)/shard_map/ppermute | solution.py:426
  (120 shorter events, 24.8 us)
Async XLA Ops:
  24.9 10.2 %collective-permute-start.15 = (s32[2,4,64]{2,1,0:T(4,128)S(1)}, s32[2,4,64]{2,1,0:T(4,128)S(1)}, u32[]{:S(2)}, u32[]{:S(2)}) collective-permute-start(s32[2,4,64]{2,1,0:T(4,128)S(1)} %get-tuple-element.103), channel_id=1, source_target_pairs={{8,0},{16,8},{24,16},{9,1},{17,9},{25,17},{10,2},{18,10},{26,18},{... | collective-permute-start | bytes 6152 | tf_op jit(solution)/shard_map/ppermute | solution.py:426
  26.2 10.8 %collective-permute-start.14 = (s32[2,4,64]{2,1,0:T(4,128)S(1)}, s32[2,4,64]{2,1,0:T(4,128)S(1)}, u32[]{:S(2)}, u32[]{:S(2)}) collective-permute-start(s32[2,4,64]{2,1,0:T(4,128)S(1)} %get-tuple-element.102), channel_id=1, source_target_pairs={{0,8},{8,16},{16,24},{1,9},{9,17},{17,25},{2,10},{10,18},{18,26},{... | collective-permute-start | bytes 6152 | tf_op jit(solution)/shard_map/ppermute | solution.py:423
  31.8 5.3 %collective-permute-start.23 = (bf16[2,2,192,128]{3,2,1,0:T(8,128)(2,1)}, bf16[2,2,192,128]{3,2,1,0:T(8,128)(2,1)S(1)}, u32[]{:S(2)}, u32[]{:S(2)}) collective-permute-start(bf16[2,2,192,128]{3,2,1,0:T(8,128)(2,1)} %get-tuple-element.79), channel_id=1, source_target_pairs={{0,1},{1,0},{2,3},{3,2},{4,5},{5,4},{6,7},{7,6},{8,9},{9,8},{10,11... | collective-permute-start | bytes 589832 | tf_op jit(solution)/shard_map/ppermute | solution.py:420
  31.9 8.0 %collective-permute-start.24 = (bf16[2,2,192,128]{3,2,1,0:T(8,128)(2,1)}, bf16[2,2,192,128]{3,2,1,0:T(8,128)(2,1)S(1)}, u32[]{:S(2)}, u32[]{:S(2)}) collective-permute-start(bf16[2,2,192,128]{3,2,1,0:T(8,128)(2,1)} %get-tuple-element.80), channel_id=1, source_target_pairs={{0,2},{1,3},{2,0},{3,1},{4,6},{5,7},{6,4},{7,5},{8,10},{9,11},{10,... | collective-permute-start | bytes 589832 | tf_op jit(solution)/shard_map/ppermute | solution.py:420
  33.9 9.8 %collective-permute-start.25 = (bf16[2,2,192,128]{3,2,1,0:T(8,128)(2,1)}, bf16[2,2,192,128]{3,2,1,0:T(8,128)(2,1)S(1)}, u32[]{:S(2)}, u32[]{:S(2)}) collective-permute-start(bf16[2,2,192,128]{3,2,1,0:T(8,128)(2,1)} %get-tuple-element.81), channel_id=1, source_target_pairs={{0,3},{1,2},{2,1},{3,0},{4,7},{5,6},{6,5},{7,4},{8,11},{9,10},{10,... | collective-permute-start | bytes 589832 | tf_op jit(solution)/shard_map/ppermute | solution.py:420
  35.1 9.8 %collective-permute-start.26 = (bf16[2,2,192,128]{3,2,1,0:T(8,128)(2,1)}, bf16[2,2,192,128]{3,2,1,0:T(8,128)(2,1)S(1)}, u32[]{:S(2)}, u32[]{:S(2)}) collective-permute-start(bf16[2,2,192,128]{3,2,1,0:T(8,128)(2,1)} %get-tuple-element.82), channel_id=1, source_target_pairs={{0,4},{1,5},{2,6},{3,7},{4,0},{5,1},{6,2},{7,3},{8,12},{9,13},{10,... | collective-permute-start | bytes 589832 | tf_op jit(solution)/shard_map/ppermute | solution.py:420
  37.0 17.7 %collective-permute-start.27 = (bf16[2,2,192,128]{3,2,1,0:T(8,128)(2,1)}, bf16[2,2,192,128]{3,2,1,0:T(8,128)(2,1)S(1)}, u32[]{:S(2)}, u32[]{:S(2)}) collective-permute-start(bf16[2,2,192,128]{3,2,1,0:T(8,128)(2,1)} %get-tuple-element.83), channel_id=1, source_target_pairs={{0,5},{1,4},{2,7},{3,6},{4,1},{5,0},{6,3},{7,2},{8,13},{9,12},{10,... | collective-permute-start | bytes 589832 | tf_op jit(solution)/shard_map/ppermute | solution.py:420
  37.0 20.3 %collective-permute-start.28 = (bf16[2,2,192,128]{3,2,1,0:T(8,128)(2,1)}, bf16[2,2,192,128]{3,2,1,0:T(8,128)(2,1)S(1)}, u32[]{:S(2)}, u32[]{:S(2)}) collective-permute-start(bf16[2,2,192,128]{3,2,1,0:T(8,128)(2,1)} %get-tuple-element.84), channel_id=1, source_target_pairs={{0,6},{1,7},{2,4},{3,5},{4,2},{5,3},{6,0},{7,1},{8,14},{9,15},{10,... | collective-permute-start | bytes 589832 | tf_op jit(solution)/shard_map/ppermute | solution.py:420
  39.9 19.7 %collective-permute-start.29 = (bf16[2,2,192,128]{3,2,1,0:T(8,128)(2,1)}, bf16[2,2,192,128]{3,2,1,0:T(8,128)(2,1)S(1)}, u32[]{:S(2)}, u32[]{:S(2)}) collective-permute-start(bf16[2,2,192,128]{3,2,1,0:T(8,128)(2,1)} %get-tuple-element.85), channel_id=1, source_target_pairs={{0,7},{1,6},{2,5},{3,4},{4,3},{5,2},{6,1},{7,0},{8,15},{9,14},{10,... | collective-permute-start | bytes 589832 | tf_op jit(solution)/shard_map/ppermute | solution.py:420
  44.4 16.5 %collective-permute-start.16 = (bf16[2,2,192,128]{3,2,1,0:T(8,128)(2,1)}, bf16[2,2,192,128]{3,2,1,0:T(8,128)(2,1)S(1)}, u32[]{:S(2)}, u32[]{:S(2)}) collective-permute-start(bf16[2,2,192,128]{3,2,1,0:T(8,128)(2,1)} %get-tuple-element.71), channel_id=1, source_target_pairs={{0,1},{1,0},{2,3},{3,2},{4,5},{5,4},{6,7},{7,6},{8,9},{9,8},{10,11... | collective-permute-start | bytes 589832 | tf_op jit(solution)/shard_map/ppermute | solution.py:420
  45.6 17.7 %collective-permute-start.17 = (bf16[2,2,192,128]{3,2,1,0:T(8,128)(2,1)}, bf16[2,2,192,128]{3,2,1,0:T(8,128)(2,1)S(1)}, u32[]{:S(2)}, u32[]{:S(2)}) collective-permute-start(bf16[2,2,192,128]{3,2,1,0:T(8,128)(2,1)} %get-tuple-element.72), channel_id=1, source_target_pairs={{0,2},{1,3},{2,0},{3,1},{4,6},{5,7},{6,4},{7,5},{8,10},{9,11},{10,... | collective-permute-start | bytes 589832 | tf_op jit(solution)/shard_map/ppermute | solution.py:420
  55.4 9.3 %collective-permute-start.18 = (bf16[2,2,192,128]{3,2,1,0:T(8,128)(2,1)}, bf16[2,2,192,128]{3,2,1,0:T(8,128)(2,1)S(1)}, u32[]{:S(2)}, u32[]{:S(2)}) collective-permute-start(bf16[2,2,192,128]{3,2,1,0:T(8,128)(2,1)} %get-tuple-element.73), channel_id=1, source_target_pairs={{0,3},{1,2},{2,1},{3,0},{4,7},{5,6},{6,5},{7,4},{8,11},{9,10},{10,... | collective-permute-start | bytes 589832 | tf_op jit(solution)/shard_map/ppermute | solution.py:420
  58.0 12.0 %collective-permute-start.19 = (bf16[2,2,192,128]{3,2,1,0:T(8,128)(2,1)}, bf16[2,2,192,128]{3,2,1,0:T(8,128)(2,1)S(1)}, u32[]{:S(2)}, u32[]{:S(2)}) collective-permute-start(bf16[2,2,192,128]{3,2,1,0:T(8,128)(2,1)} %get-tuple-element.74), channel_id=1, source_target_pairs={{0,4},{1,5},{2,6},{3,7},{4,0},{5,1},{6,2},{7,3},{8,12},{9,13},{10,... | collective-permute-start | bytes 589832 | tf_op jit(solution)/shard_map/ppermute | solution.py:420
  60.3 12.2 %collective-permute-start.20 = (bf16[2,2,192,128]{3,2,1,0:T(8,128)(2,1)}, bf16[2,2,192,128]{3,2,1,0:T(8,128)(2,1)S(1)}, u32[]{:S(2)}, u32[]{:S(2)}) collective-permute-start(bf16[2,2,192,128]{3,2,1,0:T(8,128)(2,1)} %get-tuple-element.75), channel_id=1, source_target_pairs={{0,5},{1,4},{2,7},{3,6},{4,1},{5,0},{6,3},{7,2},{8,13},{9,12},{10,... | collective-permute-start | bytes 589832 | tf_op jit(solution)/shard_map/ppermute | solution.py:420
  61.5 13.3 %collective-permute-start.21 = (bf16[2,2,192,128]{3,2,1,0:T(8,128)(2,1)}, bf16[2,2,192,128]{3,2,1,0:T(8,128)(2,1)S(1)}, u32[]{:S(2)}, u32[]{:S(2)}) collective-permute-start(bf16[2,2,192,128]{3,2,1,0:T(8,128)(2,1)} %get-tuple-element.76), channel_id=1, source_target_pairs={{0,6},{1,7},{2,4},{3,5},{4,2},{5,3},{6,0},{7,1},{8,14},{9,15},{10,... | collective-permute-start | bytes 589832 | tf_op jit(solution)/shard_map/ppermute | solution.py:420
  64.0 22.9 %collective-permute-start = (bf16[2,8,64,128]{3,2,1,0:T(8,128)(2,1)}, bf16[2,8,64,128]{3,2,1,0:T(8,128)(2,1)S(1)}, u32[]{:S(2)}, u32[]{:S(2)}) collective-permute-start(bf16[2,8,64,128]{3,2,1,0:T(8,128)(2,1)} %get-tuple-element.45), channel_id=1, source_target_pairs={{0,1},{1,0},{2,3},{3,2},{4,5},{5,4},{6,7},{7,6},{8,9},{9,8},{10,11... | collective-permute-start | bytes 786440 | tf_op jit(solution)/shard_map/ppermute | solution.py:420
  65.4 21.9 %collective-permute-start.1 = (bf16[2,8,64,128]{3,2,1,0:T(8,128)(2,1)}, bf16[2,8,64,128]{3,2,1,0:T(8,128)(2,1)S(1)}, u32[]{:S(2)}, u32[]{:S(2)}) collective-permute-start(bf16[2,8,64,128]{3,2,1,0:T(8,128)(2,1)} %get-tuple-element.46), channel_id=1, source_target_pairs={{0,2},{1,3},{2,0},{3,1},{4,6},{5,7},{6,4},{7,5},{8,10},{9,11},{10,... | collective-permute-start | bytes 786440 | tf_op jit(solution)/shard_map/ppermute | solution.py:420
  70.7 18.9 %collective-permute-start.2 = (bf16[2,8,64,128]{3,2,1,0:T(8,128)(2,1)}, bf16[2,8,64,128]{3,2,1,0:T(8,128)(2,1)S(1)}, u32[]{:S(2)}, u32[]{:S(2)}) collective-permute-start(bf16[2,8,64,128]{3,2,1,0:T(8,128)(2,1)} %get-tuple-element.47), channel_id=1, source_target_pairs={{0,3},{1,2},{2,1},{3,0},{4,7},{5,6},{6,5},{7,4},{8,11},{9,10},{10,... | collective-permute-start | bytes 786440 | tf_op jit(solution)/shard_map/ppermute | solution.py:420
  73.1 16.8 %collective-permute-start.3 = (bf16[2,8,64,128]{3,2,1,0:T(8,128)(2,1)}, bf16[2,8,64,128]{3,2,1,0:T(8,128)(2,1)S(1)}, u32[]{:S(2)}, u32[]{:S(2)}) collective-permute-start(bf16[2,8,64,128]{3,2,1,0:T(8,128)(2,1)} %get-tuple-element.48), channel_id=1, source_target_pairs={{0,4},{1,5},{2,6},{3,7},{4,0},{5,1},{6,2},{7,3},{8,12},{9,13},{10,... | collective-permute-start | bytes 786440 | tf_op jit(solution)/shard_map/ppermute | solution.py:420
  75.5 9.9 %collective-permute-start.22 = (bf16[2,2,192,128]{3,2,1,0:T(8,128)(2,1)}, bf16[2,2,192,128]{3,2,1,0:T(8,128)(2,1)}, u32[]{:S(2)}, u32[]{:S(2)}) collective-permute-start(bf16[2,2,192,128]{3,2,1,0:T(8,128)(2,1)} %get-tuple-element.77), channel_id=1, source_target_pairs={{0,7},{1,6},{2,5},{3,4},{4,3},{5,2},{6,1},{7,0},{8,15},{9,14},{10,... | collective-permute-start | bytes 589832 | tf_op jit(solution)/shard_map/ppermute | solution.py:420
  85.4 19.6 %collective-permute-start.4 = (bf16[2,8,64,128]{3,2,1,0:T(8,128)(2,1)}, bf16[2,8,64,128]{3,2,1,0:T(8,128)(2,1)S(1)}, u32[]{:S(2)}, u32[]{:S(2)}) collective-permute-start(bf16[2,8,64,128]{3,2,1,0:T(8,128)(2,1)} %get-tuple-element.49), channel_id=1, source_target_pairs={{0,5},{1,4},{2,7},{3,6},{4,1},{5,0},{6,3},{7,2},{8,13},{9,12},{10,... | collective-permute-start | bytes 786440 | tf_op jit(solution)/shard_map/ppermute | solution.py:420
  86.9 18.6 %collective-permute-start.5 = (bf16[2,8,64,128]{3,2,1,0:T(8,128)(2,1)}, bf16[2,8,64,128]{3,2,1,0:T(8,128)(2,1)S(1)}, u32[]{:S(2)}, u32[]{:S(2)}) collective-permute-start(bf16[2,8,64,128]{3,2,1,0:T(8,128)(2,1)} %get-tuple-element.50), channel_id=1, source_target_pairs={{0,6},{1,7},{2,4},{3,5},{4,2},{5,3},{6,0},{7,1},{8,14},{9,15},{10,... | collective-permute-start | bytes 786440 | tf_op jit(solution)/shard_map/ppermute | solution.py:420
  87.2 20.3 %collective-permute-start.6 = (bf16[2,8,64,128]{3,2,1,0:T(8,128)(2,1)}, bf16[2,8,64,128]{3,2,1,0:T(8,128)(2,1)S(1)}, u32[]{:S(2)}, u32[]{:S(2)}) collective-permute-start(bf16[2,8,64,128]{3,2,1,0:T(8,128)(2,1)} %get-tuple-element.51), channel_id=1, source_target_pairs={{0,7},{1,6},{2,5},{3,4},{4,3},{5,2},{6,1},{7,0},{8,15},{9,14},{10,... | collective-permute-start | bytes 786440 | tf_op jit(solution)/shard_map/ppermute | solution.py:420
  89.6 17.9 %collective-permute-start.7 = (bf16[2,4,192,128]{3,2,1,0:T(8,128)(2,1)}, bf16[2,4,192,128]{3,2,1,0:T(8,128)(2,1)S(1)}, u32[]{:S(2)}, u32[]{:S(2)}) collective-permute-start(bf16[2,4,192,128]{3,2,1,0:T(8,128)(2,1)} %get-tuple-element.54), channel_id=1, source_target_pairs={{0,1},{1,0},{2,3},{3,2},{4,5},{5,4},{6,7},{7,6},{8,9},{9,8},{10,11... | collective-permute-start | bytes 1179656 | tf_op jit(solution)/shard_map/ppermute | solution.py:420
  89.9 20.2 %collective-permute-start.8 = (bf16[2,4,192,128]{3,2,1,0:T(8,128)(2,1)}, bf16[2,4,192,128]{3,2,1,0:T(8,128)(2,1)S(1)}, u32[]{:S(2)}, u32[]{:S(2)}) collective-permute-start(bf16[2,4,192,128]{3,2,1,0:T(8,128)(2,1)} %get-tuple-element.55), channel_id=1, source_target_pairs={{0,2},{1,3},{2,0},{3,1},{4,6},{5,7},{6,4},{7,5},{8,10},{9,11},{10,... | collective-permute-start | bytes 1179656 | tf_op jit(solution)/shard_map/ppermute | solution.py:420
  105.0 25.9 %collective-permute-start.9 = (bf16[2,4,192,128]{3,2,1,0:T(8,128)(2,1)}, bf16[2,4,192,128]{3,2,1,0:T(8,128)(2,1)S(1)}, u32[]{:S(2)}, u32[]{:S(2)}) collective-permute-start(bf16[2,4,192,128]{3,2,1,0:T(8,128)(2,1)} %get-tuple-element.56), channel_id=1, source_target_pairs={{0,3},{1,2},{2,1},{3,0},{4,7},{5,6},{6,5},{7,4},{8,11},{9,10},{10,... | collective-permute-start | bytes 1179656 | tf_op jit(solution)/shard_map/ppermute | solution.py:420
  105.5 25.4 %collective-permute-start.10 = (bf16[2,4,192,128]{3,2,1,0:T(8,128)(2,1)}, bf16[2,4,192,128]{3,2,1,0:T(8,128)(2,1)S(1)}, u32[]{:S(2)}, u32[]{:S(2)}) collective-permute-start(bf16[2,4,192,128]{3,2,1,0:T(8,128)(2,1)} %get-tuple-element.57), channel_id=1, source_target_pairs={{0,4},{1,5},{2,6},{3,7},{4,0},{5,1},{6,2},{7,3},{8,12},{9,13},{10,... | collective-permute-start | bytes 1179656 | tf_op jit(solution)/shard_map/ppermute | solution.py:420
  107.6 34.4 %collective-permute-start.11 = (bf16[2,4,192,128]{3,2,1,0:T(8,128)(2,1)}, bf16[2,4,192,128]{3,2,1,0:T(8,128)(2,1)S(1)}, u32[]{:S(2)}, u32[]{:S(2)}) collective-permute-start(bf16[2,4,192,128]{3,2,1,0:T(8,128)(2,1)} %get-tuple-element.58), channel_id=1, source_target_pairs={{0,5},{1,4},{2,7},{3,6},{4,1},{5,0},{6,3},{7,2},{8,13},{9,12},{10,... | collective-permute-start | bytes 1179656 | tf_op jit(solution)/shard_map/ppermute | solution.py:420
  107.6 34.4 %collective-permute-start.12 = (bf16[2,4,192,128]{3,2,1,0:T(8,128)(2,1)}, bf16[2,4,192,128]{3,2,1,0:T(8,128)(2,1)S(1)}, u32[]{:S(2)}, u32[]{:S(2)}) collective-permute-start(bf16[2,4,192,128]{3,2,1,0:T(8,128)(2,1)} %get-tuple-element.59), channel_id=1, source_target_pairs={{0,6},{1,7},{2,4},{3,5},{4,2},{5,3},{6,0},{7,1},{8,14},{9,15},{10,... | collective-permute-start | bytes 1179656 | tf_op jit(solution)/shard_map/ppermute | solution.py:420
  110.2 31.8 %collective-permute-start.13 = (bf16[2,4,192,128]{3,2,1,0:T(8,128)(2,1)}, bf16[2,4,192,128]{3,2,1,0:T(8,128)(2,1)S(1)}, u32[]{:S(2)}, u32[]{:S(2)}) collective-permute-start(bf16[2,4,192,128]{3,2,1,0:T(8,128)(2,1)} %get-tuple-element.60), channel_id=1, source_target_pairs={{0,7},{1,6},{2,5},{3,4},{4,3},{5,2},{6,1},{7,0},{8,15},{9,14},{10,... | collective-permute-start | bytes 1179656 | tf_op jit(solution)/shard_map/ppermute | solution.py:420
  152.5 4.8 %collective-permute-start.31 = (f32[2,4,64]{2,1,0:T(4,128)S(1)}, f32[2,4,64]{2,1,0:T(4,128)S(1)}, u32[]{:S(2)}, u32[]{:S(2)}) collective-permute-start(f32[2,4,64]{2,1,0:T(4,128)S(1)} %rev.14), channel_id=1, source_target_pairs={{0,8},{8,16},{16,24},{1,9},{9,17},{17,25},{2,10},{10,18},{18,26},{... | collective-permute-start | bytes 6152 | tf_op jit(solution)/shard_map/ppermute | solution.py:423
  155.9 5.5 %collective-permute-start.30 = (f32[2,4,64]{2,1,0:T(4,128)S(1)}, f32[2,4,64]{2,1,0:T(4,128)S(1)}, u32[]{:S(2)}, u32[]{:S(2)}) collective-permute-start(f32[2,4,64]{2,1,0:T(4,128)S(1)} %get-tuple-element.100), channel_id=1, source_target_pairs={{8,0},{16,8},{24,16},{9,1},{17,9},{25,17},{10,2},{18,10},{26,18},{... | collective-permute-start | bytes 6152 | tf_op jit(solution)/shard_map/ppermute | solution.py:426
  (27 other events, 119.7 us)

commit v3 on v2

--- a/solution.py
+++ b/solution.py
@@ -16,7 +16,7 @@
 BLOCK = 16
 HEAD_STEPS = 4
 STEP_BANDS = 2
-SPLITS = (4, 2, 2)
+SPLITS = (5, 2, 1)
 
 
 def extended(array, sides, width):
@@ -293,12 +293,12 @@
         acc[...] = jnp.zeros_like(acc)
         for slot in range(slots):
 
-            @pl.loop(0, head_rows // BLOCK)
+            @pl.loop(0, head_rows // BLOCK, unroll=2)
             def _(i):
                 row = pl.multiple_of(i * BLOCK, BLOCK)
                 transform(heads, slot, row, row)
 
-            @pl.loop(0, tail_rows // BLOCK)
+            @pl.loop(0, tail_rows // BLOCK, unroll=2)
             def _(i):
                 row = pl.multiple_of(i * BLOCK, BLOCK)
                 transform(tails, slot, row, pl.multiple_of(head_rows + row, BLOCK))
@@ -310,28 +310,25 @@
             [jnp.concatenate([cos, -sin], axis=1), jnp.concatenate([sin, cos], axis=1)], axis=0
         )
         for slot in range(0, slots, 2):
-            spectra = jnp.concatenate([spec[m, slot], spec[m, slot + 1]], axis=1)
+            end = min(slot + 2, slots)
+            spectra = jnp.concatenate([spec[m, i] for i in range(slot, end)], axis=1)
             wave = jnp.dot(table, spectra, preferred_element_type=jnp.float32)
-            lanes = slice(slot * LANES, (slot + 2) * LANES)
+            lanes = slice(slot * LANES, end * LANES)
             power[j, :, lanes] = wave[:depth] * wave[:depth] + wave[depth:] * wave[depth:]
 
     first_row = lax.broadcasted_iota(jnp.int32, (BLOCK, LANES), 0)
     for j in range(together):
 
-        def windowed(i, carry):
-            row = pl.multiple_of(i * BLOCK, BLOCK)
+        for row in range(0, depth, BLOCK):
             rows = (first_row + row).astype(jnp.float32).astype(jnp.bfloat16)
             values = [
-                power[j, pl.ds(row, BLOCK), slot * LANES : (slot + 1) * LANES]
+                power[j, row : row + BLOCK, slot * LANES : (slot + 1) * LANES]
                 for slot in range(slots)
             ]
             for o, value in enumerate(five_wide(five_wide(values))):
                 inside = (rows >= window_ref[j, 0, o]) & (rows < window_ref[j, 1, o])
                 value = jnp.where(inside, value.astype(jnp.bfloat16), jnp.bfloat16(0))
-                kept[j, o, pl.ds(row, BLOCK), :] = value
-            return carry
-
-        lax.fori_loop(0, depth // BLOCK, windowed, 0, unroll=2)
+                kept[j, o, row : row + BLOCK, :] = value
 
     sum_row = lax.broadcasted_iota(jnp.int32, (BLOCK, depth), 0)
     sum_col = lax.broadcasted_iota(jnp.int32, (BLOCK, depth), 1)
@@ -340,8 +337,9 @@
         sums = jnp.where(sum_row == 0, 1, jnp.where(sum_row == 1, count * sum_col, 0))
         sums = jnp.where(sum_row == 2, m, sums).astype(jnp.float32).astype(jnp.bfloat16)
         for o in range(0, width, 2):
-            pair = jnp.concatenate([kept[j, o], kept[j, o + 1]], axis=1)
-            lanes = slice(o * LANES, (o + 2) * LANES)
+            end = min(o + 2, width)
+            pair = jnp.concatenate([kept[j, i] for i in range(o, end)], axis=1)
+            lanes = slice(o * LANES, end * LANES)
             acc[:, lanes] += jnp.dot(sums, pair, preferred_element_type=jnp.float32)[:8]
 
     @pl.when(step == count // together - 1)
@@ -352,9 +350,8 @@
 def window_sums(me, heads, tails, tables, windows, first_slot):
     count = len(heads)
     slots = tails[0].shape[1]
-    chunk = first_slot // slots
     width = 2 * REACH + slots
-    together = 2
+    together = 4
     head_rows, tail_rows = heads[0].shape[2], tails[0].shape[2]
     depth = head_rows + tail_rows
     flops = 2 * count * (2 * depth) * (2 * depth) * (slots * LANES)
@@ -365,7 +362,10 @@
             num_scalar_prefetch=1,
             grid=(count // together,),
             in_specs=[
-                pl.BlockSpec((2, slots, head_rows, LANES), lambda s, me: (0, chunk, 0, 0))
+                pl.BlockSpec(
+                    tuple(pl.Element(n) for n in (2, slots, head_rows, LANES)),
+                    lambda s, me: (0, first_slot, 0, 0),
+                )
                 for _ in range(count)
             ]
             + [
@@ -383,7 +383,7 @@
             ],
         ),
         out_shape=jax.ShapeDtypeStruct((8, width * LANES), jnp.float32),
-        compiler_params=pltpu.CompilerParams(vmem_limit_bytes=(6 + 4 * slots) << 20),
+        compiler_params=pltpu.CompilerParams(vmem_limit_bytes=(12 + 5 * slots) << 20),
         cost_estimate=pl.CostEstimate(flops=flops, bytes_accessed=moved, transcendentals=0),
         name="window_sums",
     )(me, in_place(heads[0]), *heads[1:], in_place(tails[0]), *tails[1:], *tables, windows)
@@ -468,19 +468,20 @@
             edge_right = up(jnp.flip(sums[:, :REACH, mine:], 1))
         slot += size
 
-    def placed(array, before):
-        after = pings - before - array.shape[1]
-        return jnp.pad(array, ((0, 0), (before, after), (0, 0)))
-
-    whole = placed(sums[:, REACH:, :mine], 0)
-    whole = whole + placed(jnp.flip(sums[:, REACH:, mine:], 1), pings - reach)
-    whole = whole + placed(edge_left, pings - REACH) + placed(edge_right, 0)
+    def unfolded(which):
+        def placed(array, before):
+            return jnp.pad(array, ((before, pings - before - array.shape[0]), (0, 0)))
+
+        kept = sums[which, REACH:]
+        whole = placed(kept[:, :mine], 0) + placed(jnp.flip(kept[:, mine:], 0), pings - reach)
+        return whole + placed(edge_left[which], pings - REACH) + placed(edge_right[which], 0)
 
     weight_sum = tap_weights(block * pings, blocks * pings, pings)
     scale = (1.0 / (16.0 * count * depth)) / weight_sum[:, None]
     widths = length.astype(jnp.float32)
-    energy_total = whole[0] * scale
-    moment = (whole[1] - whole[0] * (start.astype(jnp.float32) - 0.5)) * scale
+    total, first_moment = unfolded(0), unfolded(1)
+    energy_total = total * scale
+    moment = (first_moment - total * (start.astype(jnp.float32) - 0.5)) * scale
     return (moment / (widths * (energy_total + 1e-06)), energy_total / widths)
 
 
@@ -500,6 +501,8 @@
         and bins == 8
         and depth % LANES == 0
         and bands * bins % LANES == 0
+        and head_bands * bins % (2 * BLOCK) == 0
+        and (bands - head_bands) * bins % (2 * BLOCK) == 0
         and bands * bins <= 2 * LANES
         and bands > head_bands
         and (bands - head_bands) % (2 * STEP_BANDS) == 0

time: 163 us -> 164 us (level)
  waiting for transfers between devices: 48.3 us -> 57.2 us
  Pallas kernels: 49.8 us -> 44.8 us
  other arithmetic: 7.2 us -> 4.71 us
    ppermute x28, waiting for transfers between devices: 44.2 us -> 53.2 us  [send(): return lax.ppermute(array, 'band', [(i, i ^ r) for i in range(count)])]
    pallas_call x3, Pallas kernels: 25.6 us -> 20.6 us  [window_sums(): pl.pallas_call(functools.partial(turned_kernel, count=count, slots=slots,...]
    unnamed x54 -> x62, local copies, waits for them, and re-layouts: 12.2 us -> 14 us
    ppermute x28, starting transfers between devices: 30.3 us -> 28.6 us  [send(): return lax.ppermute(array, 'band', [(i, i ^ r) for i in range(count)])]
  transfers between devices with their start and end apart: 32 -> 32, of which waited for: 10 -> 10; matrix products, arithmetic and copies ran while one was open for 5% -> 3% of each run, Pallas kernels for 9% -> 6%
where the time goes in v3:
time: 164 us; the launch traced here: 163 us
  waiting for transfers between devices  57.2 us (35%)
  Pallas kernels  44.8 us (27%)
  starting transfers between devices  40.5 us (25%)
  local copies, waits for them, and re-layouts  15.2 us (9%)
  other arithmetic  4.71 us (3%)
    ppermute x28, waiting for transfers between devices, send(): return lax.ppermute(array, 'band', [(i, i ^ r) for i in range(count)])  53.2 us
    ppermute x28, starting transfers between devices, send(): return lax.ppermute(array, 'band', [(i, i ^ r) for i in range(count)])  28.6 us
    pallas_call x2, Pallas kernels, beamform(): pl.pallas_call(functools.partial(beam_kernel, count=count, first_band=fir...  24.2 us
    pallas_call x3, Pallas kernels, window_sums(): pl.pallas_call(functools.partial(turned_kernel, count=count, slots=slots,...  20.6 us
    unnamed x62, local copies, waits for them, and re-layouts  14 us
    ppermute x2, starting transfers between devices, up(): return lax.ppermute(array, 'ping', [(i, i + 1) for i in range(blocks - 1)])  9.24 us
    ppermute x2, waiting for transfers between devices, down(): return lax.ppermute(array, 'ping', [(i + 1, i) for i in range(blocks - 1)])  4.05 us
  transfers between devices with their start and end apart: 32, of which 10 were waited for; matrix products, arithmetic and copies ran while one was open for 3% of the time, Pallas kernels for 6%

profile of v3, /device:TPU:0, one launch (start us, length us, event | category | flops | bytes accessed | tf_op | source)
XLA Modules:
  0.0 163.5 jit_solution(6443051997612579886)
XLA Ops:
  0.6 7.6 %beamform.2 = (bf16[2,8,64,128]{3,2,1,0:T(8,128)(2,1)}, bf16[2,8,64,128]{3,2,1,0:T(8,128)(2,1)}, bf16[2,8,64,128]{3,2,1,0:T(8,128)(2,1)}, bf16[2,8,64,128]{3,2,1...) custom-call(s32[1]{0:T(128)} %bitcast.me_ref, ...), custom_call_target="tpu_custom_call" | custom-call | flops 2147483648 | bytes 12582912 | tf_op jit(solution)/shard_map/beamform/pallas_call | solution.py:194
  8.3 16.6 %beamform.3 = (bf16[2,5,192,128]{3,2,1,0:T(8,128)(2,1)}, bf16[2,5,192,128]{3,2,1,0:T(8,128)(2,1)}, bf16[2,5,192,128]{3,2,1,0:T(8,128)(2,1)}, bf16[2,5,192,128]{3...) custom-call(s32[1]{0:T(128)} %bitcast.me_ref, ...), custom_call_target="tpu_custom_call" | custom-call | flops 6442450944 | bytes 37748736 | tf_op jit(solution)/shard_map/beamform/pallas_call | solution.py:194
  24.9 1.3 collective-permute-start.15
  26.2 5.8 %collective-permute-start.14 = (s32[2,4,64]{2,1,0:T(4,128)S(1)}, s32[2,4,64]{2,1,0:T(4,128)S(1)}, u32[]{:S(2)}, u32[]{:S(2)}) collective-permute-start(s32[2,4,64]{2,1,0:T(4,128)S(1)} %get-tuple-element.100), channel_id=1, source_target_pairs={{0,8},{8,16},{16,24},{1,9},{9,17},{17,25},{2,10},{10,18},{18,26},{... | collective-permute-start | bytes 6152 | tf_op jit(solution)/shard_map/ppermute | solution.py:423
  32.1 2.0 %collective-permute-start.24 = (bf16[2,1,192,128]{3,2,1,0:T(8,128)(2,1)}, bf16[2,1,192,128]{3,2,1,0:T(8,128)(2,1)S(1)}, u32[]{:S(2)}, u32[]{:S(2)}) collective-permute-start(bf16[2,1,192,128]{3,2,1,0:T(8,128)(2,1)} %get-tuple-element.80), channel_id=1, source_target_pairs={{0,2},{1,3},{2,0},{3,1},{4,6},{5,7},{6,4},{7,5},{8,10},{9,11},{10,... | collective-permute-start | bytes 294920 | tf_op jit(solution)/shard_map/ppermute | solution.py:420
  34.1 1.8 %collective-permute-start.26 = (bf16[2,1,192,128]{3,2,1,0:T(8,128)(2,1)}, bf16[2,1,192,128]{3,2,1,0:T(8,128)(2,1)S(1)}, u32[]{:S(2)}, u32[]{:S(2)}) collective-permute-start(bf16[2,1,192,128]{3,2,1,0:T(8,128)(2,1)} %get-tuple-element.82), channel_id=1, source_target_pairs={{0,4},{1,5},{2,6},{3,7},{4,0},{5,1},{6,2},{7,3},{8,12},{9,13},{10,... | collective-permute-start | bytes 294920 | tf_op jit(solution)/shard_map/ppermute | solution.py:420
  36.0 1.1 fusion.5
  37.1 2.7 %collective-permute-start.28 = (bf16[2,1,192,128]{3,2,1,0:T(8,128)(2,1)}, bf16[2,1,192,128]{3,2,1,0:T(8,128)(2,1)S(1)}, u32[]{:S(2)}, u32[]{:S(2)}) collective-permute-start(bf16[2,1,192,128]{3,2,1,0:T(8,128)(2,1)} %get-tuple-element.84), channel_id=1, source_target_pairs={{0,6},{1,7},{2,4},{3,5},{4,2},{5,3},{6,0},{7,1},{8,14},{9,15},{10,... | collective-permute-start | bytes 294920 | tf_op jit(solution)/shard_map/ppermute | solution.py:420
  41.1 1.3 collective-permute-start.16
  43.7 1.5 collective-permute-done.27.refs_13_
  45.8 1.7 %collective-permute-start.18 = (bf16[2,2,192,128]{3,2,1,0:T(8,128)(2,1)}, bf16[2,2,192,128]{3,2,1,0:T(8,128)(2,1)S(1)}, u32[]{:S(2)}, u32[]{:S(2)}) collective-permute-start(bf16[2,2,192,128]{3,2,1,0:T(8,128)(2,1)} %get-tuple-element.73), channel_id=1, source_target_pairs={{0,3},{1,2},{2,1},{3,0},{4,7},{5,6},{6,5},{7,4},{8,11},{9,10},{10,... | collective-permute-start | bytes 589832 | tf_op jit(solution)/shard_map/ppermute | solution.py:420
  48.9 1.5 collective-permute-start.19
  52.1 1.5 collective-permute-start.21
  54.3 2.2 %collective-permute-start.22 = (bf16[2,2,192,128]{3,2,1,0:T(8,128)(2,1)}, bf16[2,2,192,128]{3,2,1,0:T(8,128)(2,1)S(1)}, u32[]{:S(2)}, u32[]{:S(2)}) collective-permute-start(bf16[2,2,192,128]{3,2,1,0:T(8,128)(2,1)} %get-tuple-element.77), channel_id=1, source_target_pairs={{0,7},{1,6},{2,5},{3,4},{4,3},{5,2},{6,1},{7,0},{8,15},{9,14},{10,... | collective-permute-start | bytes 589832 | tf_op jit(solution)/shard_map/ppermute | solution.py:420
  57.1 8.1 %collective-permute-done.19.refs_12_ = bf16[2,2,192,128]{3,2,1,0:T(8,128)(2,1)S(1)} collective-permute-done((bf16[2,2,192,128]{3,2,1,0:T(8,128)(2,1)}, bf16[2,2,192,128]{3,2,1,0:T(8,128)(2,1)S(1)}, u32[]{:S(2)}, u32[]{:S(2)}) %collective-permute-start.19) | collective-permute-done | bytes 196640 | tf_op jit(solution)/shard_map/ppermute | solution.py:420
  66.4 2.2 %collective-permute-done.20.refs_13_ = bf16[2,2,192,128]{3,2,1,0:T(8,128)(2,1)S(1)} collective-permute-done((bf16[2,2,192,128]{3,2,1,0:T(8,128)(2,1)}, bf16[2,2,192,128]{3,2,1,0:T(8,128)(2,1)S(1)}, u32[]{:S(2)}, u32[]{:S(2)}) %collective-permute-start.20) | collective-permute-done | bytes 196640 | tf_op jit(solution)/shard_map/ppermute | solution.py:420
  70.2 1.7 %collective-permute-start.3 = (bf16[2,8,64,128]{3,2,1,0:T(8,128)(2,1)}, bf16[2,8,64,128]{3,2,1,0:T(8,128)(2,1)S(1)}, u32[]{:S(2)}, u32[]{:S(2)}) collective-permute-start(bf16[2,8,64,128]{3,2,1,0:T(8,128)(2,1)} %get-tuple-element.48), channel_id=1, source_target_pairs={{0,4},{1,5},{2,6},{3,7},{4,0},{5,1},{6,2},{7,3},{8,12},{9,13},{10,... | collective-permute-start | bytes 786440 | tf_op jit(solution)/shard_map/ppermute | solution.py:420
  72.6 1.5 collective-permute-start.8
  75.1 2.8 %collective-permute-done.2.refs_3_ = bf16[2,8,64,128]{3,2,1,0:T(8,128)(2,1)S(1)} collective-permute-done((bf16[2,8,64,128]{3,2,1,0:T(8,128)(2,1)}, bf16[2,8,64,128]{3,2,1,0:T(8,128)(2,1)S(1)}, u32[]{:S(2)}, u32[]{:S(2)}) %collective-permute-start.2) | collective-permute-done | bytes 262176 | tf_op jit(solution)/shard_map/ppermute | solution.py:420
  77.8 1.5 collective-permute-start.5
  79.6 1.3 collective-permute-start.6
  83.8 2.1 %collective-permute-start.9 = (bf16[2,5,192,128]{3,2,1,0:T(8,128)(2,1)}, bf16[2,5,192,128]{3,2,1,0:T(8,128)(2,1)S(1)}, u32[]{:S(2)}, u32[]{:S(2)}) collective-permute-start(bf16[2,5,192,128]{3,2,1,0:T(8,128)(2,1)} %get-tuple-element.56), channel_id=1, source_target_pairs={{0,3},{1,2},{2,1},{3,0},{4,7},{5,6},{6,5},{7,4},{8,11},{9,10},{10,... | collective-permute-start | bytes 1474568 | tf_op jit(solution)/shard_map/ppermute | solution.py:420
  85.9 9.8 %collective-permute-done.5.refs_6_ = bf16[2,8,64,128]{3,2,1,0:T(8,128)(2,1)} collective-permute-done((bf16[2,8,64,128]{3,2,1,0:T(8,128)(2,1)}, bf16[2,8,64,128]{3,2,1,0:T(8,128)(2,1)}, u32[]{:S(2)}, u32[]{:S(2)}) %collective-permute-start.5) | collective-permute-done | bytes 262176 | tf_op jit(solution)/shard_map/ppermute | solution.py:420
  96.2 4.5 %collective-permute-done.6.refs_7_ = bf16[2,8,64,128]{3,2,1,0:T(8,128)(2,1)} collective-permute-done((bf16[2,8,64,128]{3,2,1,0:T(8,128)(2,1)}, bf16[2,8,64,128]{3,2,1,0:T(8,128)(2,1)}, u32[]{:S(2)}, u32[]{:S(2)}) %collective-permute-start.6) | collective-permute-done | bytes 262176 | tf_op jit(solution)/shard_map/ppermute | solution.py:420
  101.3 1.5 collective-permute-start.12
  109.3 4.9 %window_sums.5 = f32[8,1152]{1,0:T(8,128)S(1)} custom-call(s32[1]{0:T(128)} %bitcast.me_ref, bf16[2,8,64,128]{3,2,1,0:T(8,128)(2,1)} %get-tuple-element.44.refs_0_, bf16[2,8,64,128]{3,2,1,0:T(8,128)(2,1)S(1)} %collective-permute-done.refs_1_, bf16[2,8,64,128]{3,2,1,0:T(8,128)(2,1)S(1)} %collective-permute-done.1.refs_2_, ...), custom_call_target="tpu_custom_call" | custom-call | flops 536870912 | bytes 6291456 | tf_op jit(solution)/shard_map/window_sums/pallas_call | solution.py:359
  114.3 5.2 %window_sums.4 = f32[8,1280]{1,0:T(8,128)S(1)} custom-call(s32[1]{0:T(128)} %bitcast.me_ref, bf16[2,8,64,128]{3,2,1,0:T(8,128)(2,1)} %get-tuple-element.44.refs_0_, bf16[2,8,64,128]{3,2,1,0:T(8,128)(2,1)S(1)} %collective-permute-done.refs_1_, bf16[2,8,64,128]{3,2,1,0:T(8,128)(2,1)S(1)} %collective-permute-done.1.refs_2_, ...), custom_call_target="tpu_custom_call" | custom-call | flops 1073741824 | bytes 6291456 | tf_op jit(solution)/shard_map/window_sums/pallas_call | solution.py:359
  119.7 23.3 %collective-permute-done.11.refs_13_ = bf16[2,5,192,128]{3,2,1,0:T(8,128)(2,1)S(1)} collective-permute-done((bf16[2,5,192,128]{3,2,1,0:T(8,128)(2,1)}, bf16[2,5,192,128]{3,2,1,0:T(8,128)(2,1)S(1)}, u32[]{:S(2)}, u32[]{:S(2)}) %collective-permute-start.11) | collective-permute-done | bytes 491552 | tf_op jit(solution)/shard_map/ppermute | solution.py:420
  143.1 10.5 %window_sums.3 = f32[8,1664]{1,0:T(8,128)S(1)} custom-call(s32[1]{0:T(128)} %bitcast.me_ref, bf16[2,8,64,128]{3,2,1,0:T(8,128)(2,1)} %get-tuple-element.44.refs_0_, bf16[2,8,64,128]{3,2,1,0:T(8,128)(2,1)S(1)} %collective-permute-done.refs_1_, bf16[2,8,64,128]{3,2,1,0:T(8,128)(2,1)S(1)} %collective-permute-done.1.refs_2_, ...), custom_call_target="tpu_custom_call" | custom-call | flops 2684354560 | bytes 6291456 | tf_op jit(solution)/shard_map/window_sums/pallas_call | solution.py:359
  153.8 3.5 %collective-permute-start.31 = (f32[2,4,64]{2,1,0:T(4,128)S(1)}, f32[2,4,64]{2,1,0:T(4,128)S(1)}, u32[]{:S(2)}, u32[]{:S(2)}) collective-permute-start(f32[2,4,64]{2,1,0:T(4,128)S(1)} %rev.17), channel_id=1, source_target_pairs={{0,8},{8,16},{16,24},{1,9},{9,17},{17,25},{2,10},{10,18},{18,26},{... | collective-permute-start | bytes 6152 | tf_op jit(solution)/shard_map/ppermute | solution.py:423
  157.3 1.3 collective-permute-start.30
  158.7 4.0 %collective-permute-done.30 = f32[2,4,64]{2,1,0:T(4,128)S(1)} collective-permute-done((f32[2,4,64]{2,1,0:T(4,128)S(1)}, f32[2,4,64]{2,1,0:T(4,128)S(1)}, u32[]{:S(2)}, u32[]{:S(2)}) %collective-permute-start.30) | collective-permute-done | bytes 2080 | tf_op jit(solution)/shard_map/ppermute | solution.py:426
  (132 shorter events, 24.0 us)
Async XLA Ops:
  24.9 9.2 %collective-permute-start.15 = (s32[2,4,64]{2,1,0:T(4,128)S(1)}, s32[2,4,64]{2,1,0:T(4,128)S(1)}, u32[]{:S(2)}, u32[]{:S(2)}) collective-permute-start(s32[2,4,64]{2,1,0:T(4,128)S(1)} %get-tuple-element.101), channel_id=1, source_target_pairs={{8,0},{16,8},{24,16},{9,1},{17,9},{25,17},{10,2},{18,10},{26,18},{... | collective-permute-start | bytes 6152 | tf_op jit(solution)/shard_map/ppermute | solution.py:426
  26.2 9.7 %collective-permute-start.14 = (s32[2,4,64]{2,1,0:T(4,128)S(1)}, s32[2,4,64]{2,1,0:T(4,128)S(1)}, u32[]{:S(2)}, u32[]{:S(2)}) collective-permute-start(s32[2,4,64]{2,1,0:T(4,128)S(1)} %get-tuple-element.100), channel_id=1, source_target_pairs={{0,8},{8,16},{16,24},{1,9},{9,17},{17,25},{2,10},{10,18},{18,26},{... | collective-permute-start | bytes 6152 | tf_op jit(solution)/shard_map/ppermute | solution.py:423
  32.0 5.1 %collective-permute-start.23 = (bf16[2,1,192,128]{3,2,1,0:T(8,128)(2,1)}, bf16[2,1,192,128]{3,2,1,0:T(8,128)(2,1)S(1)}, u32[]{:S(2)}, u32[]{:S(2)}) collective-permute-start(bf16[2,1,192,128]{3,2,1,0:T(8,128)(2,1)} %get-tuple-element.79), channel_id=1, source_target_pairs={{0,1},{1,0},{2,3},{3,2},{4,5},{5,4},{6,7},{7,6},{8,9},{9,8},{10,11... | collective-permute-start | bytes 294920 | tf_op jit(solution)/shard_map/ppermute | solution.py:420
  32.1 7.7 %collective-permute-start.24 = (bf16[2,1,192,128]{3,2,1,0:T(8,128)(2,1)}, bf16[2,1,192,128]{3,2,1,0:T(8,128)(2,1)S(1)}, u32[]{:S(2)}, u32[]{:S(2)}) collective-permute-start(bf16[2,1,192,128]{3,2,1,0:T(8,128)(2,1)} %get-tuple-element.80), channel_id=1, source_target_pairs={{0,2},{1,3},{2,0},{3,1},{4,6},{5,7},{6,4},{7,5},{8,10},{9,11},{10,... | collective-permute-start | bytes 294920 | tf_op jit(solution)/shard_map/ppermute | solution.py:420
  34.1 6.4 %collective-permute-start.25 = (bf16[2,1,192,128]{3,2,1,0:T(8,128)(2,1)}, bf16[2,1,192,128]{3,2,1,0:T(8,128)(2,1)S(1)}, u32[]{:S(2)}, u32[]{:S(2)}) collective-permute-start(bf16[2,1,192,128]{3,2,1,0:T(8,128)(2,1)} %get-tuple-element.81), channel_id=1, source_target_pairs={{0,3},{1,2},{2,1},{3,0},{4,7},{5,6},{6,5},{7,4},{8,11},{9,10},{10,... | collective-permute-start | bytes 294920 | tf_op jit(solution)/shard_map/ppermute | solution.py:420
  34.1 8.3 %collective-permute-start.26 = (bf16[2,1,192,128]{3,2,1,0:T(8,128)(2,1)}, bf16[2,1,192,128]{3,2,1,0:T(8,128)(2,1)S(1)}, u32[]{:S(2)}, u32[]{:S(2)}) collective-permute-start(bf16[2,1,192,128]{3,2,1,0:T(8,128)(2,1)} %get-tuple-element.82), channel_id=1, source_target_pairs={{0,4},{1,5},{2,6},{3,7},{4,0},{5,1},{6,2},{7,3},{8,12},{9,13},{10,... | collective-permute-start | bytes 294920 | tf_op jit(solution)/shard_map/ppermute | solution.py:420
  35.9 9.2 %collective-permute-start.27 = (bf16[2,1,192,128]{3,2,1,0:T(8,128)(2,1)}, bf16[2,1,192,128]{3,2,1,0:T(8,128)(2,1)S(1)}, u32[]{:S(2)}, u32[]{:S(2)}) collective-permute-start(bf16[2,1,192,128]{3,2,1,0:T(8,128)(2,1)} %get-tuple-element.83), channel_id=1, source_target_pairs={{0,5},{1,4},{2,7},{3,6},{4,1},{5,0},{6,3},{7,2},{8,13},{9,12},{10,... | collective-permute-start | bytes 294920 | tf_op jit(solution)/shard_map/ppermute | solution.py:420
  37.1 10.5 %collective-permute-start.28 = (bf16[2,1,192,128]{3,2,1,0:T(8,128)(2,1)}, bf16[2,1,192,128]{3,2,1,0:T(8,128)(2,1)S(1)}, u32[]{:S(2)}, u32[]{:S(2)}) collective-permute-start(bf16[2,1,192,128]{3,2,1,0:T(8,128)(2,1)} %get-tuple-element.84), channel_id=1, source_target_pairs={{0,6},{1,7},{2,4},{3,5},{4,2},{5,3},{6,0},{7,1},{8,14},{9,15},{10,... | collective-permute-start | bytes 294920 | tf_op jit(solution)/shard_map/ppermute | solution.py:420
  40.4 7.8 %collective-permute-start.29 = (bf16[2,1,192,128]{3,2,1,0:T(8,128)(2,1)}, bf16[2,1,192,128]{3,2,1,0:T(8,128)(2,1)S(1)}, u32[]{:S(2)}, u32[]{:S(2)}) collective-permute-start(bf16[2,1,192,128]{3,2,1,0:T(8,128)(2,1)} %get-tuple-element.85), channel_id=1, source_target_pairs={{0,7},{1,6},{2,5},{3,4},{4,3},{5,2},{6,1},{7,0},{8,15},{9,14},{10,... | collective-permute-start | bytes 294920 | tf_op jit(solution)/shard_map/ppermute | solution.py:420
  41.1 9.3 %collective-permute-start.16 = (bf16[2,2,192,128]{3,2,1,0:T(8,128)(2,1)}, bf16[2,2,192,128]{3,2,1,0:T(8,128)(2,1)S(1)}, u32[]{:S(2)}, u32[]{:S(2)}) collective-permute-start(bf16[2,2,192,128]{3,2,1,0:T(8,128)(2,1)} %get-tuple-element.71), channel_id=1, source_target_pairs={{0,1},{1,0},{2,3},{3,2},{4,5},{5,4},{6,7},{7,6},{8,9},{9,8},{10,11... | collective-permute-start | bytes 589832 | tf_op jit(solution)/shard_map/ppermute | solution.py:420
  43.0 8.4 %collective-permute-start.17 = (bf16[2,2,192,128]{3,2,1,0:T(8,128)(2,1)}, bf16[2,2,192,128]{3,2,1,0:T(8,128)(2,1)S(1)}, u32[]{:S(2)}, u32[]{:S(2)}) collective-permute-start(bf16[2,2,192,128]{3,2,1,0:T(8,128)(2,1)} %get-tuple-element.72), channel_id=1, source_target_pairs={{0,2},{1,3},{2,0},{3,1},{4,6},{5,7},{6,4},{7,5},{8,10},{9,11},{10,... | collective-permute-start | bytes 589832 | tf_op jit(solution)/shard_map/ppermute | solution.py:420
  45.8 7.8 %collective-permute-start.18 = (bf16[2,2,192,128]{3,2,1,0:T(8,128)(2,1)}, bf16[2,2,192,128]{3,2,1,0:T(8,128)(2,1)S(1)}, u32[]{:S(2)}, u32[]{:S(2)}) collective-permute-start(bf16[2,2,192,128]{3,2,1,0:T(8,128)(2,1)} %get-tuple-element.73), channel_id=1, source_target_pairs={{0,3},{1,2},{2,1},{3,0},{4,7},{5,6},{6,5},{7,4},{8,11},{9,10},{10,... | collective-permute-start | bytes 589832 | tf_op jit(solution)/shard_map/ppermute | solution.py:420
  48.2 24.4 %collective-permute-start = (bf16[2,8,64,128]{3,2,1,0:T(8,128)(2,1)}, bf16[2,8,64,128]{3,2,1,0:T(8,128)(2,1)S(1)}, u32[]{:S(2)}, u32[]{:S(2)}) collective-permute-start(bf16[2,8,64,128]{3,2,1,0:T(8,128)(2,1)} %get-tuple-element.45), channel_id=1, source_target_pairs={{0,1},{1,0},{2,3},{3,2},{4,5},{5,4},{6,7},{7,6},{8,9},{9,8},{10,11... | collective-permute-start | bytes 786440 | tf_op jit(solution)/shard_map/ppermute | solution.py:420
  48.9 16.4 %collective-permute-start.19 = (bf16[2,2,192,128]{3,2,1,0:T(8,128)(2,1)}, bf16[2,2,192,128]{3,2,1,0:T(8,128)(2,1)S(1)}, u32[]{:S(2)}, u32[]{:S(2)}) collective-permute-start(bf16[2,2,192,128]{3,2,1,0:T(8,128)(2,1)} %get-tuple-element.74), channel_id=1, source_target_pairs={{0,4},{1,5},{2,6},{3,7},{4,0},{5,1},{6,2},{7,3},{8,12},{9,13},{10,... | collective-permute-start | bytes 589832 | tf_op jit(solution)/shard_map/ppermute | solution.py:420
  51.1 17.5 %collective-permute-start.20 = (bf16[2,2,192,128]{3,2,1,0:T(8,128)(2,1)}, bf16[2,2,192,128]{3,2,1,0:T(8,128)(2,1)S(1)}, u32[]{:S(2)}, u32[]{:S(2)}) collective-permute-start(bf16[2,2,192,128]{3,2,1,0:T(8,128)(2,1)} %get-tuple-element.75), channel_id=1, source_target_pairs={{0,5},{1,4},{2,7},{3,6},{4,1},{5,0},{6,3},{7,2},{8,13},{9,12},{10,... | collective-permute-start | bytes 589832 | tf_op jit(solution)/shard_map/ppermute | solution.py:420
  52.1 17.4 %collective-permute-start.21 = (bf16[2,2,192,128]{3,2,1,0:T(8,128)(2,1)}, bf16[2,2,192,128]{3,2,1,0:T(8,128)(2,1)S(1)}, u32[]{:S(2)}, u32[]{:S(2)}) collective-permute-start(bf16[2,2,192,128]{3,2,1,0:T(8,128)(2,1)} %get-tuple-element.76), channel_id=1, source_target_pairs={{0,6},{1,7},{2,4},{3,5},{4,2},{5,3},{6,0},{7,1},{8,14},{9,15},{10,... | collective-permute-start | bytes 589832 | tf_op jit(solution)/shard_map/ppermute | solution.py:420
  54.3 17.6 %collective-permute-start.22 = (bf16[2,2,192,128]{3,2,1,0:T(8,128)(2,1)}, bf16[2,2,192,128]{3,2,1,0:T(8,128)(2,1)S(1)}, u32[]{:S(2)}, u32[]{:S(2)}) collective-permute-start(bf16[2,2,192,128]{3,2,1,0:T(8,128)(2,1)} %get-tuple-element.77), channel_id=1, source_target_pairs={{0,7},{1,6},{2,5},{3,4},{4,3},{5,2},{6,1},{7,0},{8,15},{9,14},{10,... | collective-permute-start | bytes 589832 | tf_op jit(solution)/shard_map/ppermute | solution.py:420
  66.0 8.7 %collective-permute-start.1 = (bf16[2,8,64,128]{3,2,1,0:T(8,128)(2,1)}, bf16[2,8,64,128]{3,2,1,0:T(8,128)(2,1)S(1)}, u32[]{:S(2)}, u32[]{:S(2)}) collective-permute-start(bf16[2,8,64,128]{3,2,1,0:T(8,128)(2,1)} %get-tuple-element.46), channel_id=1, source_target_pairs={{0,2},{1,3},{2,0},{3,1},{4,6},{5,7},{6,4},{7,5},{8,10},{9,11},{10,... | collective-permute-start | bytes 786440 | tf_op jit(solution)/shard_map/ppermute | solution.py:420
  69.2 8.6 %collective-permute-start.2 = (bf16[2,8,64,128]{3,2,1,0:T(8,128)(2,1)}, bf16[2,8,64,128]{3,2,1,0:T(8,128)(2,1)S(1)}, u32[]{:S(2)}, u32[]{:S(2)}) collective-permute-start(bf16[2,8,64,128]{3,2,1,0:T(8,128)(2,1)} %get-tuple-element.47), channel_id=1, source_target_pairs={{0,3},{1,2},{2,1},{3,0},{4,7},{5,6},{6,5},{7,4},{8,11},{9,10},{10,... | collective-permute-start | bytes 786440 | tf_op jit(solution)/shard_map/ppermute | solution.py:420
  70.2 9.4 %collective-permute-start.3 = (bf16[2,8,64,128]{3,2,1,0:T(8,128)(2,1)}, bf16[2,8,64,128]{3,2,1,0:T(8,128)(2,1)S(1)}, u32[]{:S(2)}, u32[]{:S(2)}) collective-permute-start(bf16[2,8,64,128]{3,2,1,0:T(8,128)(2,1)} %get-tuple-element.48), channel_id=1, source_target_pairs={{0,4},{1,5},{2,6},{3,7},{4,0},{5,1},{6,2},{7,3},{8,12},{9,13},{10,... | collective-permute-start | bytes 786440 | tf_op jit(solution)/shard_map/ppermute | solution.py:420
  72.6 28.7 %collective-permute-start.7 = (bf16[2,5,192,128]{3,2,1,0:T(8,128)(2,1)}, bf16[2,5,192,128]{3,2,1,0:T(8,128)(2,1)}, u32[]{:S(2)}, u32[]{:S(2)}) collective-permute-start(bf16[2,5,192,128]{3,2,1,0:T(8,128)(2,1)} %get-tuple-element.54), channel_id=1, source_target_pairs={{0,1},{1,0},{2,3},{3,2},{4,5},{5,4},{6,7},{7,6},{8,9},{9,8},{10,11... | collective-permute-start | bytes 1474568 | tf_op jit(solution)/shard_map/ppermute | solution.py:420
  72.6 30.3 %collective-permute-start.8 = (bf16[2,5,192,128]{3,2,1,0:T(8,128)(2,1)}, bf16[2,5,192,128]{3,2,1,0:T(8,128)(2,1)}, u32[]{:S(2)}, u32[]{:S(2)}) collective-permute-start(bf16[2,5,192,128]{3,2,1,0:T(8,128)(2,1)} %get-tuple-element.55), channel_id=1, source_target_pairs={{0,2},{1,3},{2,0},{3,1},{4,6},{5,7},{6,4},{7,5},{8,10},{9,11},{10,... | collective-permute-start | bytes 1474568 | tf_op jit(solution)/shard_map/ppermute | solution.py:420
  74.7 9.1 %collective-permute-start.4 = (bf16[2,8,64,128]{3,2,1,0:T(8,128)(2,1)}, bf16[2,8,64,128]{3,2,1,0:T(8,128)(2,1)S(1)}, u32[]{:S(2)}, u32[]{:S(2)}) collective-permute-start(bf16[2,8,64,128]{3,2,1,0:T(8,128)(2,1)} %get-tuple-element.49), channel_id=1, source_target_pairs={{0,5},{1,4},{2,7},{3,6},{4,1},{5,0},{6,3},{7,2},{8,13},{9,12},{10,... | collective-permute-start | bytes 786440 | tf_op jit(solution)/shard_map/ppermute | solution.py:420
  77.8 17.9 %collective-permute-start.5 = (bf16[2,8,64,128]{3,2,1,0:T(8,128)(2,1)}, bf16[2,8,64,128]{3,2,1,0:T(8,128)(2,1)}, u32[]{:S(2)}, u32[]{:S(2)}) collective-permute-start(bf16[2,8,64,128]{3,2,1,0:T(8,128)(2,1)} %get-tuple-element.50), channel_id=1, source_target_pairs={{0,6},{1,7},{2,4},{3,5},{4,2},{5,3},{6,0},{7,1},{8,14},{9,15},{10,... | collective-permute-start | bytes 786440 | tf_op jit(solution)/shard_map/ppermute | solution.py:420
  79.6 21.2 %collective-permute-start.6 = (bf16[2,8,64,128]{3,2,1,0:T(8,128)(2,1)}, bf16[2,8,64,128]{3,2,1,0:T(8,128)(2,1)}, u32[]{:S(2)}, u32[]{:S(2)}) collective-permute-start(bf16[2,8,64,128]{3,2,1,0:T(8,128)(2,1)} %get-tuple-element.51), channel_id=1, source_target_pairs={{0,7},{1,6},{2,5},{3,4},{4,3},{5,2},{6,1},{7,0},{8,15},{9,14},{10,... | collective-permute-start | bytes 786440 | tf_op jit(solution)/shard_map/ppermute | solution.py:420
  83.8 35.9 %collective-permute-start.9 = (bf16[2,5,192,128]{3,2,1,0:T(8,128)(2,1)}, bf16[2,5,192,128]{3,2,1,0:T(8,128)(2,1)S(1)}, u32[]{:S(2)}, u32[]{:S(2)}) collective-permute-start(bf16[2,5,192,128]{3,2,1,0:T(8,128)(2,1)} %get-tuple-element.56), channel_id=1, source_target_pairs={{0,3},{1,2},{2,1},{3,0},{4,7},{5,6},{6,5},{7,4},{8,11},{9,10},{10,... | collective-permute-start | bytes 1474568 | tf_op jit(solution)/shard_map/ppermute | solution.py:420
  95.7 23.9 %collective-permute-start.10 = (bf16[2,5,192,128]{3,2,1,0:T(8,128)(2,1)}, bf16[2,5,192,128]{3,2,1,0:T(8,128)(2,1)S(1)}, u32[]{:S(2)}, u32[]{:S(2)}) collective-permute-start(bf16[2,5,192,128]{3,2,1,0:T(8,128)(2,1)} %get-tuple-element.57), channel_id=1, source_target_pairs={{0,4},{1,5},{2,6},{3,7},{4,0},{5,1},{6,2},{7,3},{8,12},{9,13},{10,... | collective-permute-start | bytes 1474568 | tf_op jit(solution)/shard_map/ppermute | solution.py:420
  100.8 42.2 %collective-permute-start.11 = (bf16[2,5,192,128]{3,2,1,0:T(8,128)(2,1)}, bf16[2,5,192,128]{3,2,1,0:T(8,128)(2,1)S(1)}, u32[]{:S(2)}, u32[]{:S(2)}) collective-permute-start(bf16[2,5,192,128]{3,2,1,0:T(8,128)(2,1)} %get-tuple-element.58), channel_id=1, source_target_pairs={{0,5},{1,4},{2,7},{3,6},{4,1},{5,0},{6,3},{7,2},{8,13},{9,12},{10,... | collective-permute-start | bytes 1474568 | tf_op jit(solution)/shard_map/ppermute | solution.py:420
  101.3 41.6 %collective-permute-start.12 = (bf16[2,5,192,128]{3,2,1,0:T(8,128)(2,1)}, bf16[2,5,192,128]{3,2,1,0:T(8,128)(2,1)S(1)}, u32[]{:S(2)}, u32[]{:S(2)}) collective-permute-start(bf16[2,5,192,128]{3,2,1,0:T(8,128)(2,1)} %get-tuple-element.59), channel_id=1, source_target_pairs={{0,6},{1,7},{2,4},{3,5},{4,2},{5,3},{6,0},{7,1},{8,14},{9,15},{10,... | collective-permute-start | bytes 1474568 | tf_op jit(solution)/shard_map/ppermute | solution.py:420
  102.9 40.1 %collective-permute-start.13 = (bf16[2,5,192,128]{3,2,1,0:T(8,128)(2,1)}, bf16[2,5,192,128]{3,2,1,0:T(8,128)(2,1)S(1)}, u32[]{:S(2)}, u32[]{:S(2)}) collective-permute-start(bf16[2,5,192,128]{3,2,1,0:T(8,128)(2,1)} %get-tuple-element.60), channel_id=1, source_target_pairs={{0,7},{1,6},{2,5},{3,4},{4,3},{5,2},{6,1},{7,0},{8,15},{9,14},{10,... | collective-permute-start | bytes 1474568 | tf_op jit(solution)/shard_map/ppermute | solution.py:420
  153.8 4.9 %collective-permute-start.31 = (f32[2,4,64]{2,1,0:T(4,128)S(1)}, f32[2,4,64]{2,1,0:T(4,128)S(1)}, u32[]{:S(2)}, u32[]{:S(2)}) collective-permute-start(f32[2,4,64]{2,1,0:T(4,128)S(1)} %rev.17), channel_id=1, source_target_pairs={{0,8},{8,16},{16,24},{1,9},{9,17},{17,25},{2,10},{10,18},{18,26},{... | collective-permute-start | bytes 6152 | tf_op jit(solution)/shard_map/ppermute | solution.py:423
  157.3 5.5 %collective-permute-start.30 = (f32[2,4,64]{2,1,0:T(4,128)S(1)}, f32[2,4,64]{2,1,0:T(4,128)S(1)}, u32[]{:S(2)}, u32[]{:S(2)}) collective-permute-start(f32[2,4,64]{2,1,0:T(4,128)S(1)} %get-tuple-element.98), channel_id=1, source_target_pairs={{8,0},{16,8},{24,16},{9,1},{17,9},{25,17},{10,2},{18,10},{26,18},{... | collective-permute-start | bytes 6152 | tf_op jit(solution)/shard_map/ppermute | solution.py:426
  (31 other events, 140.3 us)

commit v4 on v3

--- a/solution.py
+++ b/solution.py
@@ -14,9 +14,9 @@
 LANES = 128
 PAIR = 2
 BLOCK = 16
-HEAD_STEPS = 4
-STEP_BANDS = 2
-SPLITS = (5, 2, 1)
+HEAD_STEPS = 2
+STEP_BANDS = 4
+SPLITS = (4, 3, 1)
 
 
 def extended(array, sides, width):
@@ -429,11 +429,9 @@
     heads = beamform(me, staves, weights, replica, count, 0, HEAD_STEPS, STEP_BANDS, (half,))
     got_heads = [heads[0]] + [send(heads[r], r) for r in range(1, count)]
 
-    rest = (bands - head_bands) // (2 * STEP_BANDS)
+    rest = (bands - head_bands) // STEP_BANDS
     me_next, _ = lax.optimization_barrier((me, heads[0]))
-    tails = beamform(
-        me_next, staves, weights, replica, count, head_bands, rest, 2 * STEP_BANDS, sizes
-    )
+    tails = beamform(me_next, staves, weights, replica, count, head_bands, rest, STEP_BANDS, sizes)
     got_tails = []
     for i in range(len(sizes)):
         own = tails[i * count : (i + 1) * count]
@@ -455,31 +453,45 @@
 
     tables = wave_tables(count, depth, tails[0])
 
+    def placed(array, before):
+        return jnp.pad(array, ((before, pings - before - array.shape[0]), (0, 0)))
+
+    def unfolded(sums, slot):
+        left, right = sums[:, :mine], jnp.flip(sums[:, mine:], 0)
+        return placed(left, slot) + placed(right, pings - slot - right.shape[0])
+
+    starts = [sum(sizes[:i]) for i in range(len(sizes))]
+    nears = [
+        windows[:, :, slot : slot + 2 * REACH + size] for slot, size in zip(starts, sizes)
+    ]
+    tables, nears = lax.optimization_barrier((tables, nears))
+
     reached = half + 2 * REACH
     sums = jnp.zeros((2, reached, LANES), jnp.float32)
-    slot = 0
-    for i, size in enumerate(sizes):
+    for i, (slot, size) in enumerate(zip(starts, sizes)):
         width = 2 * REACH + size
-        near = windows[:, :, slot : slot + width]
+        near = nears[i]
+        if i == len(sizes) - 1:
+            so_far = [
+                unfolded(sums[which, REACH:], 0)
+                + placed(edge_left[which], pings - REACH)
+                + placed(edge_right[which], 0)
+                for which in range(2)
+            ]
+            near, *so_far = lax.optimization_barrier((near, *so_far))
         part = window_sums(me, got_heads, got_tails[i], tables, near, slot)
         sums = sums + jnp.pad(part, ((0, 0), (slot, reached - width - slot), (0, 0)))
         if slot < REACH <= slot + size:
             edge_left = down(sums[:, :REACH, :mine])
             edge_right = up(jnp.flip(sums[:, :REACH, mine:], 1))
-        slot += size
-
-    def unfolded(which):
-        def placed(array, before):
-            return jnp.pad(array, ((before, pings - before - array.shape[0]), (0, 0)))
-
-        kept = sums[which, REACH:]
-        whole = placed(kept[:, :mine], 0) + placed(jnp.flip(kept[:, mine:], 0), pings - reach)
-        return whole + placed(edge_left[which], pings - REACH) + placed(edge_right[which], 0)
+
+    total, first_moment = [
+        so_far[which] + unfolded(part[which], starts[-1] - REACH) for which in range(2)
+    ]
 
     weight_sum = tap_weights(block * pings, blocks * pings, pings)
     scale = (1.0 / (16.0 * count * depth)) / weight_sum[:, None]
     widths = length.astype(jnp.float32)
-    total, first_moment = unfolded(0), unfolded(1)
     energy_total = total * scale
     moment = (first_moment - total * (start.astype(jnp.float32) - 0.5)) * scale
     return (moment / (widths * (energy_total + 1e-06)), energy_total / widths)
@@ -505,8 +517,7 @@
         and (bands - head_bands) * bins % (2 * BLOCK) == 0
         and bands * bins <= 2 * LANES
         and bands > head_bands
-        and (bands - head_bands) % (2 * STEP_BANDS) == 0
-        and head_bands % (2 * STEP_BANDS) == 0
+        and (bands - head_bands) % STEP_BANDS == 0
     )
 
 

time: 164 us -> 167 us (1.018)
  waiting for transfers between devices: 57.2 us -> 63.2 us
  local copies, waits for them, and re-layouts: 15.2 us -> 10.8 us
    ppermute x28, waiting for transfers between devices: 53.2 us -> 57.6 us  [send(): return lax.ppermute(array, 'band', [(i, i ^ r) for i in range(count)])]
    unnamed x62 -> x58, local copies, waits for them, and re-layouts: 14 us -> 10 us
  transfers between devices with their start and end apart: 32 -> 32, of which waited for: 10 -> 11; matrix products, arithmetic and copies ran while one was open for 3% -> 3% of each run, Pallas kernels for 6% -> 10%
where the time goes in v4:
time: 167 us; the launch traced here: 166 us
  waiting for transfers between devices  63.2 us (38%)
  Pallas kernels  44.6 us (27%)
  starting transfers between devices  41.8 us (25%)
  local copies, waits for them, and re-layouts  10.8 us (6%)
  other arithmetic  4.79 us (3%)
    ppermute x28, waiting for transfers between devices, send(): return lax.ppermute(array, 'band', [(i, i ^ r) for i in range(count)])  57.6 us
    ppermute x28, starting transfers between devices, send(): return lax.ppermute(array, 'band', [(i, i ^ r) for i in range(count)])  30 us
    pallas_call x2, Pallas kernels, beamform(): pl.pallas_call(functools.partial(beam_kernel, count=count, first_band=fir...  23.4 us
    pallas_call x3, Pallas kernels, window_sums(): pl.pallas_call(functools.partial(turned_kernel, count=count, slots=slots,...  21.1 us
    unnamed x58, local copies, waits for them, and re-layouts  10 us
    ppermute x2, starting transfers between devices, up(): return lax.ppermute(array, 'ping', [(i, i + 1) for i in range(blocks - 1)])  9.24 us
    ppermute x2, waiting for transfers between devices, down(): return lax.ppermute(array, 'ping', [(i + 1, i) for i in range(blocks - 1)])  4.46 us
  transfers between devices with their start and end apart: 32, of which 11 were waited for; matrix products, arithmetic and copies ran while one was open for 3% of the time, Pallas kernels for 10%

profile of v4, /device:TPU:0, one launch (start us, length us, event | category | flops | bytes accessed | tf_op | source)
XLA Modules:
  0.0 166.3 jit_solution(13321962591974617398)
XLA Ops:
  0.6 6.8 %beamform.2 = (bf16[2,8,64,128]{3,2,1,0:T(8,128)(2,1)}, bf16[2,8,64,128]{3,2,1,0:T(8,128)(2,1)}, bf16[2,8,64,128]{3,2,1,0:T(8,128)(2,1)}, bf16[2,8,64,128]{3,2,1...) custom-call(s32[1]{0:T(128)} %bitcast.me_ref, ...), custom_call_target="tpu_custom_call" | custom-call | flops 2147483648 | bytes 12582912 | tf_op jit(solution)/shard_map/beamform/pallas_call | solution.py:194
  7.5 16.6 %beamform.3 = (bf16[2,4,192,128]{3,2,1,0:T(8,128)(2,1)}, bf16[2,4,192,128]{3,2,1,0:T(8,128)(2,1)}, bf16[2,4,192,128]{3,2,1,0:T(8,128)(2,1)}, bf16[2,4,192,128]{3...) custom-call(s32[1]{0:T(128)} %bitcast.me_ref, ...), custom_call_target="tpu_custom_call" | custom-call | flops 6442450944 | bytes 37748736 | tf_op jit(solution)/shard_map/beamform/pallas_call | solution.py:194
  24.2 1.3 collective-permute-start.1
  25.5 5.8 %collective-permute-start = (s32[2,4,64]{2,1,0:T(4,128)S(1)}, s32[2,4,64]{2,1,0:T(4,128)S(1)}, u32[]{:S(2)}, u32[]{:S(2)}) collective-permute-start(s32[2,4,64]{2,1,0:T(4,128)S(1)} %get-tuple-element.116), channel_id=1, source_target_pairs={{0,8},{8,16},{16,24},{1,9},{9,17},{17,25},{2,10},{10,18},{18,26},{... | collective-permute-start | bytes 6152 | tf_op jit(solution)/shard_map/ppermute | solution.py:423
  31.3 2.0 %collective-permute-start.3 = (bf16[2,8,64,128]{3,2,1,0:T(8,128)(2,1)}, bf16[2,8,64,128]{3,2,1,0:T(8,128)(2,1)S(1)}, u32[]{:S(2)}, u32[]{:S(2)}) collective-permute-start(bf16[2,8,64,128]{3,2,1,0:T(8,128)(2,1)} %get-tuple-element.66), channel_id=1, source_target_pairs={{0,2},{1,3},{2,0},{3,1},{4,6},{5,7},{6,4},{7,5},{8,10},{9,11},{10,... | collective-permute-start | bytes 786440 | tf_op jit(solution)/shard_map/ppermute | solution.py:420
  33.4 1.9 %fusion.5 = (f32[256,256]{1,0:T(8,128)}, f32[256,256]{1,0:T(8,128)}) fusion(s32[256]{0:T(256)S(1)} %iota.15), kind=kLoop, calls=%fused_computation.16 | loop fusion | flops 917504 | bytes 525312 | tf_op jit(solution)/shard_map/sin | solution.py:400
  35.4 1.8 %collective-permute-start.5 = (bf16[2,8,64,128]{3,2,1,0:T(8,128)(2,1)}, bf16[2,8,64,128]{3,2,1,0:T(8,128)(2,1)S(1)}, u32[]{:S(2)}, u32[]{:S(2)}) collective-permute-start(bf16[2,8,64,128]{3,2,1,0:T(8,128)(2,1)} %get-tuple-element.68), channel_id=1, source_target_pairs={{0,4},{1,5},{2,6},{3,7},{4,0},{5,1},{6,2},{7,3},{8,12},{9,13},{10,... | collective-permute-start | bytes 786440 | tf_op jit(solution)/shard_map/ppermute | solution.py:420
  37.2 2.6 %collective-permute-start.7 = (bf16[2,8,64,128]{3,2,1,0:T(8,128)(2,1)}, bf16[2,8,64,128]{3,2,1,0:T(8,128)(2,1)S(1)}, u32[]{:S(2)}, u32[]{:S(2)}) collective-permute-start(bf16[2,8,64,128]{3,2,1,0:T(8,128)(2,1)} %get-tuple-element.70), channel_id=1, source_target_pairs={{0,6},{1,7},{2,4},{3,5},{4,2},{5,3},{6,0},{7,1},{8,14},{9,15},{10,... | collective-permute-start | bytes 786440 | tf_op jit(solution)/shard_map/ppermute | solution.py:420
  39.8 1.6 add_convert_fusion
  42.2 3.7 %collective-permute-done.4.refs_3_ = bf16[2,8,64,128]{3,2,1,0:T(8,128)(2,1)S(1)} collective-permute-done((bf16[2,8,64,128]{3,2,1,0:T(8,128)(2,1)}, bf16[2,8,64,128]{3,2,1,0:T(8,128)(2,1)S(1)}, u32[]{:S(2)}, u32[]{:S(2)}) %collective-permute-start.4) | collective-permute-done | bytes 262176 | tf_op jit(solution)/shard_map/ppermute | solution.py:420
  46.5 2.0 %collective-permute-start.17 = (bf16[2,3,192,128]{3,2,1,0:T(8,128)(2,1)S(1)}, bf16[2,3,192,128]{3,2,1,0:T(8,128)(2,1)S(1)}, u32[]{:S(2)}, u32[]{:S(2)}) collective-permute-start(bf16[2,3,192,128]{3,2,1,0:T(8,128)(2,1)S(1)} %copy-done.26), channel_id=1, source_target_pairs={{0,2},{1,3},{2,0},{3,1},{4,6},{5,7},{6,4},{7,5},{8,10},{9,11},{10,... | collective-permute-start | bytes 884744 | tf_op jit(solution)/shard_map/ppermute | solution.py:420
  48.5 11.9 %collective-permute-done.6.refs_5_ = bf16[2,8,64,128]{3,2,1,0:T(8,128)(2,1)S(1)} collective-permute-done((bf16[2,8,64,128]{3,2,1,0:T(8,128)(2,1)}, bf16[2,8,64,128]{3,2,1,0:T(8,128)(2,1)S(1)}, u32[]{:S(2)}, u32[]{:S(2)}) %collective-permute-start.6) | collective-permute-done | bytes 262176 | tf_op jit(solution)/shard_map/ppermute | solution.py:420
  60.4 2.1 %collective-permute-start.18 = (bf16[2,3,192,128]{3,2,1,0:T(8,128)(2,1)S(1)}, bf16[2,3,192,128]{3,2,1,0:T(8,128)(2,1)S(1)}, u32[]{:S(2)}, u32[]{:S(2)}) collective-permute-start(bf16[2,3,192,128]{3,2,1,0:T(8,128)(2,1)S(1)} %copy-done.25), channel_id=1, source_target_pairs={{0,3},{1,2},{2,1},{3,0},{4,7},{5,6},{6,5},{7,4},{8,11},{9,10},{10,... | collective-permute-start | bytes 884744 | tf_op jit(solution)/shard_map/ppermute | solution.py:420
  63.3 1.5 collective-permute-start.19
  67.7 2.3 %collective-permute-done.18.refs_11_ = bf16[2,3,192,128]{3,2,1,0:T(8,128)(2,1)S(1)} collective-permute-done((bf16[2,3,192,128]{3,2,1,0:T(8,128)(2,1)S(1)}, bf16[2,3,192,128]{3,2,1,0:T(8,128)(2,1)S(1)}, u32[]{:S(2)}, u32[]{:S(2)}) %collective-permute-start.18) | collective-permute-done | bytes 294944 | tf_op jit(solution)/shard_map/ppermute | solution.py:420
  70.7 1.9 %collective-permute-start.21 = (bf16[2,3,192,128]{3,2,1,0:T(8,128)(2,1)}, bf16[2,3,192,128]{3,2,1,0:T(8,128)(2,1)}, u32[]{:S(2)}, u32[]{:S(2)}) collective-permute-start(bf16[2,3,192,128]{3,2,1,0:T(8,128)(2,1)} %get-tuple-element.88), channel_id=1, source_target_pairs={{0,6},{1,7},{2,4},{3,5},{4,2},{5,3},{6,0},{7,1},{8,14},{9,15},{10,... | collective-permute-start | bytes 884744 | tf_op jit(solution)/shard_map/ppermute | solution.py:420
  74.8 2.7 %collective-permute-done.20.refs_13_ = bf16[2,3,192,128]{3,2,1,0:T(8,128)(2,1)} collective-permute-done((bf16[2,3,192,128]{3,2,1,0:T(8,128)(2,1)}, bf16[2,3,192,128]{3,2,1,0:T(8,128)(2,1)}, u32[]{:S(2)}, u32[]{:S(2)}) %collective-permute-start.20) | collective-permute-done | bytes 294944 | tf_op jit(solution)/shard_map/ppermute | solution.py:420
  77.5 1.3 collective-permute-start.11
  78.8 7.9 %collective-permute-done.21.refs_14_ = bf16[2,3,192,128]{3,2,1,0:T(8,128)(2,1)} collective-permute-done((bf16[2,3,192,128]{3,2,1,0:T(8,128)(2,1)}, bf16[2,3,192,128]{3,2,1,0:T(8,128)(2,1)}, u32[]{:S(2)}, u32[]{:S(2)}) %collective-permute-start.21) | collective-permute-done | bytes 294944 | tf_op jit(solution)/shard_map/ppermute | solution.py:420
  87.0 4.7 %collective-permute-done.22.refs_15_ = bf16[2,3,192,128]{3,2,1,0:T(8,128)(2,1)} collective-permute-done((bf16[2,3,192,128]{3,2,1,0:T(8,128)(2,1)}, bf16[2,3,192,128]{3,2,1,0:T(8,128)(2,1)}, u32[]{:S(2)}, u32[]{:S(2)}) %collective-permute-start.22) | collective-permute-done | bytes 294944 | tf_op jit(solution)/shard_map/ppermute | solution.py:420
  92.8 2.7 %collective-permute-start.14 = (bf16[2,4,192,128]{3,2,1,0:T(8,128)(2,1)}, bf16[2,4,192,128]{3,2,1,0:T(8,128)(2,1)S(1)}, u32[]{:S(2)}, u32[]{:S(2)}) collective-permute-start(bf16[2,4,192,128]{3,2,1,0:T(8,128)(2,1)} %get-tuple-element.77), channel_id=1, source_target_pairs={{0,6},{1,7},{2,4},{3,5},{4,2},{5,3},{6,0},{7,1},{8,14},{9,15},{10,... | collective-permute-start | bytes 1179656 | tf_op jit(solution)/shard_map/ppermute | solution.py:420
  97.9 7.3 %window_sums.4 = f32[8,1408]{1,0:T(8,128)S(1)} custom-call(s32[1]{0:T(128)} %bitcast.me_ref, bf16[2,8,64,128]{3,2,1,0:T(8,128)(2,1)} %get-tuple-element.52.refs_0_, bf16[2,8,64,128]{3,2,1,0:T(8,128)(2,1)S(1)} %collective-permute-done.2.refs_1_, bf16[2,8,64,128]{3,2,1,0:T(8,128)(2,1)S(1)} %collective-permute-done.3.refs_2_, ...), custom_call_target="tpu_custom_call" | custom-call | flops 1610612736 | bytes 6291456 | tf_op jit(solution)/shard_map/window_sums/pallas_call | solution.py:359
  105.7 1.8 %collective-permute-start.26 = (bf16[2,1,192,128]{3,2,1,0:T(8,128)(2,1)}, bf16[2,1,192,128]{3,2,1,0:T(8,128)(2,1)}, u32[]{:S(2)}, u32[]{:S(2)}) collective-permute-start(bf16[2,1,192,128]{3,2,1,0:T(8,128)(2,1)} %get-tuple-element.94), channel_id=1, source_target_pairs={{0,2},{1,3},{2,0},{3,1},{4,6},{5,7},{6,4},{7,5},{8,10},{9,11},{10,... | collective-permute-start | bytes 294920 | tf_op jit(solution)/shard_map/ppermute | solution.py:420
  107.5 18.2 %collective-permute-done.13.refs_13_ = bf16[2,4,192,128]{3,2,1,0:T(8,128)(2,1)S(1)} collective-permute-done((bf16[2,4,192,128]{3,2,1,0:T(8,128)(2,1)}, bf16[2,4,192,128]{3,2,1,0:T(8,128)(2,1)S(1)}, u32[]{:S(2)}, u32[]{:S(2)}) %collective-permute-start.13) | collective-permute-done | bytes 393248 | tf_op jit(solution)/shard_map/ppermute | solution.py:420
  127.6 9.0 %window_sums.3 = f32[8,1536]{1,0:T(8,128)S(1)} custom-call(s32[1]{0:T(128)} %bitcast.me_ref, bf16[2,8,64,128]{3,2,1,0:T(8,128)(2,1)} %get-tuple-element.52.refs_0_, bf16[2,8,64,128]{3,2,1,0:T(8,128)(2,1)S(1)} %collective-permute-done.2.refs_1_, bf16[2,8,64,128]{3,2,1,0:T(8,128)(2,1)S(1)} %collective-permute-done.3.refs_2_, ...), custom_call_target="tpu_custom_call" | custom-call | flops 2147483648 | bytes 6291456 | tf_op jit(solution)/shard_map/window_sums/pallas_call | solution.py:359
  136.7 3.5 %collective-permute-start.24 = (f32[2,4,64]{2,1,0:T(4,128)S(1)}, f32[2,4,64]{2,1,0:T(4,128)S(1)}, u32[]{:S(2)}, u32[]{:S(2)}) collective-permute-start(f32[2,4,64]{2,1,0:T(4,128)S(1)} %rev.24), channel_id=1, source_target_pairs={{0,8},{8,16},{16,24},{1,9},{9,17},{17,25},{2,10},{10,18},{18,26},{... | collective-permute-start | bytes 6152 | tf_op jit(solution)/shard_map/ppermute | solution.py:423
  141.5 1.3 collective-permute-start.23
  142.8 4.5 %collective-permute-done.23 = f32[2,4,64]{2,1,0:T(4,128)S(1)} collective-permute-done((f32[2,4,64]{2,1,0:T(4,128)S(1)}, f32[2,4,64]{2,1,0:T(4,128)S(1)}, u32[]{:S(2)}, u32[]{:S(2)}) %collective-permute-start.23) | collective-permute-done | bytes 2080 | tf_op jit(solution)/shard_map/ppermute | solution.py:426
  147.3 1.5 collective-permute-start.30
  148.8 2.3 %collective-permute-start.31 = (bf16[2,1,192,128]{3,2,1,0:T(8,128)(2,1)}, bf16[2,1,192,128]{3,2,1,0:T(8,128)(2,1)S(1)}, u32[]{:S(2)}, u32[]{:S(2)}) collective-permute-start(bf16[2,1,192,128]{3,2,1,0:T(8,128)(2,1)} %get-tuple-element.99), channel_id=1, source_target_pairs={{0,7},{1,6},{2,5},{3,4},{4,3},{5,2},{6,1},{7,0},{8,15},{9,14},{10,... | collective-permute-start | bytes 294920 | tf_op jit(solution)/shard_map/ppermute | solution.py:420
  151.1 5.6 %collective-permute-done.29.refs_13_ = bf16[2,1,192,128]{3,2,1,0:T(8,128)(2,1)S(1)} collective-permute-done((bf16[2,1,192,128]{3,2,1,0:T(8,128)(2,1)}, bf16[2,1,192,128]{3,2,1,0:T(8,128)(2,1)S(1)}, u32[]{:S(2)}, u32[]{:S(2)}) %collective-permute-start.29) | collective-permute-done | bytes 98336 | tf_op jit(solution)/shard_map/ppermute | solution.py:420
  160.6 4.8 %window_sums.5 = f32[8,1152]{1,0:T(8,128)S(1)} custom-call(s32[1]{0:T(128)} %bitcast.me_ref, bf16[2,8,64,128]{3,2,1,0:T(8,128)(2,1)} %get-tuple-element.52.refs_0_, bf16[2,8,64,128]{3,2,1,0:T(8,128)(2,1)S(1)} %collective-permute-done.2.refs_1_, bf16[2,8,64,128]{3,2,1,0:T(8,128)(2,1)S(1)} %collective-permute-done.3.refs_2_, ...), custom_call_target="tpu_custom_call" | custom-call | flops 536870912 | bytes 6291456 | tf_op jit(solution)/shard_map/window_sums/pallas_call | solution.py:359
  (134 shorter events, 20.4 us)
Async XLA Ops:
  24.2 11.2 %collective-permute-start.1 = (s32[2,4,64]{2,1,0:T(4,128)S(1)}, s32[2,4,64]{2,1,0:T(4,128)S(1)}, u32[]{:S(2)}, u32[]{:S(2)}) collective-permute-start(s32[2,4,64]{2,1,0:T(4,128)S(1)} %get-tuple-element.117), channel_id=1, source_target_pairs={{8,0},{16,8},{24,16},{9,1},{17,9},{25,17},{10,2},{18,10},{26,18},{... | collective-permute-start | bytes 6152 | tf_op jit(solution)/shard_map/ppermute | solution.py:426
  25.5 11.7 %collective-permute-start = (s32[2,4,64]{2,1,0:T(4,128)S(1)}, s32[2,4,64]{2,1,0:T(4,128)S(1)}, u32[]{:S(2)}, u32[]{:S(2)}) collective-permute-start(s32[2,4,64]{2,1,0:T(4,128)S(1)} %get-tuple-element.116), channel_id=1, source_target_pairs={{0,8},{8,16},{16,24},{1,9},{9,17},{17,25},{2,10},{10,18},{18,26},{... | collective-permute-start | bytes 6152 | tf_op jit(solution)/shard_map/ppermute | solution.py:423
  31.2 6.0 %collective-permute-start.2 = (bf16[2,8,64,128]{3,2,1,0:T(8,128)(2,1)S(1)}, bf16[2,8,64,128]{3,2,1,0:T(8,128)(2,1)S(1)}, u32[]{:S(2)}, u32[]{:S(2)}) collective-permute-start(bf16[2,8,64,128]{3,2,1,0:T(8,128)(2,1)S(1)} %copy-done.28), channel_id=1, source_target_pairs={{0,1},{1,0},{2,3},{3,2},{4,5},{5,4},{6,7},{7,6},{8,9},{9,8},{10,11... | collective-permute-start | bytes 786440 | tf_op jit(solution)/shard_map/ppermute | solution.py:420
  31.3 10.1 %collective-permute-start.3 = (bf16[2,8,64,128]{3,2,1,0:T(8,128)(2,1)}, bf16[2,8,64,128]{3,2,1,0:T(8,128)(2,1)S(1)}, u32[]{:S(2)}, u32[]{:S(2)}) collective-permute-start(bf16[2,8,64,128]{3,2,1,0:T(8,128)(2,1)} %get-tuple-element.66), channel_id=1, source_target_pairs={{0,2},{1,3},{2,0},{3,1},{4,6},{5,7},{6,4},{7,5},{8,10},{9,11},{10,... | collective-permute-start | bytes 786440 | tf_op jit(solution)/shard_map/ppermute | solution.py:420
  33.3 12.6 %collective-permute-start.4 = (bf16[2,8,64,128]{3,2,1,0:T(8,128)(2,1)}, bf16[2,8,64,128]{3,2,1,0:T(8,128)(2,1)S(1)}, u32[]{:S(2)}, u32[]{:S(2)}) collective-permute-start(bf16[2,8,64,128]{3,2,1,0:T(8,128)(2,1)} %get-tuple-element.67), channel_id=1, source_target_pairs={{0,3},{1,2},{2,1},{3,0},{4,7},{5,6},{6,5},{7,4},{8,11},{9,10},{10,... | collective-permute-start | bytes 786440 | tf_op jit(solution)/shard_map/ppermute | solution.py:420
  35.4 11.1 %collective-permute-start.5 = (bf16[2,8,64,128]{3,2,1,0:T(8,128)(2,1)}, bf16[2,8,64,128]{3,2,1,0:T(8,128)(2,1)S(1)}, u32[]{:S(2)}, u32[]{:S(2)}) collective-permute-start(bf16[2,8,64,128]{3,2,1,0:T(8,128)(2,1)} %get-tuple-element.68), channel_id=1, source_target_pairs={{0,4},{1,5},{2,6},{3,7},{4,0},{5,1},{6,2},{7,3},{8,12},{9,13},{10,... | collective-permute-start | bytes 786440 | tf_op jit(solution)/shard_map/ppermute | solution.py:420
  37.2 23.3 %collective-permute-start.6 = (bf16[2,8,64,128]{3,2,1,0:T(8,128)(2,1)}, bf16[2,8,64,128]{3,2,1,0:T(8,128)(2,1)S(1)}, u32[]{:S(2)}, u32[]{:S(2)}) collective-permute-start(bf16[2,8,64,128]{3,2,1,0:T(8,128)(2,1)} %get-tuple-element.69), channel_id=1, source_target_pairs={{0,5},{1,4},{2,7},{3,6},{4,1},{5,0},{6,3},{7,2},{8,13},{9,12},{10,... | collective-permute-start | bytes 786440 | tf_op jit(solution)/shard_map/ppermute | solution.py:420
  37.2 25.4 %collective-permute-start.7 = (bf16[2,8,64,128]{3,2,1,0:T(8,128)(2,1)}, bf16[2,8,64,128]{3,2,1,0:T(8,128)(2,1)S(1)}, u32[]{:S(2)}, u32[]{:S(2)}) collective-permute-start(bf16[2,8,64,128]{3,2,1,0:T(8,128)(2,1)} %get-tuple-element.70), channel_id=1, source_target_pairs={{0,6},{1,7},{2,4},{3,5},{4,2},{5,3},{6,0},{7,1},{8,14},{9,15},{10,... | collective-permute-start | bytes 786440 | tf_op jit(solution)/shard_map/ppermute | solution.py:420
  41.4 23.4 %collective-permute-start.8 = (bf16[2,8,64,128]{3,2,1,0:T(8,128)(2,1)}, bf16[2,8,64,128]{3,2,1,0:T(8,128)(2,1)S(1)}, u32[]{:S(2)}, u32[]{:S(2)}) collective-permute-start(bf16[2,8,64,128]{3,2,1,0:T(8,128)(2,1)} %get-tuple-element.71), channel_id=1, source_target_pairs={{0,7},{1,6},{2,5},{3,4},{4,3},{5,2},{6,1},{7,0},{8,15},{9,14},{10,... | collective-permute-start | bytes 786440 | tf_op jit(solution)/shard_map/ppermute | solution.py:420
  45.9 19.6 %collective-permute-start.16 = (bf16[2,3,192,128]{3,2,1,0:T(8,128)(2,1)S(1)}, bf16[2,3,192,128]{3,2,1,0:T(8,128)(2,1)S(1)}, u32[]{:S(2)}, u32[]{:S(2)}) collective-permute-start(bf16[2,3,192,128]{3,2,1,0:T(8,128)(2,1)S(1)} %copy-done.27), channel_id=1, source_target_pairs={{0,1},{1,0},{2,3},{3,2},{4,5},{5,4},{6,7},{7,6},{8,9},{9,8},{10,11... | collective-permute-start | bytes 884744 | tf_op jit(solution)/shard_map/ppermute | solution.py:420
  46.5 20.3 %collective-permute-start.17 = (bf16[2,3,192,128]{3,2,1,0:T(8,128)(2,1)S(1)}, bf16[2,3,192,128]{3,2,1,0:T(8,128)(2,1)S(1)}, u32[]{:S(2)}, u32[]{:S(2)}) collective-permute-start(bf16[2,3,192,128]{3,2,1,0:T(8,128)(2,1)S(1)} %copy-done.26), channel_id=1, source_target_pairs={{0,2},{1,3},{2,0},{3,1},{4,6},{5,7},{6,4},{7,5},{8,10},{9,11},{10,... | collective-permute-start | bytes 884744 | tf_op jit(solution)/shard_map/ppermute | solution.py:420
  60.4 9.5 %collective-permute-start.18 = (bf16[2,3,192,128]{3,2,1,0:T(8,128)(2,1)S(1)}, bf16[2,3,192,128]{3,2,1,0:T(8,128)(2,1)S(1)}, u32[]{:S(2)}, u32[]{:S(2)}) collective-permute-start(bf16[2,3,192,128]{3,2,1,0:T(8,128)(2,1)S(1)} %copy-done.25), channel_id=1, source_target_pairs={{0,3},{1,2},{2,1},{3,0},{4,7},{5,6},{6,5},{7,4},{8,11},{9,10},{10,... | collective-permute-start | bytes 884744 | tf_op jit(solution)/shard_map/ppermute | solution.py:420
  63.3 9.9 %collective-permute-start.19 = (bf16[2,3,192,128]{3,2,1,0:T(8,128)(2,1)S(1)}, bf16[2,3,192,128]{3,2,1,0:T(8,128)(2,1)S(1)}, u32[]{:S(2)}, u32[]{:S(2)}) collective-permute-start(bf16[2,3,192,128]{3,2,1,0:T(8,128)(2,1)S(1)} %copy-done.24), channel_id=1, source_target_pairs={{0,4},{1,5},{2,6},{3,7},{4,0},{5,1},{6,2},{7,3},{8,12},{9,13},{10,... | collective-permute-start | bytes 884744 | tf_op jit(solution)/shard_map/ppermute | solution.py:420
  65.6 27.2 %collective-permute-start.9 = (bf16[2,4,192,128]{3,2,1,0:T(8,128)(2,1)}, bf16[2,4,192,128]{3,2,1,0:T(8,128)(2,1)}, u32[]{:S(2)}, u32[]{:S(2)}) collective-permute-start(bf16[2,4,192,128]{3,2,1,0:T(8,128)(2,1)} %get-tuple-element.72), channel_id=1, source_target_pairs={{0,1},{1,0},{2,3},{3,2},{4,5},{5,4},{6,7},{7,6},{8,9},{9,8},{10,11... | collective-permute-start | bytes 1179656 | tf_op jit(solution)/shard_map/ppermute | solution.py:420
  66.3 29.2 %collective-permute-start.10 = (bf16[2,4,192,128]{3,2,1,0:T(8,128)(2,1)}, bf16[2,4,192,128]{3,2,1,0:T(8,128)(2,1)}, u32[]{:S(2)}, u32[]{:S(2)}) collective-permute-start(bf16[2,4,192,128]{3,2,1,0:T(8,128)(2,1)} %get-tuple-element.73), channel_id=1, source_target_pairs={{0,2},{1,3},{2,0},{3,1},{4,6},{5,7},{6,4},{7,5},{8,10},{9,11},{10,... | collective-permute-start | bytes 1179656 | tf_op jit(solution)/shard_map/ppermute | solution.py:420
  67.5 10.0 %collective-permute-start.20 = (bf16[2,3,192,128]{3,2,1,0:T(8,128)(2,1)}, bf16[2,3,192,128]{3,2,1,0:T(8,128)(2,1)}, u32[]{:S(2)}, u32[]{:S(2)}) collective-permute-start(bf16[2,3,192,128]{3,2,1,0:T(8,128)(2,1)} %get-tuple-element.87), channel_id=1, source_target_pairs={{0,5},{1,4},{2,7},{3,6},{4,1},{5,0},{6,3},{7,2},{8,13},{9,12},{10,... | collective-permute-start | bytes 884744 | tf_op jit(solution)/shard_map/ppermute | solution.py:420
  70.7 16.0 %collective-permute-start.21 = (bf16[2,3,192,128]{3,2,1,0:T(8,128)(2,1)}, bf16[2,3,192,128]{3,2,1,0:T(8,128)(2,1)}, u32[]{:S(2)}, u32[]{:S(2)}) collective-permute-start(bf16[2,3,192,128]{3,2,1,0:T(8,128)(2,1)} %get-tuple-element.88), channel_id=1, source_target_pairs={{0,6},{1,7},{2,4},{3,5},{4,2},{5,3},{6,0},{7,1},{8,14},{9,15},{10,... | collective-permute-start | bytes 884744 | tf_op jit(solution)/shard_map/ppermute | solution.py:420
  73.9 17.7 %collective-permute-start.22 = (bf16[2,3,192,128]{3,2,1,0:T(8,128)(2,1)}, bf16[2,3,192,128]{3,2,1,0:T(8,128)(2,1)}, u32[]{:S(2)}, u32[]{:S(2)}) collective-permute-start(bf16[2,3,192,128]{3,2,1,0:T(8,128)(2,1)} %get-tuple-element.89), channel_id=1, source_target_pairs={{0,7},{1,6},{2,5},{3,4},{4,3},{5,2},{6,1},{7,0},{8,15},{9,14},{10,... | collective-permute-start | bytes 884744 | tf_op jit(solution)/shard_map/ppermute | solution.py:420
  77.5 27.8 %collective-permute-start.11 = (bf16[2,4,192,128]{3,2,1,0:T(8,128)(2,1)}, bf16[2,4,192,128]{3,2,1,0:T(8,128)(2,1)S(1)}, u32[]{:S(2)}, u32[]{:S(2)}) collective-permute-start(bf16[2,4,192,128]{3,2,1,0:T(8,128)(2,1)} %get-tuple-element.74), channel_id=1, source_target_pairs={{0,3},{1,2},{2,1},{3,0},{4,7},{5,6},{6,5},{7,4},{8,11},{9,10},{10,... | collective-permute-start | bytes 1179656 | tf_op jit(solution)/shard_map/ppermute | solution.py:420
  86.7 19.1 %collective-permute-start.12 = (bf16[2,4,192,128]{3,2,1,0:T(8,128)(2,1)}, bf16[2,4,192,128]{3,2,1,0:T(8,128)(2,1)S(1)}, u32[]{:S(2)}, u32[]{:S(2)}) collective-permute-start(bf16[2,4,192,128]{3,2,1,0:T(8,128)(2,1)} %get-tuple-element.75), channel_id=1, source_target_pairs={{0,4},{1,5},{2,6},{3,7},{4,0},{5,1},{6,2},{7,3},{8,12},{9,13},{10,... | collective-permute-start | bytes 1179656 | tf_op jit(solution)/shard_map/ppermute | solution.py:420
  91.6 34.1 %collective-permute-start.13 = (bf16[2,4,192,128]{3,2,1,0:T(8,128)(2,1)}, bf16[2,4,192,128]{3,2,1,0:T(8,128)(2,1)S(1)}, u32[]{:S(2)}, u32[]{:S(2)}) collective-permute-start(bf16[2,4,192,128]{3,2,1,0:T(8,128)(2,1)} %get-tuple-element.76), channel_id=1, source_target_pairs={{0,5},{1,4},{2,7},{3,6},{4,1},{5,0},{6,3},{7,2},{8,13},{9,12},{10,... | collective-permute-start | bytes 1179656 | tf_op jit(solution)/shard_map/ppermute | solution.py:420
  92.8 34.2 %collective-permute-start.14 = (bf16[2,4,192,128]{3,2,1,0:T(8,128)(2,1)}, bf16[2,4,192,128]{3,2,1,0:T(8,128)(2,1)S(1)}, u32[]{:S(2)}, u32[]{:S(2)}) collective-permute-start(bf16[2,4,192,128]{3,2,1,0:T(8,128)(2,1)} %get-tuple-element.77), channel_id=1, source_target_pairs={{0,6},{1,7},{2,4},{3,5},{4,2},{5,3},{6,0},{7,1},{8,14},{9,15},{10,... | collective-permute-start | bytes 1179656 | tf_op jit(solution)/shard_map/ppermute | solution.py:420
  95.4 32.1 %collective-permute-start.15 = (bf16[2,4,192,128]{3,2,1,0:T(8,128)(2,1)}, bf16[2,4,192,128]{3,2,1,0:T(8,128)(2,1)S(1)}, u32[]{:S(2)}, u32[]{:S(2)}) collective-permute-start(bf16[2,4,192,128]{3,2,1,0:T(8,128)(2,1)} %get-tuple-element.78), channel_id=1, source_target_pairs={{0,7},{1,6},{2,5},{3,4},{4,3},{5,2},{6,1},{7,0},{8,15},{9,14},{10,... | collective-permute-start | bytes 1179656 | tf_op jit(solution)/shard_map/ppermute | solution.py:420
  105.3 42.0 %collective-permute-start.25 = (bf16[2,1,192,128]{3,2,1,0:T(8,128)(2,1)}, bf16[2,1,192,128]{3,2,1,0:T(8,128)(2,1)}, u32[]{:S(2)}, u32[]{:S(2)}) collective-permute-start(bf16[2,1,192,128]{3,2,1,0:T(8,128)(2,1)} %get-tuple-element.93), channel_id=1, source_target_pairs={{0,1},{1,0},{2,3},{3,2},{4,5},{5,4},{6,7},{7,6},{8,9},{9,8},{10,11... | collective-permute-start | bytes 294920 | tf_op jit(solution)/shard_map/ppermute | solution.py:420
  105.7 43.0 %collective-permute-start.26 = (bf16[2,1,192,128]{3,2,1,0:T(8,128)(2,1)}, bf16[2,1,192,128]{3,2,1,0:T(8,128)(2,1)}, u32[]{:S(2)}, u32[]{:S(2)}) collective-permute-start(bf16[2,1,192,128]{3,2,1,0:T(8,128)(2,1)} %get-tuple-element.94), channel_id=1, source_target_pairs={{0,2},{1,3},{2,0},{3,1},{4,6},{5,7},{6,4},{7,5},{8,10},{9,11},{10,... | collective-permute-start | bytes 294920 | tf_op jit(solution)/shard_map/ppermute | solution.py:420
  125.8 25.4 %collective-permute-start.27 = (bf16[2,1,192,128]{3,2,1,0:T(8,128)(2,1)}, bf16[2,1,192,128]{3,2,1,0:T(8,128)(2,1)}, u32[]{:S(2)}, u32[]{:S(2)}) collective-permute-start(bf16[2,1,192,128]{3,2,1,0:T(8,128)(2,1)} %get-tuple-element.95), channel_id=1, source_target_pairs={{0,3},{1,2},{2,1},{3,0},{4,7},{5,6},{6,5},{7,4},{8,11},{9,10},{10,... | collective-permute-start | bytes 294920 | tf_op jit(solution)/shard_map/ppermute | solution.py:420
  127.0 24.1 %collective-permute-start.28 = (bf16[2,1,192,128]{3,2,1,0:T(8,128)(2,1)}, bf16[2,1,192,128]{3,2,1,0:T(8,128)(2,1)}, u32[]{:S(2)}, u32[]{:S(2)}) collective-permute-start(bf16[2,1,192,128]{3,2,1,0:T(8,128)(2,1)} %get-tuple-element.96), channel_id=1, source_target_pairs={{0,4},{1,5},{2,6},{3,7},{4,0},{5,1},{6,2},{7,3},{8,12},{9,13},{10,... | collective-permute-start | bytes 294920 | tf_op jit(solution)/shard_map/ppermute | solution.py:420
  136.7 4.8 %collective-permute-start.24 = (f32[2,4,64]{2,1,0:T(4,128)S(1)}, f32[2,4,64]{2,1,0:T(4,128)S(1)}, u32[]{:S(2)}, u32[]{:S(2)}) collective-permute-start(f32[2,4,64]{2,1,0:T(4,128)S(1)} %rev.24), channel_id=1, source_target_pairs={{0,8},{8,16},{16,24},{1,9},{9,17},{17,25},{2,10},{10,18},{18,26},{... | collective-permute-start | bytes 6152 | tf_op jit(solution)/shard_map/ppermute | solution.py:423
  141.5 5.8 %collective-permute-start.23 = (f32[2,4,64]{2,1,0:T(4,128)S(1)}, f32[2,4,64]{2,1,0:T(4,128)S(1)}, u32[]{:S(2)}, u32[]{:S(2)}) collective-permute-start(f32[2,4,64]{2,1,0:T(4,128)S(1)} %get-tuple-element.114), channel_id=1, source_target_pairs={{8,0},{16,8},{24,16},{9,1},{17,9},{25,17},{10,2},{18,10},{26,18},{... | collective-permute-start | bytes 6152 | tf_op jit(solution)/shard_map/ppermute | solution.py:426
  147.3 9.5 %collective-permute-start.29 = (bf16[2,1,192,128]{3,2,1,0:T(8,128)(2,1)}, bf16[2,1,192,128]{3,2,1,0:T(8,128)(2,1)S(1)}, u32[]{:S(2)}, u32[]{:S(2)}) collective-permute-start(bf16[2,1,192,128]{3,2,1,0:T(8,128)(2,1)} %get-tuple-element.97), channel_id=1, source_target_pairs={{0,5},{1,4},{2,7},{3,6},{4,1},{5,0},{6,3},{7,2},{8,13},{9,12},{10,... | collective-permute-start | bytes 294920 | tf_op jit(solution)/shard_map/ppermute | solution.py:420
  147.3 9.5 %collective-permute-start.30 = (bf16[2,1,192,128]{3,2,1,0:T(8,128)(2,1)}, bf16[2,1,192,128]{3,2,1,0:T(8,128)(2,1)S(1)}, u32[]{:S(2)}, u32[]{:S(2)}) collective-permute-start(bf16[2,1,192,128]{3,2,1,0:T(8,128)(2,1)} %get-tuple-element.98), channel_id=1, source_target_pairs={{0,6},{1,7},{2,4},{3,5},{4,2},{5,3},{6,0},{7,1},{8,14},{9,15},{10,... | collective-permute-start | bytes 294920 | tf_op jit(solution)/shard_map/ppermute | solution.py:420
  148.8 8.0 %collective-permute-start.31 = (bf16[2,1,192,128]{3,2,1,0:T(8,128)(2,1)}, bf16[2,1,192,128]{3,2,1,0:T(8,128)(2,1)S(1)}, u32[]{:S(2)}, u32[]{:S(2)}) collective-permute-start(bf16[2,1,192,128]{3,2,1,0:T(8,128)(2,1)} %get-tuple-element.99), channel_id=1, source_target_pairs={{0,7},{1,6},{2,5},{3,4},{4,3},{5,2},{6,1},{7,0},{8,15},{9,14},{10,... | collective-permute-start | bytes 294920 | tf_op jit(solution)/shard_map/ppermute | solution.py:420
  (29 other events, 413.7 us)
